TPU v7x, 32 devices: a whole 2x2x4 slice. The times are simulated.
32 devices in a mesh: gx: 4 (over x, core), gy: 8 (over z, y).
Axes of the slice: x: 2, y: 2, z: 4, core: 2. Of those that a mesh axis runs over, the one named last changes fastest.
Arguments:
- probes: float32 [32, 64, 64, 256], P(None, 'gx', 'gy'), may hold values from -108 to 108, as said below
- diffusion: float32 [64, 64, 256], P('gx', 'gy'), may hold values from 0.03 to 0.16
- velocity: float32 [3, 64, 64, 256], P(None, 'gx', 'gy'), may hold values from -0.2 to 0.2
Outputs:
- basis: float32 [32, 64, 64, 256], P(None, 'gx', 'gy')
- factor: float32 [32, 32], replicated
Inputs may be any that keep to these rules, and one draw needn't show every extreme that they name: `probes`: each entry is finite and real-valued.
All inputs are finite; a program needn't handle non-finite values.
Results may differ from a plain program's by a relative error of at most 0.00011.
Values sent between devices are 32-bit elements; how exact they have to be, the bound alone decides.
No kernel may reach another device: no remote copies, remote signals or barrier semaphores. Data moves between devices by JAX's collectives and lax.ppermute only.
A program may use at most 64 MiB of HBM per device.

v0:
```python
import jax
import jax.numpy as jnp
from jax import lax
from jax.sharding import PartitionSpec as P

STEPS = 2


def with_halo(cells, sides, width):
    for axis, dim in sides:
        count = lax.axis_size(axis)
        ends = count - 1
        head = lax.slice_in_dim(cells, 0, width, axis=dim)
        tail = lax.slice_in_dim(cells, cells.shape[dim] - width, cells.shape[dim], axis=dim)
        cells = jnp.concatenate(
            [
                lax.ppermute(tail, axis, [(i, (i + 1) % count) for i in range(ends)]),
                cells,
                lax.ppermute(head, axis, [((i + 1) % count, i) for i in range(ends)]),
            ],
            axis=dim,
        )
    return cells


def stencil_step(padded, diffusion, velocity):
    center = padded[:, 1:-1, 1:-1, :]
    deeper = jnp.pad(center, ((0, 0), (0, 0), (0, 0), (1, 1)))
    result = (1.0 - 6.0 * diffusion) * center
    result = (
        result
        + (diffusion - 0.5 * velocity[0]) * padded[:, 2:, 1:-1, :]
        + (diffusion + 0.5 * velocity[0]) * padded[:, :-2, 1:-1, :]
    )
    result = (
        result
        + (diffusion - 0.5 * velocity[1]) * padded[:, 1:-1, 2:, :]
        + (diffusion + 0.5 * velocity[1]) * padded[:, 1:-1, :-2, :]
    )
    result = (
        result
        + (diffusion - 0.5 * velocity[2]) * deeper[:, :, :, 2:]
        + (diffusion + 0.5 * velocity[2]) * deeper[:, :, :, :-2]
    )
    return result


def on_device(probes, diffusion, velocity):
    field = probes
    for sweep_index in range(STEPS):
        padded = with_halo(field, (("gx", 1), ("gy", 2)), 1)
        field = stencil_step(padded, diffusion, velocity)
    probe_count = field.shape[0]
    flat = field.reshape(probe_count, -1)
    total_cells = flat.shape[1] * lax.axis_size("gx") * lax.axis_size("gy")
    local_gram = jnp.dot(
        flat, flat.T, precision=lax.Precision.HIGHEST, preferred_element_type=jnp.float32
    )
    gram = lax.psum(local_gram, ("gx", "gy")) * (1.0 / total_cells)
    lower = jnp.linalg.cholesky(gram)
    basis = jax.scipy.linalg.solve_triangular(lower, flat, lower=True)
    return (basis.reshape(field.shape), lower.T)


def solution(mesh):
    return jax.shard_map(
        on_device,
        mesh=mesh,
        in_specs=(P(None, "gx", "gy", None), P("gx", "gy", None), P(None, "gx", "gy", None)),
        out_specs=(P(None, "gx", "gy", None), P()),
        check_vma=False,
    )
```

profile of v0, /device:TPU:0, one launch (start us, length us, event | category | flops | bytes accessed | tf_op | source)
XLA Modules:
  0.0 177.1 jit_solution(3824144828677573553)
XLA Ops:
  0.6 0.0 copy-start.2
  0.6 4.8 %copy.33 = f32[32,16,8,256]{3,0,2,1:T(8,128)S(1)} copy(f32[32,16,8,256]{3,2,1,0:T(8,128)} %param.3) | data formatting | bytes 8388608 | tf_op args[0]
  5.5 2.4 %collective-permute-start.1 = (f32[32,1,8,256]{3,0,2,1:T(8,128)S(1)}, f32[32,1,8,256]{3,0,2,1:T(8,128)S(1)}, u32[]{:S(2)}, u32[]{:S(2)}) collective-permute-start(f32[32,1,8,256]{3,0,2,1:T(8,128)S(1)} %get-tuple-element.17), channel_id=1, source_target_pairs={{0,8},{8,16},{16,24},{1,9},{9,17},{17,25},{2,10},{10,18},{18,26},{... | collective-permute-start | bytes 786440 | tf_op jit(solution)/shard_map/ppermute | solution.py:17
  7.8 1.3 collective-permute-start
  9.1 0.0 collective-permute-done.1
  9.2 0.0 copy-done.2
  9.2 0.0 copy-start.4
  9.2 0.0 copy-start.5
  9.2 2.7 %constant_dynamic-update-slice_fusion.1 = f32[32,18,8,256]{3,0,2,1:T(8,128)S(1)} fusion(f32[32,18,8,256]{3,0,2,1:T(8,128)S(1)} %constant_dynamic-update-slice_fusion.2, f32[32,16,8,256]{3,2,1,0:T(8,128)S(1)} %copy-done.2), kind=kLoop, calls=%fused_computation.66 | loop fusion | bytes 8388608
  11.9 1.4 collective-permute-done
  13.4 0.0 copy-start.3
  13.4 0.1 fusion.29
  13.5 1.3 collective-permute-start.2
  14.8 4.6 %collective-permute-start.3 = (f32[32,18,1,256]{3,0,2,1:T(8,128)S(1)}, f32[32,18,1,256]{3,0,2,1:T(8,128)S(1)}, u32[]{:S(2)}, u32[]{:S(2)}) collective-permute-start(f32[32,18,1,256]{3,0,2,1:T(8,128)S(1)} %get-tuple-element.13), channel_id=1, source_target_pairs={{0,1},{1,2},{2,3},{3,4},{4,5},{5,6},{6,7},{8,9},{9,10},{10,11},{11... | collective-permute-start | bytes 1769480 | tf_op jit(solution)/shard_map/ppermute | solution.py:17
  19.4 0.0 copy-done.4
  19.4 0.0 copy-done.5
  19.4 0.1 bitcast_subtract_fusion.2
  19.5 8.2 %collective-permute-done.2 = f32[32,18,1,256]{3,0,2,1:T(8,128)S(1)} collective-permute-done((f32[32,18,1,256]{3,0,2,1:T(8,128)S(1)}, f32[32,18,1,256]{3,0,2,1:T(8,128)S(1)}, u32[]{:S(2)}, u32[]{:S(2)}) %collective-permute-start.2) | collective-permute-done | bytes 589856 | tf_op jit(solution)/shard_map/ppermute | solution.py:19
  27.7 16.3 %collective-permute-done.3 = f32[32,18,1,256]{3,0,2,1:T(8,128)S(1)} collective-permute-done((f32[32,18,1,256]{3,0,2,1:T(8,128)S(1)}, f32[32,18,1,256]{3,0,2,1:T(8,128)S(1)}, u32[]{:S(2)}, u32[]{:S(2)}) %collective-permute-start.3) | collective-permute-done | bytes 589856 | tf_op jit(solution)/shard_map/ppermute | solution.py:17
  44.1 0.0 copy-done.3
  44.1 9.5 %fusion.2 = f32[32,16,8,256]{3,0,2,1:T(8,128)S(1)} fusion(f32[32,16,8,256]{3,0,2,1:T(8,128)S(1)} %copy.33, f32[32,18,8,256]{3,0,2,1:T(8,128)} %copy-done.3, f32[32,18,1,256]{3,0,2,1:T(8,128)S(1)} %collective-permute-done.3, f32[32,18,1,256]{3,0,2,1:T(8,128)S(1)} %collective-permute-done.2, f32[32,1,8,256]{3,0,2,1:T(8,128)S(1)} %collective-permute-done.1, ...), kind=kLoop, calls=%fused_computation.6 | loop fusion | flops 17825792 | bytes 15728640 | tf_op jit(solution)/shard_map/add | solution.py:41
  53.5 0.0 copy-start.1
  53.6 2.2 %collective-permute-start.5 = (f32[32,1,8,256]{3,0,2,1:T(8,128)S(1)}, f32[32,1,8,256]{3,0,2,1:T(8,128)S(1)}, u32[]{:S(2)}, u32[]{:S(2)}) collective-permute-start(f32[32,1,8,256]{3,0,2,1:T(8,128)S(1)} %get-tuple-element.14), channel_id=1, source_target_pairs={{0,8},{8,16},{16,24},{1,9},{9,17},{17,25},{2,10},{10,18},{18,26},{... | collective-permute-start | bytes 786440 | tf_op jit(solution)/shard_map/ppermute | solution.py:17
  55.8 1.3 collective-permute-start.4
  57.1 0.0 collective-permute-done.5
  57.1 2.7 %collective-permute-done.4 = f32[32,1,8,256]{3,0,2,1:T(8,128)S(1)} collective-permute-done((f32[32,1,8,256]{3,0,2,1:T(8,128)S(1)}, f32[32,1,8,256]{3,0,2,1:T(8,128)S(1)}, u32[]{:S(2)}, u32[]{:S(2)}) %collective-permute-start.4) | collective-permute-done | bytes 262176 | tf_op jit(solution)/shard_map/ppermute | solution.py:19
  59.9 0.1 pad_maximum_fusion.14
  60.0 1.3 collective-permute-start.6
  61.3 5.2 %collective-permute-start.7 = (f32[32,18,1,256]{3,0,2,1:T(8,128)S(1)}, f32[32,18,1,256]{3,0,2,1:T(8,128)S(1)}, u32[]{:S(2)}, u32[]{:S(2)}) collective-permute-start(f32[32,18,1,256]{3,0,2,1:T(8,128)S(1)} %get-tuple-element.11), channel_id=1, source_target_pairs={{0,1},{1,2},{2,3},{3,4},{4,5},{5,6},{6,7},{8,9},{9,10},{10,11},{11... | collective-permute-start | bytes 1769480 | tf_op jit(solution)/shard_map/ppermute | solution.py:17
  66.5 7.9 %collective-permute-done.6 = f32[32,18,1,256]{3,0,2,1:T(8,128)S(1)} collective-permute-done((f32[32,18,1,256]{3,0,2,1:T(8,128)S(1)}, f32[32,18,1,256]{3,0,2,1:T(8,128)S(1)}, u32[]{:S(2)}, u32[]{:S(2)}) %collective-permute-start.6) | collective-permute-done | bytes 589856 | tf_op jit(solution)/shard_map/ppermute | solution.py:19
  74.4 0.0 copy-done.1
  74.4 17.1 %collective-permute-done.7 = f32[32,18,1,256]{3,0,2,1:T(8,128)S(1)} collective-permute-done((f32[32,18,1,256]{3,0,2,1:T(8,128)S(1)}, f32[32,18,1,256]{3,0,2,1:T(8,128)S(1)}, u32[]{:S(2)}, u32[]{:S(2)}) %collective-permute-start.7) | collective-permute-done | bytes 589856 | tf_op jit(solution)/shard_map/ppermute | solution.py:17
  91.5 17.3 %fusion.6 = f32[32,16,8,256]{3,0,2,1:T(8,128)S(1)} fusion(f32[32,16,8,256]{3,0,2,1:T(8,128)} %copy-done.1, f32[32,18,1,256]{3,0,2,1:T(8,128)S(1)} %collective-permute-done.7, f32[32,1,8,256]{3,0,2,1:T(8,128)S(1)} %collective-permute-done.4, f32[32,1,8,256]{3,0,2,1:T(8,128)S(1)} %collective-permute-done.5, f32[32,18,1,256]{3,0,2,1:T(8,128)S(1)} %collective-permute-done.6, ...), kind=kLoop, calls=%fused_computation.10 | loop fusion | flops 22020096 | bytes 11010048 | tf_op jit(solution)/shard_map/add | solution.py:41
  108.9 0.0 copy-start
  108.9 2.0 %copy-done = f32[32,16,8,256]{3,0,2,1:T(8,128)} copy-done((f32[32,16,8,256]{3,0,2,1:T(8,128)}, f32[32,16,8,256]{3,0,2,1:T(8,128)S(1)}, u32[]{:S(2)}) %copy-start) | copy-done | bytes 4194328
  110.9 3.4 %convolution_bitcast_fusion = f32[32,32]{0,1:T(8,128)S(1)} fusion(f32[32,16,8,256]{3,0,2,1:T(8,128)S(1)} %fusion.6), kind=kOutput, calls=%fused_computation.42 | convolution fusion | flops 402653184 | bytes 4198400 | tf_op jit(solution)/shard_map/dot_general | solution.py:56
  114.3 40.3 %psum.7 = f32[32,32]{0,1:T(8,128)S(1)} all-reduce(f32[32,32]{0,1:T(8,128)S(1)} %convolution_bitcast_fusion), channel_id=1, replica_groups=mesh['gx'=4,'gy'=8] {'gx','gy'}, use_global_device_ids=true, to_apply=%region_0.1 | all-reduce | flops 1024 | bytes 8192 | tf_op jit(solution)/shard_map/psum | solution.py:59
  154.6 0.1 copy.41
  154.7 2.9 %cholesky.16 = f32[32,32]{1,0:T(8,128)S(1)} custom-call(f32[32,32]{1,0:T(8,128)S(1)} %fusion.27), custom_call_target="Cholesky" | custom-call | tf_op jit(solution)/shard_map/jit(cholesky)/cholesky | solution.py:60
  157.7 0.6 compare_reduce_fusion
  158.3 0.7 fusion.28
  159.0 0.7 copy.46
  159.6 2.4 %custom-call.7 = f32[1,32,32]{1,2,0:T(8,128)S(1)} custom-call(f32[1,32,32]{2,1,0:T(8,128)S(1)} %get-tuple-element.26), custom_call_target="InvertDiagBlocksLowerTriangular" | custom-call | tf_op jit(solution)/shard_map/jit(_solve_triangular)/triangular_solve | solution.py:61
  162.1 4.6 %copy.52 = f32[4,8,128,256]{3,2,1,0:T(8,128)S(1)} copy(f32[4,8,128,256]{3,1,0,2:T(8,128)} %bitcast.37) | data formatting | bytes 8388608
  166.7 5.9 %fusion.24 = f32[32,16,8,256]{3,0,2,1:T(8,128)S(1)} fusion(f32[16,8,256,32]{2,1,0,3:T(8,128)S(1)} %bitcast.38, f32[1,32,32]{1,2,0:T(8,128)S(1)} %custom-call.7), kind=kOutput, calls=%fused_computation.40 | convolution fusion | flops 402653184 | bytes 8392704 | tf_op jit(solution)/shard_map/jit(_solve_triangular)/triangular_solve | solution.py:61
  172.7 4.4 %copy.45 = f32[32,16,8,256]{3,2,1,0:T(8,128)} copy(f32[32,16,8,256]{3,0,2,1:T(8,128)S(1)} %fusion.24) | data formatting | bytes 8388608
  (7 shorter events, 0.2 us)
Async XLA Ops:
  0.6 8.5 %copy-start.2 = (f32[32,16,8,256]{3,2,1,0:T(8,128)S(1)}, f32[32,16,8,256]{3,2,1,0:T(8,128)}, u32[]{:S(2)}) copy-start(f32[32,16,8,256]{3,2,1,0:T(8,128)} %param.3) | copy-start | bytes 12582916
  5.5 3.7 %collective-permute-start.1 = (f32[32,1,8,256]{3,0,2,1:T(8,128)S(1)}, f32[32,1,8,256]{3,0,2,1:T(8,128)S(1)}, u32[]{:S(2)}, u32[]{:S(2)}) collective-permute-start(f32[32,1,8,256]{3,0,2,1:T(8,128)S(1)} %get-tuple-element.17), channel_id=1, source_target_pairs={{0,8},{8,16},{16,24},{1,9},{9,17},{17,25},{2,10},{10,18},{18,26},{... | collective-permute-start | bytes 786440 | tf_op jit(solution)/shard_map/ppermute | solution.py:17
  7.8 5.5 %collective-permute-start = (f32[32,1,8,256]{3,0,2,1:T(8,128)S(1)}, f32[32,1,8,256]{3,0,2,1:T(8,128)S(1)}, u32[]{:S(2)}, u32[]{:S(2)}) collective-permute-start(f32[32,1,8,256]{3,0,2,1:T(8,128)S(1)} %get-tuple-element.16), channel_id=1, source_target_pairs={{8,0},{16,8},{24,16},{9,1},{17,9},{25,17},{10,2},{18,10},{26,18},{... | collective-permute-start | bytes 786440 | tf_op jit(solution)/shard_map/ppermute | solution.py:19
  9.2 10.2 %copy-start.4 = (f32[3,16,8,256]{3,2,1,0:T(8,128)S(1)}, f32[3,16,8,256]{3,2,1,0:T(8,128)}, u32[]{:S(2)}) copy-start(f32[3,16,8,256]{3,2,1,0:T(8,128)} %param.5) | copy-start | bytes 1179652
  9.2 10.2 %copy-start.5 = (f32[16,8,256]{2,1,0:T(8,128)S(1)}, f32[16,8,256]{2,1,0:T(8,128)}, u32[]{:S(2)}) copy-start(f32[16,8,256]{2,1,0:T(8,128)} %param.4) | copy-start | bytes 393220
  13.4 30.7 %copy-start.3 = (f32[32,18,8,256]{3,0,2,1:T(8,128)}, f32[32,18,8,256]{3,0,2,1:T(8,128)S(1)}, u32[]{:S(2)}) copy-start(f32[32,18,8,256]{3,0,2,1:T(8,128)S(1)} %constant_dynamic-update-slice_fusion) | copy-start | bytes 14155780
  13.5 14.2 %collective-permute-start.2 = (f32[32,18,1,256]{3,0,2,1:T(8,128)S(1)}, f32[32,18,1,256]{3,0,2,1:T(8,128)S(1)}, u32[]{:S(2)}, u32[]{:S(2)}) collective-permute-start(f32[32,18,1,256]{3,0,2,1:T(8,128)S(1)} %get-tuple-element.12), channel_id=1, source_target_pairs={{1,0},{2,1},{3,2},{4,3},{5,4},{6,5},{7,6},{9,8},{10,9},{11,10},{12... | collective-permute-start | bytes 1769480 | tf_op jit(solution)/shard_map/ppermute | solution.py:19
  14.8 29.3 %collective-permute-start.3 = (f32[32,18,1,256]{3,0,2,1:T(8,128)S(1)}, f32[32,18,1,256]{3,0,2,1:T(8,128)S(1)}, u32[]{:S(2)}, u32[]{:S(2)}) collective-permute-start(f32[32,18,1,256]{3,0,2,1:T(8,128)S(1)} %get-tuple-element.13), channel_id=1, source_target_pairs={{0,1},{1,2},{2,3},{3,4},{4,5},{5,6},{6,7},{8,9},{9,10},{10,11},{11... | collective-permute-start | bytes 1769480 | tf_op jit(solution)/shard_map/ppermute | solution.py:17
  53.5 20.9 %copy-start.1 = (f32[32,16,8,256]{3,0,2,1:T(8,128)}, f32[32,16,8,256]{3,0,2,1:T(8,128)S(1)}, u32[]{:S(2)}) copy-start(f32[32,16,8,256]{3,0,2,1:T(8,128)S(1)} %fusion.2) | copy-start | bytes 12582916
  53.6 3.5 %collective-permute-start.5 = (f32[32,1,8,256]{3,0,2,1:T(8,128)S(1)}, f32[32,1,8,256]{3,0,2,1:T(8,128)S(1)}, u32[]{:S(2)}, u32[]{:S(2)}) collective-permute-start(f32[32,1,8,256]{3,0,2,1:T(8,128)S(1)} %get-tuple-element.14), channel_id=1, source_target_pairs={{0,8},{8,16},{16,24},{1,9},{9,17},{17,25},{2,10},{10,18},{18,26},{... | collective-permute-start | bytes 786440 | tf_op jit(solution)/shard_map/ppermute | solution.py:17
  55.8 4.1 %collective-permute-start.4 = (f32[32,1,8,256]{3,0,2,1:T(8,128)S(1)}, f32[32,1,8,256]{3,0,2,1:T(8,128)S(1)}, u32[]{:S(2)}, u32[]{:S(2)}) collective-permute-start(f32[32,1,8,256]{3,0,2,1:T(8,128)S(1)} %get-tuple-element.15), channel_id=1, source_target_pairs={{8,0},{16,8},{24,16},{9,1},{17,9},{25,17},{10,2},{18,10},{26,18},{... | collective-permute-start | bytes 786440 | tf_op jit(solution)/shard_map/ppermute | solution.py:19
  60.0 14.4 %collective-permute-start.6 = (f32[32,18,1,256]{3,0,2,1:T(8,128)S(1)}, f32[32,18,1,256]{3,0,2,1:T(8,128)S(1)}, u32[]{:S(2)}, u32[]{:S(2)}) collective-permute-start(f32[32,18,1,256]{3,0,2,1:T(8,128)S(1)} %get-tuple-element.10), channel_id=1, source_target_pairs={{1,0},{2,1},{3,2},{4,3},{5,4},{6,5},{7,6},{9,8},{10,9},{11,10},{12... | collective-permute-start | bytes 1769480 | tf_op jit(solution)/shard_map/ppermute | solution.py:19
  61.3 30.2 %collective-permute-start.7 = (f32[32,18,1,256]{3,0,2,1:T(8,128)S(1)}, f32[32,18,1,256]{3,0,2,1:T(8,128)S(1)}, u32[]{:S(2)}, u32[]{:S(2)}) collective-permute-start(f32[32,18,1,256]{3,0,2,1:T(8,128)S(1)} %get-tuple-element.11), channel_id=1, source_target_pairs={{0,1},{1,2},{2,3},{3,4},{4,5},{5,6},{6,7},{8,9},{9,10},{10,11},{11... | collective-permute-start | bytes 1769480 | tf_op jit(solution)/shard_map/ppermute | solution.py:17
  108.9 2.0 %copy-start = (f32[32,16,8,256]{3,0,2,1:T(8,128)}, f32[32,16,8,256]{3,0,2,1:T(8,128)S(1)}, u32[]{:S(2)}) copy-start(f32[32,16,8,256]{3,0,2,1:T(8,128)S(1)} %fusion.6) | copy-start | bytes 12582916
where the time goes:
time: 178 us; the launch traced here: 177 us
  waiting for transfers between devices  53.8 us (30%)
  blocking collectives  40.3 us (23%)
  other arithmetic  33.7 us (19%)
  local copies, waits for them, and re-layouts  19.6 us (11%)
  starting transfers between devices  19.6 us (11%)
  matrix products  9.3 us (5%)
    psum x1, blocking collectives, on_device(): gram = lax.psum(local_gram, ('gx', 'gy')) * (1.0 / total_cells)  40.3 us
    ppermute x4, waiting for transfers between devices, with_halo(): lax.ppermute(tail, axis, [(i, (i + 1) % count) for i in range(ends)])  33.4 us
    add x2, other arithmetic, stencil_step(): result + (diffusion - 0.5 * velocity[2]) * deeper[:, :, :, 2:]  26.8 us
    ppermute x4, waiting for transfers between devices, with_halo(): lax.ppermute(head, axis, [((i + 1) % count, i) for i in range(ends)])  20.3 us
    unnamed x18, local copies, waits for them, and re-layouts  19.3 us
    ppermute x4, starting transfers between devices, with_halo(): lax.ppermute(tail, axis, [(i, (i + 1) % count) for i in range(ends)])  14.4 us
    another operation x1, matrix products, on_device(): basis = jax.scipy.linalg.solve_triangular(lower, flat, lower=True)  5.92 us
    ppermute x4, starting transfers between devices, with_halo(): lax.ppermute(head, axis, [((i + 1) % count, i) for i in range(ends)])  5.17 us
  transfers between devices with their start and end apart: 8, of which 6 were waited for; matrix products, arithmetic and copies ran while one was open for 2% of the time, Pallas kernels for 0%

commit v1 on v0

v1 whole, which is shorter than its diff:
```python
import functools

import jax
import jax.numpy as jnp
from jax import lax
from jax.experimental import pallas as pl
from jax.experimental.pallas import tpu as pltpu
from jax.sharding import PartitionSpec as P

F32 = jnp.float32
VMEM = pl.BlockSpec(memory_space=pltpu.VMEM)
ANY = pl.BlockSpec(memory_space=pl.ANY)
LANES = 128
W0, XP, XM, YP, YM, ZP, ZM = range(7)


def call(body, outs, ins, scratch=(), in_specs=None, out_specs=None, name=None):
    return pl.pallas_call(
        body,
        out_shape=[jax.ShapeDtypeStruct(s, F32) for s in outs],
        in_specs=in_specs or [VMEM] * len(ins),
        out_specs=out_specs or [VMEM] * len(outs),
        scratch_shapes=list(scratch),
        compiler_params=pltpu.CompilerParams(vmem_limit_bytes=24 << 20),
        name=name,
    )(*ins)


def spread_kernel(nx, ny, np_, nz, p_ref, d_ref, v_ref, u_ref, c_ref, up_ref, dn_ref, xlo_ref, xhi_ref):
    half = nx * np_
    parts = nz // LANES
    for x in range(nx):
        for y in range(ny):
            block = jnp.concatenate(
                [p_ref[pl.ds((x * parts + h) * ny + y, np_, stride=nx * parts * ny), :] for h in range(parts)], axis=1
            )
            u_ref[x, y] = block
            if y == 0:
                dn_ref[x * np_ : (x + 1) * np_, :] = block
            if y == ny - 1:
                up_ref[x * np_ : (x + 1) * np_, :] = block
            if x == 0:
                xlo_ref[y] = block
            if x == nx - 1:
                xhi_ref[y] = block
    d = d_ref[...]
    vx, vy, vz = 0.5 * v_ref[0], 0.5 * v_ref[1], 0.5 * v_ref[2]
    z = lax.broadcasted_iota(jnp.int32, (nx, ny, nz), 2)
    c_ref[W0] = 1.0 - 6.0 * d
    c_ref[XP] = d - vx
    c_ref[XM] = d + vx
    c_ref[YP] = d - vy
    c_ref[YM] = d + vy
    c_ref[ZP] = jnp.where(z == nz - 1, 0.0, d - vz)
    c_ref[ZM] = jnp.where(z == 0, 0.0, d + vz)
    for x in range(nx):
        dn_ref[half + x : half + x + 1, :] = c_ref[YM, x, 0:1, :]
        up_ref[half + x : half + x + 1, :] = c_ref[YP, x, ny - 1 : ny, :]


def sweep(nx, ny, nz, get, c_ref, lo, hi, ring, emit):
    def column(x, before, after):
        rows = [get(x, y) for y in range(ny)]
        for y in range(ny):
            here = rows[y]
            k = lambda i: c_ref[i, x, pl.ds(y, 1), :]
            total = k(W0) * here
            total = total + k(XP) * after(y) + k(XM) * before(y)
            if y + 1 < ny:
                total = total + k(YP) * rows[y + 1]
            elif ring is not None:
                total = total + k(YP) * ring(x, y)
            if y > 0:
                total = total + k(YM) * rows[y - 1]
            elif ring is not None:
                total = total + k(YM) * ring(x, y)
            total = total + k(ZP) * pltpu.roll(here, nz - 1, 1) + k(ZM) * pltpu.roll(here, 1, 1)
            emit(x, y, total)

    column(0, lambda y: lo[y], lambda y: get(1, y))

    @pl.loop(1, nx - 1)
    def _(x):
        column(x, lambda y: get(x - 1, y), lambda y: get(x + 1, y))

    column(nx - 1, lambda y: get(nx - 2, y), lambda y: hi[y])


def split(ny, low, inner, high):
    def get(x, y):
        return low[x] if y == 0 else high[x] if y == ny - 1 else inner[x, y - 1]

    def put(x, y, value):
        if y == 0:
            low[x] = value
        elif y == ny - 1:
            high[x] = value
        else:
            inner[x, y - 1] = value

    return get, put


def first_kernel(nx, ny, nz, u_ref, c_ref, lo_ref, hi_ref, v_ref, dn_ref, up_ref):
    _, put = split(ny, dn_ref, v_ref, up_ref)
    sweep(nx, ny, nz, lambda x, y: u_ref[x, y], c_ref, lo_ref, hi_ref, None, put)


def close_kernel(nx, ny, np_, c_ref, below_ref, above_ref, v_ref, dn_ref, up_ref, low_ref, high_ref, xlo_ref, xhi_ref):
    last = ny - 1
    for x in range(nx):
        rows = slice(x * np_, (x + 1) * np_)
        low_ref[x] = dn_ref[x] + c_ref[YM, x, 0:1, :] * below_ref[rows, :]
        high_ref[x] = up_ref[x] + c_ref[YP, x, last : last + 1, :] * above_ref[rows, :]
    get, _ = split(ny, low_ref, v_ref, high_ref)
    for y in range(ny):
        xlo_ref[y] = get(0, y)
        xhi_ref[y] = get(nx - 1, y)


def dot(a, b, dims):
    return lax.dot_general(a, b, (dims, ((), ())), precision=lax.Precision.HIGHEST, preferred_element_type=F32)


def second_kernel(
    nx, ny, np_, nz, u_ref, v_ref, vlow_ref, vhigh_ref, c_ref, below_ref, above_ref, lo_ref, hi_ref,
    w_ref, wlow_ref, whigh_ref, g_ref,
):
    half = nx * np_
    get, _ = split(ny, vlow_ref, v_ref, vhigh_ref)
    _, put = split(ny, wlow_ref, w_ref, whigh_ref)

    def ring(x, y):
        side = below_ref if y == 0 else above_ref
        return side[pl.ds(half + x, 1), :] * u_ref[x, y]

    g_ref[...] = jnp.zeros_like(g_ref)

    def emit(x, y, total):
        put(x, y, total)
        if 0 < y < ny - 1:
            g_ref[...] += dot(total, total, ((1,), (1,)))

    sweep(nx, ny, nz, get, c_ref, lo_ref, hi_ref, ring, emit)


def last_kernel(nx, ny, np_, copies, c_ref, below_ref, above_ref, g_in, wlow_in, whigh_in, wlow_ref, whigh_ref, g_ref):
    last = ny - 1
    gram = g_in[...]
    for x in range(nx):
        low = wlow_in[x] + c_ref[YM, x, 0:1, :] * below_ref[x]
        wlow_ref[x] = low
        gram = gram + dot(low, low, ((1,), (1,)))
        high = whigh_in[x] + c_ref[YP, x, last : last + 1, :] * above_ref[x]
        whigh_ref[x] = high
        gram = gram + dot(high, high, ((1,), (1,)))
    packed = jnp.concatenate([gram[8 * i : 8 * i + 8, :] for i in range(np_ // 8)], axis=1)
    for i in range(copies):
        g_ref[i] = packed


def basis_kernel(nx, ny, np_, scale, g_ref, w_ref, wlow_ref, whigh_ref, out_ref, factor_ref, inv_ref, stage, sems):
    get, _ = split(ny, wlow_ref, w_ref, whigh_ref)
    n = np_
    total = jnp.sum(g_ref[...], axis=0) * scale
    gram = jnp.concatenate([total[:, n * i : n * i + n] for i in range(n // 8)], axis=0)
    lane = lax.broadcasted_iota(jnp.int32, (1, n), 1)
    sub = lax.broadcasted_iota(jnp.int32, (n, 1), 0)
    right = jnp.where(lax.broadcasted_iota(jnp.int32, (n, n), 0) == lax.broadcasted_iota(jnp.int32, (n, n), 1), 1.0, 0.0)
    left = gram
    for k in range(n):
        r = lax.rsqrt(left[k : k + 1, k : k + 1])
        frow = left[k : k + 1, :] * r
        irow = right[k : k + 1, :] * r
        factor_ref[k : k + 1, :] = jnp.where(lane >= k, frow, 0.0)
        inv_ref[k : k + 1, :] = irow
        if k + 1 < n:
            col = jnp.where(sub > k, left[:, k : k + 1] * r, 0.0)
            left = left - col * frow
            right = right - col * irow
    inv = inv_ref[...]
    parts = wlow_ref.shape[2] // LANES
    group = parts * ny

    def copy(x):
        return pltpu.make_async_copy(stage.at[x % 2].reshape(n, group, LANES), out_ref.at[:, x], sems.at[x % 2])

    for x in range(nx):
        if x >= 2:
            copy(x - 2).wait()
        for y in range(ny):
            block = dot(inv, get(x, y), ((1,), (0,)))
            for h in range(parts):
                stage.at[x % 2][pl.ds(h * ny + y, n, stride=group), :] = block[:, h * LANES : (h + 1) * LANES]
        copy(x).start()
    copy(nx - 2).wait()
    copy(nx - 1).wait()


def on_device(probes, diffusion, velocity):
    np_, nx, ny, nz = probes.shape
    mx, my = lax.axis_size("gx"), lax.axis_size("gy")
    cells = mx * my * nx * ny * nz
    grid = (nx, ny, np_, nz)
    inner = (nx, ny - 2, np_, nz)
    plane = (nx, np_, nz)
    face = (ny, np_, nz)
    tall = (nx * np_ + nx, nz)
    up_x = [(i, i + 1) for i in range(mx - 1)]
    dn_x = [(i + 1, i) for i in range(mx - 1)]
    up_y = [(i, i + 1) for i in range(my - 1)]
    dn_y = [(i + 1, i) for i in range(my - 1)]

    parts = nz // LANES
    rows = probes.reshape(np_, nx, ny, parts, LANES).transpose(0, 1, 3, 2, 4).reshape(-1, LANES)
    u, coef, up, dn, xlo, xhi = call(
        functools.partial(spread_kernel, nx, ny, np_, nz),
        [grid, (7, nx, ny, nz), tall, tall, face, face],
        [rows, diffusion, velocity],
        name="spread",
    )
    below = lax.ppermute(up, "gy", up_y)
    above = lax.ppermute(dn, "gy", dn_y)
    before = lax.ppermute(xhi, "gx", up_x)
    after = lax.ppermute(xlo, "gx", dn_x)
    v, dn2, up2 = call(
        functools.partial(first_kernel, nx, ny, nz),
        [inner, plane, plane],
        [u, coef, before, after],
        name="first",
    )
    below2 = lax.ppermute(up2, "gy", up_y)
    above2 = lax.ppermute(dn2, "gy", dn_y)
    vlow, vhigh, xlo2, xhi2 = call(
        functools.partial(close_kernel, nx, ny, np_),
        [plane, plane, face, face],
        [coef, below, above, v, dn2, up2],
        name="close",
    )
    before2 = lax.ppermute(xhi2, "gx", up_x)
    after2 = lax.ppermute(xlo2, "gx", dn_x)
    w, wlow, whigh, gram = call(
        functools.partial(second_kernel, nx, ny, np_, nz),
        [inner, plane, plane, (np_, np_)],
        [u, v, vlow, vhigh, coef, below, above, before2, after2],
        name="second",
    )
    wlow, whigh, grams = call(
        functools.partial(last_kernel, nx, ny, np_, mx * my),
        [plane, plane, (mx * my, 8, np_ * np_ // 8)],
        [coef, below2, above2, gram, wlow, whigh],
        name="last",
    )
    grams = lax.all_to_all(grams, ("gx", "gy"), 0, 0, tiled=True)
    basis, factor = call(
        functools.partial(basis_kernel, nx, ny, np_, 1.0 / cells),
        [(np_, nx, parts * ny, LANES), (np_, np_)],
        [grams, w, wlow, whigh],
        scratch=[
            pltpu.VMEM((np_, np_), F32),
            pltpu.VMEM((2, np_ * parts * ny, LANES), F32),
            pltpu.SemaphoreType.DMA((2,)),
        ],
        out_specs=[ANY, VMEM],
        name="basis",
    )
    basis = basis.reshape(np_, nx, parts, ny, LANES).transpose(0, 1, 3, 2, 4).reshape(np_, nx, ny, nz)
    return basis, factor


def solution(mesh):
    return jax.shard_map(
        on_device,
        mesh=mesh,
        in_specs=(P(None, "gx", "gy", None), P("gx", "gy", None), P(None, "gx", "gy", None)),
        out_specs=(P(None, "gx", "gy", None), P()),
        check_vma=False,
    )
```

time: 178 us -> 91.2 us (0.51)
  other arithmetic: 33.7 us -> 0 us
  waiting for transfers between devices: 53.8 us -> 25.9 us
  Pallas kernels: 0 us -> 25.8 us
  blocking collectives: 40.3 us -> 16.8 us
  local copies, waits for them, and re-layouts: 19.6 us -> 4.08 us
  matrix products: 9.3 us -> 0 us
  starting transfers between devices: 19.6 us -> 17.4 us
    psum x1 -> x0, blocking collectives: 40.3 us -> none  [on_device(): gram = lax.psum(local_gram, ('gx', 'gy')) * (1.0 / total_cells)]
    ppermute x8, waiting for transfers between devices: 53.8 us -> 25.9 us  [the longest x1 18.4 us: on_device(): below = lax.ppermute(up, 'gy', up_y)]
    add x2 -> x0, other arithmetic: 26.8 us -> none  [stencil_step(): result + (diffusion - 0.5 * velocity[2]) * deeper[:, :, :, 2:]]
    pallas_call x0 -> x6, Pallas kernels: none -> 25.8 us  [call(): pl.pallas_call(body, out_shape=[jax.ShapeDtypeStruct(s, F32) for s in out...]
    all_to_all x0 -> x1, blocking collectives: none -> 16.8 us  [on_device(): grams = lax.all_to_all(grams, ('gx', 'gy'), 0, 0, tiled=True)]
    unnamed x18 -> x6, local copies, waits for them, and re-layouts: 19.3 us -> 4.08 us
    another operation x4 -> x0, other arithmetic: 6.03 us -> none  [the longest x3 3.6 us: on_device(): lower = jnp.linalg.cholesky(gram)]
    another operation x1 -> x0, matrix products: 5.92 us -> none  [on_device(): basis = jax.scipy.linalg.solve_triangular(lower, flat, lower=True)]
  transfers between devices with their start and end apart: 8 -> 8, of which waited for: 6 -> 3; matrix products, arithmetic and copies ran while one was open for 2% -> 0% of each run, Pallas kernels for 0% -> 11%
where the time goes in v1:
time: 91.2 us; the launch traced here: 90.8 us
  waiting for transfers between devices  25.9 us (28%)
  Pallas kernels  25.8 us (28%)
  starting transfers between devices  17.4 us (19%)
  blocking collectives  16.8 us (18%)
  local copies, waits for them, and re-layouts  4.08 us (4%)
    pallas_call x6, Pallas kernels, call(): pl.pallas_call(body, out_shape=[jax.ShapeDtypeStruct(s, F32) for s in out...  25.8 us
    ppermute x1, waiting for transfers between devices, on_device(): below = lax.ppermute(up, 'gy', up_y)  18.4 us
    all_to_all x1, blocking collectives, on_device(): grams = lax.all_to_all(grams, ('gx', 'gy'), 0, 0, tiled=True)  16.8 us
    ppermute x1, starting transfers between devices, on_device(): below = lax.ppermute(up, 'gy', up_y)  4.9 us
    ppermute x1, starting transfers between devices, on_device(): below2 = lax.ppermute(up2, 'gy', up_y)  4.58 us
    unnamed x6, local copies, waits for them, and re-layouts  4.08 us
    ppermute x1, waiting for transfers between devices, on_device(): after2 = lax.ppermute(xlo2, 'gx', dn_x)  3.83 us
    ppermute x1, waiting for transfers between devices, on_device(): after = lax.ppermute(xlo, 'gx', dn_x)  3.66 us
  transfers between devices with their start and end apart: 8, of which 3 were waited for; matrix products, arithmetic and copies ran while one was open for 0% of the time, Pallas kernels for 11%

profile of v1, /device:TPU:0, one launch (start us, length us, event | category | flops | bytes accessed | tf_op | source)
XLA Modules:
  0.0 90.8 jit_solution(17244339513719367448)
XLA Ops:
  0.6 0.0 copy-start
  0.6 2.2 %copy-done = f32[32,16,8,256]{3,2,1,0:T(8,128)S(1)} copy-done((f32[32,16,8,256]{3,2,1,0:T(8,128)S(1)}, f32[32,16,8,256]{3,2,1,0:T(8,128)}, u32[]{:S(2)}) %copy-start) | copy-done | bytes 4194328
  2.8 0.0 copy-start.1
  2.8 1.0 %copy-done.1 = f32[3,16,8,256]{3,2,1,0:T(8,128)S(1)} copy-done((f32[3,16,8,256]{3,2,1,0:T(8,128)S(1)}, f32[3,16,8,256]{3,2,1,0:T(8,128)}, u32[]{:S(2)}) %copy-start.1) | copy-done | bytes 393240
  3.8 0.0 copy-start.2
  3.8 0.9 copy-done.2
  4.7 2.5 %spread.1 = (f32[16,8,32,256]{3,2,1,0:T(8,128)S(1)}, f32[7,16,8,256]{3,2,1,0:T(8,128)S(1)}, f32[528,256]{1,0:T(8,128)S(1)}, f32[528,256]{1,0:T(8,128)S(1)}, f32[...) custom-call(f32[8192,128]{1,0:T(8,128)S(1)} %bitcast.10, f32[16,8,256]{2,1,0:T(8,128)S(1)} %copy-done.2, ...), custom_call_target="tpu_custom_call" | custom-call | tf_op jit(solution)/shard_map/spread/pallas_call | solution.py:18
  7.3 4.9 %collective-permute-start.4 = (f32[528,256]{1,0:T(8,128)S(1)}, f32[528,256]{1,0:T(8,128)S(1)}, u32[]{:S(2)}, u32[]{:S(2)}) collective-permute-start(f32[528,256]{1,0:T(8,128)S(1)} %get-tuple-element.31), channel_id=1, source_target_pairs={{0,1},{1,2},{2,3},{3,4},{4,5},{5,6},{6,7},{8,9},{9,10},{10,11},{11... | collective-permute-start | bytes 1622024 | tf_op jit(solution)/shard_map/ppermute | solution.py:222
  12.2 1.3 %collective-permute-start.5 = (f32[528,256]{1,0:T(8,128)S(1)}, f32[528,256]{1,0:T(8,128)S(1)}, u32[]{:S(2)}, u32[]{:S(2)}) collective-permute-start(f32[528,256]{1,0:T(8,128)S(1)} %get-tuple-element.32), channel_id=1, source_target_pairs={{1,0},{2,1},{3,2},{4,3},{5,4},{6,5},{7,6},{9,8},{10,9},{11,10},{12... | collective-permute-start | bytes 1622024 | tf_op jit(solution)/shard_map/ppermute | solution.py:223
  13.5 1.5 %collective-permute-start = (f32[8,32,256]{2,1,0:T(8,128)S(1)}, f32[8,32,256]{2,1,0:T(8,128)S(1)}, u32[]{:S(2)}, u32[]{:S(2)}) collective-permute-start(f32[8,32,256]{2,1,0:T(8,128)S(1)} %get-tuple-element.26), channel_id=1, source_target_pairs={{0,8},{8,16},{16,24},{1,9},{9,17},{17,25},{2,10},{10,18},{18,26},{... | collective-permute-start | bytes 786440 | tf_op jit(solution)/shard_map/ppermute | solution.py:224
  15.0 1.3 %collective-permute-start.1 = (f32[8,32,256]{2,1,0:T(8,128)S(1)}, f32[8,32,256]{2,1,0:T(8,128)S(1)}, u32[]{:S(2)}, u32[]{:S(2)}) collective-permute-start(f32[8,32,256]{2,1,0:T(8,128)S(1)} %get-tuple-element.27), channel_id=1, source_target_pairs={{8,0},{16,8},{24,16},{9,1},{17,9},{25,17},{10,2},{18,10},{26,18},{... | collective-permute-start | bytes 786440 | tf_op jit(solution)/shard_map/ppermute | solution.py:225
  16.3 0.0 collective-permute-done.lo_ref
  16.3 3.7 %collective-permute-done.1.hi_ref = f32[8,32,256]{2,1,0:T(8,128)S(1)} collective-permute-done((f32[8,32,256]{2,1,0:T(8,128)S(1)}, f32[8,32,256]{2,1,0:T(8,128)S(1)}, u32[]{:S(2)}, u32[]{:S(2)}) %collective-permute-start.1) | collective-permute-done | bytes 262176 | tf_op jit(solution)/shard_map/ppermute | solution.py:225
  19.9 3.4 %first.1 = (f32[16,6,32,256]{3,2,1,0:T(8,128)S(1)}, f32[16,32,256]{2,1,0:T(8,128)S(1)}, f32[16,32,256]{2,1,0:T(8,128)S(1)}) custom-call(f32[16,8,32,256]{3,2,1,0:T(8,128)S(1)} %get-tuple-element.25.u_ref, f32[7,16,8,256]{3,2,1,0:T(8,128)S(1)} %get-tuple-element.24.c_ref, f32[8,32,256]{2,1,0:T(8,128)S(1)} %collective-permute-done.lo_ref, ...), custom_call_target="tpu_custom_call" | custom-call | tf_op jit(solution)/shard_map/first/pallas_call | solution.py:18
  23.3 4.6 %collective-permute-start.2 = (f32[16,32,256]{2,1,0:T(8,128)S(1)}, f32[16,32,256]{2,1,0:T(8,128)S(1)}, u32[]{:S(2)}, u32[]{:S(2)}) collective-permute-start(f32[16,32,256]{2,1,0:T(8,128)S(1)} %get-tuple-element.28.up_ref), channel_id=1, source_target_pairs={{0,1},{1,2},{2,3},{3,4},{4,5},{5,6},{6,7},{8,9},{9,10},{10,11},{11... | collective-permute-start | bytes 1572872 | tf_op jit(solution)/shard_map/ppermute | solution.py:232
  27.9 1.3 %collective-permute-start.3 = (f32[16,32,256]{2,1,0:T(8,128)S(1)}, f32[16,32,256]{2,1,0:T(8,128)S(1)}, u32[]{:S(2)}, u32[]{:S(2)}) collective-permute-start(f32[16,32,256]{2,1,0:T(8,128)S(1)} %get-tuple-element.29.dn_ref), channel_id=1, source_target_pairs={{1,0},{2,1},{3,2},{4,3},{5,4},{6,5},{7,6},{9,8},{10,9},{11,10},{12... | collective-permute-start | bytes 1572872 | tf_op jit(solution)/shard_map/ppermute | solution.py:233
  29.2 18.4 %collective-permute-done.4.below_ref = f32[528,256]{1,0:T(8,128)S(1)} collective-permute-done((f32[528,256]{1,0:T(8,128)S(1)}, f32[528,256]{1,0:T(8,128)S(1)}, u32[]{:S(2)}, u32[]{:S(2)}) %collective-permute-start.4) | collective-permute-done | bytes 540704 | tf_op jit(solution)/shard_map/ppermute | solution.py:222
  47.6 0.0 collective-permute-done.5.above_ref
  47.6 0.2 close.1
  47.8 1.3 %collective-permute-start.6 = (f32[8,32,256]{2,1,0:T(8,128)S(1)}, f32[8,32,256]{2,1,0:T(8,128)S(1)}, u32[]{:S(2)}, u32[]{:S(2)}) collective-permute-start(f32[8,32,256]{2,1,0:T(8,128)S(1)} %get-tuple-element.35), channel_id=1, source_target_pairs={{0,8},{8,16},{16,24},{1,9},{9,17},{17,25},{2,10},{10,18},{18,26},{... | collective-permute-start | bytes 786440 | tf_op jit(solution)/shard_map/ppermute | solution.py:240
  49.1 1.3 %collective-permute-start.7 = (f32[8,32,256]{2,1,0:T(8,128)S(1)}, f32[8,32,256]{2,1,0:T(8,128)S(1)}, u32[]{:S(2)}, u32[]{:S(2)}) collective-permute-start(f32[8,32,256]{2,1,0:T(8,128)S(1)} %get-tuple-element.36), channel_id=1, source_target_pairs={{8,0},{16,8},{24,16},{9,1},{17,9},{25,17},{10,2},{18,10},{26,18},{... | collective-permute-start | bytes 786440 | tf_op jit(solution)/shard_map/ppermute | solution.py:241
  50.4 0.0 collective-permute-done.6.lo_ref
  50.4 3.8 %collective-permute-done.7.hi_ref = f32[8,32,256]{2,1,0:T(8,128)S(1)} collective-permute-done((f32[8,32,256]{2,1,0:T(8,128)S(1)}, f32[8,32,256]{2,1,0:T(8,128)S(1)}, u32[]{:S(2)}, u32[]{:S(2)}) %collective-permute-start.7) | collective-permute-done | bytes 262176 | tf_op jit(solution)/shard_map/ppermute | solution.py:241
  54.2 6.4 %second.1 = (f32[16,6,32,256]{3,2,1,0:T(8,128)S(1)}, f32[16,32,256]{2,1,0:T(8,128)S(1)}, f32[16,32,256]{2,1,0:T(8,128)S(1)}, f32[32,32]{1,0:T(8,128)S(1)}) custom-call(f32[16,8,32,256]{3,2,1,0:T(8,128)S(1)} %get-tuple-element.25.u_ref, f32[16,6,32,256]{3,2,1,0:T(8,128)S(1)} %get-tuple-element.30.v_ref, f32[16,32,256]{2,1,0:T(8,128)S(1)} %get-tuple-element.33.vlow_ref, ...), custom_call_target="tpu_custom_call" | custom-call | tf_op jit(solution)/shard_map/second/pallas_call | solution.py:18
  60.7 0.0 collective-permute-done.2.below_ref
  60.7 0.0 collective-permute-done.3.above_ref
  60.7 1.1 %last.1 = (f32[16,32,256]{2,1,0:T(8,128)S(1)}, f32[16,32,256]{2,1,0:T(8,128)S(1)}, f32[32,8,128]{2,1,0:T(8,128)S(1)}) custom-call(f32[7,16,8,256]{3,2,1,0:T(8,128)S(1)} %get-tuple-element.24.c_ref, f32[16,32,256]{2,1,0:T(8,128)S(1)} %collective-permute-done.2.below_ref, f32[16,32,256]{2,1,0:T(8,128)S(1)} %collective-permute-done.3.above_ref, ...), custom_call_target="tpu_custom_call" | custom-call | tf_op jit(solution)/shard_map/last/pallas_call | solution.py:18
  61.8 16.8 %all_to_all.5.g_ref = f32[32,8,128]{2,1,0:T(8,128)S(1)} all-to-all(f32[32,8,128]{2,1,0:T(8,128)S(1)} %get-tuple-element.40), channel_id=1, replica_groups=mesh['gx'=4,'gy'=8] {'gx','gy'}, dimensions={0} | all-to-all | bytes 262144 | tf_op jit(solution)/shard_map/all_to_all | solution.py:254
  78.6 12.2 %basis.1 = (f32[32,16,16,128]{3,2,1,0:T(8,128)}, f32[32,32]{1,0:T(8,128)}) custom-call(f32[32,8,128]{2,1,0:T(8,128)S(1)} %all_to_all.5.g_ref, f32[16,6,32,256]{3,2,1,0:T(8,128)S(1)} %get-tuple-element.41.w_ref, f32[16,32,256]{2,1,0:T(8,128)S(1)} %get-tuple-element.42.wlow_ref, f32[16,32,256]{2,1,0:T(8,128)S(1)} %get-tuple-element.43.whigh_ref), custom_call_target="tpu_custom_call" | custom-call | tf_op jit(solution)/shard_map/basis/pallas_call | solution.py:18
Async XLA Ops:
  0.6 2.2 %copy-start = (f32[32,16,8,256]{3,2,1,0:T(8,128)S(1)}, f32[32,16,8,256]{3,2,1,0:T(8,128)}, u32[]{:S(2)}) copy-start(f32[32,16,8,256]{3,2,1,0:T(8,128)} %param.3) | copy-start | bytes 12582916
  2.8 1.0 %copy-start.1 = (f32[3,16,8,256]{3,2,1,0:T(8,128)S(1)}, f32[3,16,8,256]{3,2,1,0:T(8,128)}, u32[]{:S(2)}) copy-start(f32[3,16,8,256]{3,2,1,0:T(8,128)} %v_ref.1) | copy-start | bytes 1179652
  3.8 0.9 copy-start.2
  7.3 40.4 %collective-permute-start.4 = (f32[528,256]{1,0:T(8,128)S(1)}, f32[528,256]{1,0:T(8,128)S(1)}, u32[]{:S(2)}, u32[]{:S(2)}) collective-permute-start(f32[528,256]{1,0:T(8,128)S(1)} %get-tuple-element.31), channel_id=1, source_target_pairs={{0,1},{1,2},{2,3},{3,4},{4,5},{5,6},{6,7},{8,9},{9,10},{10,11},{11... | collective-permute-start | bytes 1622024 | tf_op jit(solution)/shard_map/ppermute | solution.py:222
  12.2 35.5 %collective-permute-start.5 = (f32[528,256]{1,0:T(8,128)S(1)}, f32[528,256]{1,0:T(8,128)S(1)}, u32[]{:S(2)}, u32[]{:S(2)}) collective-permute-start(f32[528,256]{1,0:T(8,128)S(1)} %get-tuple-element.32), channel_id=1, source_target_pairs={{1,0},{2,1},{3,2},{4,3},{5,4},{6,5},{7,6},{9,8},{10,9},{11,10},{12... | collective-permute-start | bytes 1622024 | tf_op jit(solution)/shard_map/ppermute | solution.py:223
  13.5 2.8 %collective-permute-start = (f32[8,32,256]{2,1,0:T(8,128)S(1)}, f32[8,32,256]{2,1,0:T(8,128)S(1)}, u32[]{:S(2)}, u32[]{:S(2)}) collective-permute-start(f32[8,32,256]{2,1,0:T(8,128)S(1)} %get-tuple-element.26), channel_id=1, source_target_pairs={{0,8},{8,16},{16,24},{1,9},{9,17},{17,25},{2,10},{10,18},{18,26},{... | collective-permute-start | bytes 786440 | tf_op jit(solution)/shard_map/ppermute | solution.py:224
  15.0 5.0 %collective-permute-start.1 = (f32[8,32,256]{2,1,0:T(8,128)S(1)}, f32[8,32,256]{2,1,0:T(8,128)S(1)}, u32[]{:S(2)}, u32[]{:S(2)}) collective-permute-start(f32[8,32,256]{2,1,0:T(8,128)S(1)} %get-tuple-element.27), channel_id=1, source_target_pairs={{8,0},{16,8},{24,16},{9,1},{17,9},{25,17},{10,2},{18,10},{26,18},{... | collective-permute-start | bytes 786440 | tf_op jit(solution)/shard_map/ppermute | solution.py:225
  23.3 37.4 %collective-permute-start.2 = (f32[16,32,256]{2,1,0:T(8,128)S(1)}, f32[16,32,256]{2,1,0:T(8,128)S(1)}, u32[]{:S(2)}, u32[]{:S(2)}) collective-permute-start(f32[16,32,256]{2,1,0:T(8,128)S(1)} %get-tuple-element.28.up_ref), channel_id=1, source_target_pairs={{0,1},{1,2},{2,3},{3,4},{4,5},{5,6},{6,7},{8,9},{9,10},{10,11},{11... | collective-permute-start | bytes 1572872 | tf_op jit(solution)/shard_map/ppermute | solution.py:232
  27.9 32.8 %collective-permute-start.3 = (f32[16,32,256]{2,1,0:T(8,128)S(1)}, f32[16,32,256]{2,1,0:T(8,128)S(1)}, u32[]{:S(2)}, u32[]{:S(2)}) collective-permute-start(f32[16,32,256]{2,1,0:T(8,128)S(1)} %get-tuple-element.29.dn_ref), channel_id=1, source_target_pairs={{1,0},{2,1},{3,2},{4,3},{5,4},{6,5},{7,6},{9,8},{10,9},{11,10},{12... | collective-permute-start | bytes 1572872 | tf_op jit(solution)/shard_map/ppermute | solution.py:233
  47.8 2.6 %collective-permute-start.6 = (f32[8,32,256]{2,1,0:T(8,128)S(1)}, f32[8,32,256]{2,1,0:T(8,128)S(1)}, u32[]{:S(2)}, u32[]{:S(2)}) collective-permute-start(f32[8,32,256]{2,1,0:T(8,128)S(1)} %get-tuple-element.35), channel_id=1, source_target_pairs={{0,8},{8,16},{16,24},{1,9},{9,17},{17,25},{2,10},{10,18},{18,26},{... | collective-permute-start | bytes 786440 | tf_op jit(solution)/shard_map/ppermute | solution.py:240
  49.1 5.1 %collective-permute-start.7 = (f32[8,32,256]{2,1,0:T(8,128)S(1)}, f32[8,32,256]{2,1,0:T(8,128)S(1)}, u32[]{:S(2)}, u32[]{:S(2)}) collective-permute-start(f32[8,32,256]{2,1,0:T(8,128)S(1)} %get-tuple-element.36), channel_id=1, source_target_pairs={{8,0},{16,8},{24,16},{9,1},{17,9},{25,17},{10,2},{18,10},{26,18},{... | collective-permute-start | bytes 786440 | tf_op jit(solution)/shard_map/ppermute | solution.py:241

commit v2 on v1

v2 whole, which is shorter than its diff:
```python
import functools

import jax
import jax.numpy as jnp
from jax import lax
from jax.experimental import pallas as pl
from jax.experimental.pallas import tpu as pltpu
from jax.sharding import PartitionSpec as P

F32 = jnp.float32
BF16 = jnp.bfloat16
VMEM = pl.BlockSpec(memory_space=pltpu.VMEM)
ANY = pl.BlockSpec(memory_space=pl.ANY)
LANES = 128
BLOCK = 8
W0, XP, XM, YP, YM, ZP, ZM = range(7)


def call(body, outs, ins, scratch=(), in_specs=None, out_specs=None, name=None, vmem=24):
    return pl.pallas_call(
        body,
        out_shape=[jax.ShapeDtypeStruct(s, F32) for s in outs],
        in_specs=in_specs or [VMEM] * len(ins),
        out_specs=out_specs or [VMEM] * len(outs),
        scratch_shapes=list(scratch),
        compiler_params=pltpu.CompilerParams(vmem_limit_bytes=vmem << 20),
        name=name,
    )(*ins)


def edge_kernel(nx, ny, np_, parts, p_ref, d_ref, v_ref, up_ref, dn_ref, xlo_ref, xhi_ref, terms, sem):
    last = ny - 1
    half = nx * np_
    copies = []
    for x in range(nx):
        rows = pl.ds(x * np_, np_)
        for h in range(parts):
            lanes = pl.ds(h * LANES, LANES)
            copies.append((p_ref.at[:, x, h, last, :], up_ref.at[rows, lanes]))
            copies.append((p_ref.at[:, x, h, 0, :], dn_ref.at[rows, lanes]))
    for h in range(parts):
        for i, y in enumerate((0, last)):
            copies.append((d_ref.at[:, h, y, :], terms.at[i, :, pl.ds(h * LANES, LANES)]))
            copies.append((v_ref.at[1, :, h, y, :], terms.at[2 + i, :, pl.ds(h * LANES, LANES)]))
    layers = np_ * 2 * parts * ny
    some = parts * ny
    for ref, first, outer in ((xlo_ref, 0, 0), (xhi_ref, nx - 2, nx - 1)):
        face = ref.at[pl.ds(0, layers)].reshape(np_, 2, parts, ny, LANES)
        copies.append((p_ref.at[:, pl.ds(first, 2)], face))
        copies.append((d_ref.at[outer], ref.at[pl.ds(layers, some)].reshape(parts, ny, LANES)))
        copies.append((v_ref.at[:, outer], ref.at[pl.ds(layers + some, 3 * some)].reshape(3, parts, ny, LANES)))
    copies = [pltpu.make_async_copy(src, dst, sem) for src, dst in copies]
    for copy in copies:
        copy.start()
    for copy in copies:
        copy.wait()
    dn_ref[half : half + nx, :] = terms[0] + 0.5 * terms[2]
    up_ref[half : half + nx, :] = terms[1] - 0.5 * terms[3]


def coefficients(d, vx, vy, vz):
    z = lax.broadcasted_iota(jnp.int32, d.shape, d.ndim - 1)
    return (
        1.0 - 6.0 * d,
        d - 0.5 * vx,
        d + 0.5 * vx,
        d - 0.5 * vy,
        d + 0.5 * vy,
        jnp.where(z == d.shape[-1] - 1, 0.0, d - 0.5 * vz),
        jnp.where(z == 0, 0.0, d + 0.5 * vz),
    )


def spread_kernel(nx, ny, np_, nz, p_ref, d_ref, v_ref, u_ref, c_ref):
    parts = nz // LANES
    for x in range(nx):
        for y in range(ny):
            for h in range(parts):
                block = p_ref[pl.ds((x * parts + h) * ny + y, np_, stride=nx * parts * ny), :]
                u_ref[x, y, :, h * LANES : (h + 1) * LANES] = block
    for i, c in enumerate(coefficients(d_ref[...], v_ref[0], v_ref[1], v_ref[2])):
        c_ref[i] = c


def column(ny, nz, ys, row, before, after, coef, ring, emit):
    rows = {y: row(y) for y in sorted({n for y in ys for n in (y - 1, y, y + 1) if 0 <= n < ny})}
    for y in ys:
        here = rows[y]
        k = lambda i: coef(i, y)
        total = k(W0) * here
        total = total + k(XP) * after(y) + k(XM) * before(y)
        if y + 1 < ny:
            total = total + k(YP) * rows[y + 1]
        elif ring is not None:
            total = total + k(YP) * ring(y)
        if y > 0:
            total = total + k(YM) * rows[y - 1]
        elif ring is not None:
            total = total + k(YM) * ring(y)
        total = total + k(ZP) * pltpu.roll(here, nz - 1, 1) + k(ZM) * pltpu.roll(here, 1, 1)
        emit(y, total)


def sweep(nx, ny, nz, ys, get, c_ref, lo, hi, ring, emit):
    def at(x, before, after):
        outside = None if ring is None else lambda y: ring(x, y)
        coef = lambda i, y: c_ref[i, x, pl.ds(y, 1), :]
        column(ny, nz, ys, lambda y: get(x, y), before, after, coef, outside, lambda y, total: emit(x, y, total))

    at(0, lo, lambda y: get(1, y))

    @pl.loop(1, nx - 1)
    def _(x):
        at(x, lambda y: get(x - 1, y), lambda y: get(x + 1, y))

    at(nx - 1, lambda y: get(nx - 2, y), hi)


def split(ny, low, inner, high):
    def get(x, y):
        return low[x] if y == 0 else high[x] if y == ny - 1 else inner[x, y - 1]

    def put(x, y, value):
        if y == 0:
            low[x] = value
        elif y == ny - 1:
            high[x] = value
        else:
            inner[x, y - 1] = value

    return get, put


def first_kernel(nx, ny, np_, nz, u_ref, c_ref, lo_ref, hi_ref, v_ref, dn_ref, up_ref, vlo_ref, vhi_ref, k_ref):
    parts = nz // LANES
    layers = np_ * 2 * parts * ny

    def layer(ref, i):
        def get(y):
            each = [ref[pl.ds((i * parts + h) * ny + y, np_, stride=2 * parts * ny), :] for h in range(parts)]
            return jnp.concatenate(each, axis=1)

        return get

    for side, ref in enumerate((lo_ref, hi_ref)):
        tile = lambda i: jnp.concatenate(
            [ref[layers + (i * parts + h) * ny : layers + (i * parts + h + 1) * ny, :] for h in range(parts)], axis=1
        )
        for i, c in enumerate(coefficients(tile(0), tile(1), tile(2), tile(3))):
            k_ref[side, i] = c

    def outer(side, row, before, after, out_ref):
        def emit(y, total):
            out_ref[y] = total

        column(ny, nz, range(ny), row, before, after, lambda i, y: k_ref[side, i, pl.ds(y, 1), :], None, emit)

    get = lambda x, y: u_ref[x, y]
    outer(0, layer(lo_ref, 1), layer(lo_ref, 0), lambda y: get(0, y), vlo_ref)
    outer(1, layer(hi_ref, 0), lambda y: get(nx - 1, y), layer(hi_ref, 1), vhi_ref)
    _, put = split(ny, dn_ref, v_ref, up_ref)
    sweep(nx, ny, nz, range(ny), get, c_ref, layer(lo_ref, 1), layer(hi_ref, 0), None, put)


def close_kernel(nx, ny, np_, c_ref, below_ref, above_ref, dn_ref, up_ref, low_ref, high_ref, xlo_ref, xhi_ref):
    last = ny - 1
    for x in range(nx):
        rows = slice(x * np_, (x + 1) * np_)
        low = c_ref[YM, x, 0:1, :] * below_ref[rows, :]
        high = c_ref[YP, x, last : last + 1, :] * above_ref[rows, :]
        low_ref[x] = dn_ref[x] + low
        high_ref[x] = up_ref[x] + high
        if x == 0:
            xlo_ref[0], xlo_ref[1] = low, high
        if x == nx - 1:
            xhi_ref[0], xhi_ref[1] = low, high


def pieces(a):
    high = a.astype(BF16)
    rest = a - high.astype(F32)
    mid = rest.astype(BF16)
    return high, mid, (rest - mid.astype(F32)).astype(BF16)


def square(a):
    stack = jnp.concatenate(pieces(a), axis=0)
    return lax.dot_general(stack, stack, (((1,), (1,)), ((), ())), preferred_element_type=F32)


def fold(n, a):
    block = lambda i, j: a[i * n : i * n + n, j * n : j * n + n]
    return block(0, 0) + ((block(0, 1) + block(1, 0)) + (block(1, 1) + (block(0, 2) + block(2, 0))))


def face(ref):
    return lambda y: ref[y]


def middle_kernel(nx, ny, nz, v_ref, c_ref, lo_ref, hi_ref, dn_ref, up_ref, w_ref, g_ref, dn_out, up_out):
    g_ref[...] = jnp.zeros_like(g_ref)

    def emit(x, y, total):
        w_ref[x, y - 2] = total
        g_ref[...] += square(total)

    sweep(nx, ny, nz, range(2, ny - 2), lambda x, y: v_ref[x, y - 1], c_ref, face(lo_ref), face(hi_ref), None, emit)
    dn_out[...] = dn_ref[...]
    up_out[...] = up_ref[...]


def border_kernel(
    nx, ny, np_, nz, u_ref, v_ref, vlow_ref, vhigh_ref, c_ref, below_ref, above_ref, lo_ref, hi_ref,
    w_ref, wlow_ref, whigh_ref, g_ref,
):
    half = nx * np_
    get, _ = split(ny, vlow_ref, v_ref, vhigh_ref)

    def ring(x, y):
        side = below_ref if y == 0 else above_ref
        return side[pl.ds(half + x, 1), :] * u_ref[x, y]

    g_ref[...] = jnp.zeros_like(g_ref)

    def emit(x, y, total):
        if y == 0:
            wlow_ref[x] = total
        elif y == ny - 1:
            whigh_ref[x] = total
        else:
            w_ref[x, 0 if y == 1 else 1] = total
            g_ref[...] += square(total)

    sweep(nx, ny, nz, (0, 1, ny - 2, ny - 1), get, c_ref, face(lo_ref), face(hi_ref), ring, emit)


def last_kernel(
    nx, ny, np_, copies, c_ref, below_ref, above_ref, lo_ref, hi_ref, ga_ref, gb_ref, wlow_in, whigh_in,
    wlow_ref, whigh_ref, g_ref,
):
    last = ny - 1
    gram = ga_ref[...] + gb_ref[...]
    for x in range(nx):
        low = wlow_in[x] + c_ref[YM, x, 0:1, :] * below_ref[x]
        high = whigh_in[x] + c_ref[YP, x, last : last + 1, :] * above_ref[x]
        if x == 0:
            low = low + c_ref[XM, x, 0:1, :] * lo_ref[0]
            high = high + c_ref[XM, x, last : last + 1, :] * lo_ref[1]
        if x == nx - 1:
            low = low + c_ref[XP, x, 0:1, :] * hi_ref[0]
            high = high + c_ref[XP, x, last : last + 1, :] * hi_ref[1]
        wlow_ref[x] = low
        whigh_ref[x] = high
        gram = gram + (square(low) + square(high))
    gram = fold(np_, gram)
    packed = jnp.concatenate([gram[8 * i : 8 * i + 8, :] for i in range(np_ // 8)], axis=1)
    for i in range(copies):
        g_ref[i] = packed


def factor_and_inverse(n, gram, factor_ref, inv_ref):
    eye = lax.broadcasted_iota(jnp.int32, (n, n), 0) == lax.broadcasted_iota(jnp.int32, (n, n), 1)
    a = jnp.concatenate([gram, jnp.where(eye, 1.0, 0.0)], axis=1)
    sub = lax.broadcasted_iota(jnp.int32, (n, 2 * n), 0)
    lane = lax.broadcasted_iota(jnp.int32, (1, n), 1)
    for k0 in range(0, n, BLOCK):
        cols = [jnp.broadcast_to(a[k0:, k : k + 1], (n - k0, 2 * n)) for k in range(k0, k0 + BLOCK)]
        low, rows = a[k0:], sub[k0:]
        for j in range(BLOCK):
            k = k0 + j
            r = lax.rsqrt(cols[j][j : j + 1, :])
            row = low[j : j + 1, :] * r
            factor_ref[k : k + 1, :] = jnp.where(lane >= k, row[:, :n], 0.0)
            inv_ref[k : k + 1, :] = row[:, n:]
            col = jnp.where(rows > k, cols[j] * r, 0.0)
            for m in range(j + 1, BLOCK):
                cols[m] = cols[m] - col * (cols[m][j : j + 1, :] * r)
            low = low - col * row
        a = low if k0 == 0 else jnp.concatenate([a[:k0], low], axis=0)


def basis_kernel(
    nx, ny, np_, scale, g_ref, w_ref, wside_ref, wlow_ref, whigh_ref, out_ref, factor_ref, inv_ref, stage, sems
):
    def get(x, y):
        if y in (0, ny - 1):
            return wlow_ref[x] if y == 0 else whigh_ref[x]
        if y in (1, ny - 2):
            return wside_ref[x, 0 if y == 1 else 1]
        return w_ref[x, y - 2]

    n = np_
    total = jnp.sum(g_ref[...], axis=0) * scale
    gram = jnp.concatenate([total[:, n * i : n * i + n] for i in range(n // 8)], axis=0)
    factor_and_inverse(n, gram, factor_ref, inv_ref)
    high, mid, low = pieces(inv_ref[...])
    none = jnp.zeros_like(high)
    left = jnp.concatenate(
        [jnp.concatenate(row, axis=1) for row in ((high, high, high), (mid, mid, none), (low, none, none))], axis=0
    )
    parts = wlow_ref.shape[2] // LANES
    group = parts * ny
    copies = []
    for x in range(nx):
        for y in range(ny):
            right = jnp.concatenate(pieces(get(x, y)), axis=0)
            terms = lax.dot_general(left, right, (((1,), (0,)), ((), ())), preferred_element_type=F32)
            block = terms[:n] + (terms[n : 2 * n] + terms[2 * n :])
            for h in range(parts):
                stage.at[x][pl.ds(h * ny + y, n, stride=group), :] = block[:, h * LANES : (h + 1) * LANES]
        copy = pltpu.make_async_copy(stage.at[x].reshape(n, group, LANES), out_ref.at[:, x], sems.at[x])
        copy.start()
        copies.append(copy)
    for copy in copies:
        copy.wait()


def on_device(probes, diffusion, velocity):
    np_, nx, ny, nz = probes.shape
    mx, my = lax.axis_size("gx"), lax.axis_size("gy")
    cells = mx * my * nx * ny * nz
    grid = (nx, ny, np_, nz)
    corner = (2, np_, nz)
    square_sum = (3 * np_, 3 * np_)
    plane = (nx, np_, nz)
    face_shape = (ny, np_, nz)
    tall = (nx * np_ + nx, nz)
    up_x = [(i, i + 1) for i in range(mx - 1)]
    dn_x = [(i + 1, i) for i in range(mx - 1)]
    up_y = [(i, i + 1) for i in range(my - 1)]
    dn_y = [(i + 1, i) for i in range(my - 1)]

    parts = nz // LANES
    tiled = lambda a: jnp.swapaxes(a.reshape(a.shape[:-1] + (parts, LANES)), -2, -3)
    tiles = tiled(probes)
    wide = ((2 * np_ + 4) * parts * ny, LANES)
    up, dn, xlo, xhi = call(
        functools.partial(edge_kernel, nx, ny, np_, parts),
        [tall, tall, wide, wide],
        [tiles, tiled(diffusion), tiled(velocity)],
        scratch=[pltpu.VMEM((4, nx, nz), F32), pltpu.SemaphoreType.DMA],
        in_specs=[pl.BlockSpec(memory_space=pltpu.HBM)] * 3,
        name="edge",
        vmem=61,
    )
    below = lax.ppermute(up, "gy", up_y)
    above = lax.ppermute(dn, "gy", dn_y)
    before = lax.ppermute(xhi, "gx", up_x)
    after = lax.ppermute(xlo, "gx", dn_x)
    u, coef = call(
        functools.partial(spread_kernel, nx, ny, np_, nz),
        [grid, (7, nx, ny, nz)],
        [tiles.reshape(-1, LANES), diffusion, velocity],
        name="spread",
    )
    v, dn2, up2, vlo, vhi = call(
        functools.partial(first_kernel, nx, ny, np_, nz),
        [(nx, ny - 2, np_, nz), plane, plane, face_shape, face_shape],
        [u, coef, before, after],
        scratch=[pltpu.VMEM((2, 7, ny, nz), F32)],
        name="first",
    )
    w, gram, dn2, up2 = call(
        functools.partial(middle_kernel, nx, ny, nz),
        [(nx, ny - 4, np_, nz), square_sum, plane, plane],
        [v, coef, vlo, vhi, dn2, up2],
        name="middle",
    )
    below2 = lax.ppermute(up2, "gy", up_y)
    above2 = lax.ppermute(dn2, "gy", dn_y)
    vlow, vhigh, xlo3, xhi3 = call(
        functools.partial(close_kernel, nx, ny, np_),
        [plane, plane, corner, corner],
        [coef, below, above, dn2, up2],
        name="close",
    )
    before3 = lax.ppermute(xhi3, "gx", up_x)
    after3 = lax.ppermute(xlo3, "gx", dn_x)
    wside, wlow, whigh, gram2 = call(
        functools.partial(border_kernel, nx, ny, np_, nz),
        [(nx, 2, np_, nz), plane, plane, square_sum],
        [u, v, vlow, vhigh, coef, below, above, vlo, vhi],
        name="border",
    )
    wlow, whigh, grams = call(
        functools.partial(last_kernel, nx, ny, np_, mx * my),
        [plane, plane, (mx * my, 8, np_ * np_ // 8)],
        [coef, below2, above2, before3, after3, gram, gram2, wlow, whigh],
        name="last",
    )
    grams = lax.all_to_all(grams, ("gx", "gy"), 0, 0, tiled=True)
    basis, factor = call(
        functools.partial(basis_kernel, nx, ny, np_, 1.0 / cells),
        [(np_, nx, parts * ny, LANES), (np_, np_)],
        [grams, w, wside, wlow, whigh],
        scratch=[
            pltpu.VMEM((np_, np_), F32),
            pltpu.VMEM((nx, np_ * parts * ny, LANES), F32),
            pltpu.SemaphoreType.DMA((nx,)),
        ],
        out_specs=[ANY, VMEM],
        name="basis",
    )
    basis = basis.reshape(np_, nx, parts, ny, LANES).transpose(0, 1, 3, 2, 4).reshape(np_, nx, ny, nz)
    return basis, factor


def solution(mesh):
    return jax.shard_map(
        on_device,
        mesh=mesh,
        in_specs=(P(None, "gx", "gy", None), P("gx", "gy", None), P(None, "gx", "gy", None)),
        out_specs=(P(None, "gx", "gy", None), P()),
        check_vma=False,
    )
```

time: 91.2 us -> 78.9 us (0.87)
  waiting for transfers between devices: 25.9 us -> 13.5 us
  starting transfers between devices: 17.4 us -> 21.4 us
  local copies, waits for them, and re-layouts: 4.08 us -> 2.19 us
  Pallas kernels: 25.8 us -> 24.4 us
    ppermute x1, waiting for transfers between devices: 18.4 us -> 1.87 us  [on_device(): below = lax.ppermute(up, 'gy', up_y)]
    ppermute x2, waiting for transfers between devices: 3.83 us -> 10.8 us  [the longest x1 10.8 us: on_device(): after3 = lax.ppermute(xlo3, 'gx', dn_x)]
    ppermute x1, waiting for transfers between devices: 3.66 us -> 0.01 us  [on_device(): after = lax.ppermute(xlo, 'gx', dn_x)]
    ppermute x2, starting transfers between devices: 2.6 us -> 6.23 us  [the longest x1 4.94 us: on_device(): before3 = lax.ppermute(xhi3, 'gx', up_x)]
    unnamed x6, local copies, waits for them, and re-layouts: 4.08 us -> 2.19 us
    pallas_call x6 -> x8, Pallas kernels: 25.8 us -> 24.4 us  [call(): pl.pallas_call(body, out_shape=[jax.ShapeDtypeStruct(s, F32) for s in out...]
    ppermute x1, starting transfers between devices: 1.47 us -> 2.39 us  [on_device(): before = lax.ppermute(xhi, 'gx', up_x)]
  transfers between devices with their start and end apart: 8 -> 8, of which waited for: 3 -> 3; matrix products, arithmetic and copies ran while one was open for 0% -> 0% of each run, Pallas kernels for 11% -> 21%
where the time goes in v2:
time: 78.9 us; the launch traced here: 78.5 us
  Pallas kernels  24.4 us (31%)
  starting transfers between devices  21.4 us (27%)
  blocking collectives  16.2 us (21%)
  waiting for transfers between devices  13.5 us (17%)
  local copies, waits for them, and re-layouts  2.19 us (3%)
  between operations  0.8 us (1%)
    pallas_call x8, Pallas kernels, call(): pl.pallas_call(body, out_shape=[jax.ShapeDtypeStruct(s, F32) for s in out...  24.4 us
    all_to_all x1, blocking collectives, on_device(): grams = lax.all_to_all(grams, ('gx', 'gy'), 0, 0, tiled=True)  16.2 us
    ppermute x1, waiting for transfers between devices, on_device(): after3 = lax.ppermute(xlo3, 'gx', dn_x)  10.8 us
    ppermute x1, starting transfers between devices, on_device(): before3 = lax.ppermute(xhi3, 'gx', up_x)  4.94 us
    ppermute x1, starting transfers between devices, on_device(): below2 = lax.ppermute(up2, 'gy', up_y)  4.58 us
    ppermute x1, starting transfers between devices, on_device(): below = lax.ppermute(up, 'gy', up_y)  4.29 us
    ppermute x1, starting transfers between devices, on_device(): before = lax.ppermute(xhi, 'gx', up_x)  2.39 us
    unnamed x6, local copies, waits for them, and re-layouts  2.19 us
  transfers between devices with their start and end apart: 8, of which 3 were waited for; matrix products, arithmetic and copies ran while one was open for 0% of the time, Pallas kernels for 21%

profile of v2, /device:TPU:0, one launch (start us, length us, event | category | flops | bytes accessed | tf_op | source)
XLA Modules:
  0.0 78.5 jit_solution(16970417386399602574)
XLA Ops:
  0.6 0.0 copy-start.2
  0.6 0.0 copy-start.1
  0.6 3.2 %edge.1 = (f32[528,256]{1,0:T(8,128)}, f32[528,256]{1,0:T(8,128)}, f32[1088,128]{1,0:T(8,128)}, f32[1088,128]{1,0:T(8,128)}) custom-call(f32[32,16,2,8,128]{4,3,2,1,0:T(8,128)} %bitcast.16, f32[16,2,8,128]{3,2,1,0:T(8,128)} %bitcast.19, f32[3,16,2,8,128]{4,3,2,1,0:T(8,128)} %bitcast.18), custom_call_target="tpu_custom_call" | custom-call | tf_op jit(solution)/shard_map/edge/pallas_call | solution.py:20
  3.9 2.4 %collective-permute-start = (f32[1088,128]{1,0:T(8,128)}, f32[1088,128]{1,0:T(8,128)S(1)}, u32[]{:S(2)}, u32[]{:S(2)}) collective-permute-start(f32[1088,128]{1,0:T(8,128)} %get-tuple-element.32), channel_id=1, source_target_pairs={{0,8},{8,16},{16,24},{1,9},{9,17},{17,25},{2,10},{10,18},{18,26},{... | collective-permute-start | bytes 1671176 | tf_op jit(solution)/shard_map/ppermute | solution.py:348
  6.3 1.3 %collective-permute-start.1 = (f32[1088,128]{1,0:T(8,128)}, f32[1088,128]{1,0:T(8,128)S(1)}, u32[]{:S(2)}, u32[]{:S(2)}) collective-permute-start(f32[1088,128]{1,0:T(8,128)} %get-tuple-element.33), channel_id=1, source_target_pairs={{8,0},{16,8},{24,16},{9,1},{17,9},{25,17},{10,2},{18,10},{26,18},{... | collective-permute-start | bytes 1671176 | tf_op jit(solution)/shard_map/ppermute | solution.py:349
  7.6 4.3 %collective-permute-start.4 = (f32[528,256]{1,0:T(8,128)}, f32[528,256]{1,0:T(8,128)S(1)}, u32[]{:S(2)}, u32[]{:S(2)}) collective-permute-start(f32[528,256]{1,0:T(8,128)} %get-tuple-element.41), channel_id=1, source_target_pairs={{0,1},{1,2},{2,3},{3,4},{4,5},{5,6},{6,7},{8,9},{9,10},{10,11},{11... | collective-permute-start | bytes 1622024 | tf_op jit(solution)/shard_map/ppermute | solution.py:346
  11.9 1.3 %collective-permute-start.5 = (f32[528,256]{1,0:T(8,128)}, f32[528,256]{1,0:T(8,128)S(1)}, u32[]{:S(2)}, u32[]{:S(2)}) collective-permute-start(f32[528,256]{1,0:T(8,128)} %get-tuple-element.42), channel_id=1, source_target_pairs={{1,0},{2,1},{3,2},{4,3},{5,4},{6,5},{7,6},{9,8},{10,9},{11,10},{12... | collective-permute-start | bytes 1622024 | tf_op jit(solution)/shard_map/ppermute | solution.py:347
  13.2 0.0 copy-done.2
  13.2 0.0 copy-done.1
  13.2 0.0 copy-start
  13.2 2.2 %copy-done = f32[32,16,8,256]{3,2,1,0:T(8,128)S(1)} copy-done((f32[32,16,8,256]{3,2,1,0:T(8,128)S(1)}, f32[32,16,8,256]{3,2,1,0:T(8,128)}, u32[]{:S(2)}) %copy-start) | copy-done | bytes 4194328
  15.4 2.5 %spread.1 = (f32[16,8,32,256]{3,2,1,0:T(8,128)S(1)}, f32[7,16,8,256]{3,2,1,0:T(8,128)S(1)}) custom-call(f32[8192,128]{1,0:T(8,128)S(1)} %bitcast.17, f32[16,8,256]{2,1,0:T(8,128)S(1)} %copy-done.2, f32[3,16,8,256]{3,2,1,0:T(8,128)S(1)} %copy-done.1), custom_call_target="tpu_custom_call" | custom-call | tf_op jit(solution)/shard_map/spread/pallas_call | solution.py:20
  17.9 0.0 collective-permute-done.lo_ref
  17.9 0.0 collective-permute-done.1.hi_ref
  17.9 4.2 %first.1 = (f32[16,6,32,256]{3,2,1,0:T(8,128)S(1)}, f32[16,32,256]{2,1,0:T(8,128)S(1)}, f32[16,32,256]{2,1,0:T(8,128)S(1)}, f32[8,32,256]{2,1,0:T(8,128)S(1)}, f32[8,32,256]{2,1,0:T(8,128)S(1)}) custom-call(f32[16,8,32,256]{3,2,1,0:T(8,128)S(1)} %get-tuple-element.31.u_ref, f32[7,16,8,256]{3,2,1,0:T(8,128)S(1)} %get-tuple-element.30.c_ref, ...), custom_call_target="tpu_custom_call" | custom-call | tf_op jit(solution)/shard_map/first/pallas_call | solution.py:20
  22.1 5.1 %middle.1 = (f32[16,4,32,256]{3,2,1,0:T(8,128)S(1)}, f32[96,96]{1,0:T(8,128)S(1)}, f32[16,32,256]{2,1,0:T(8,128)S(1)}, f32[16,32,256]{2,1,0:T(8,128)S(1)}) custom-call(f32[16,6,32,256]{3,2,1,0:T(8,128)S(1)} %get-tuple-element.34.v_ref, f32[7,16,8,256]{3,2,1,0:T(8,128)S(1)} %get-tuple-element.30.c_ref, f32[8,32,256]{2,1,0:T(8,128)S(1)} %get-tuple-element.35.lo_ref, ...), custom_call_target="tpu_custom_call" | custom-call | tf_op jit(solution)/shard_map/middle/pallas_call | solution.py:20
  27.2 4.6 %collective-permute-start.2 = (f32[16,32,256]{2,1,0:T(8,128)S(1)}, f32[16,32,256]{2,1,0:T(8,128)S(1)}, u32[]{:S(2)}, u32[]{:S(2)}) collective-permute-start(f32[16,32,256]{2,1,0:T(8,128)S(1)} %get-tuple-element.39.up_ref), channel_id=1, source_target_pairs={{0,1},{1,2},{2,3},{3,4},{4,5},{5,6},{6,7},{8,9},{9,10},{10,11},{11... | collective-permute-start | bytes 1572872 | tf_op jit(solution)/shard_map/ppermute | solution.py:369
  31.8 1.3 %collective-permute-start.3 = (f32[16,32,256]{2,1,0:T(8,128)S(1)}, f32[16,32,256]{2,1,0:T(8,128)S(1)}, u32[]{:S(2)}, u32[]{:S(2)}) collective-permute-start(f32[16,32,256]{2,1,0:T(8,128)S(1)} %get-tuple-element.40.dn_ref), channel_id=1, source_target_pairs={{1,0},{2,1},{3,2},{4,3},{5,4},{6,5},{7,6},{9,8},{10,9},{11,10},{12... | collective-permute-start | bytes 1572872 | tf_op jit(solution)/shard_map/ppermute | solution.py:370
  33.1 1.9 %collective-permute-done.4.below_ref = f32[528,256]{1,0:T(8,128)S(1)} collective-permute-done((f32[528,256]{1,0:T(8,128)}, f32[528,256]{1,0:T(8,128)S(1)}, u32[]{:S(2)}, u32[]{:S(2)}) %collective-permute-start.4) | collective-permute-done | bytes 540704 | tf_op jit(solution)/shard_map/ppermute | solution.py:346
  34.9 0.0 collective-permute-done.5.above_ref
  34.9 0.1 close.1
  35.1 4.9 %collective-permute-start.6 = (f32[2,32,256]{2,1,0:T(8,128)S(1)}, f32[2,32,256]{2,1,0:T(8,128)S(1)}, u32[]{:S(2)}, u32[]{:S(2)}) collective-permute-start(f32[2,32,256]{2,1,0:T(8,128)S(1)} %get-tuple-element.43), channel_id=1, source_target_pairs={{0,8},{8,16},{16,24},{1,9},{9,17},{17,25},{2,10},{10,18},{18,26},{... | collective-permute-start | bytes 196616 | tf_op jit(solution)/shard_map/ppermute | solution.py:377
  40.0 1.3 %collective-permute-start.7 = (f32[2,32,256]{2,1,0:T(8,128)S(1)}, f32[2,32,256]{2,1,0:T(8,128)S(1)}, u32[]{:S(2)}, u32[]{:S(2)}) collective-permute-start(f32[2,32,256]{2,1,0:T(8,128)S(1)} %get-tuple-element.44), channel_id=1, source_target_pairs={{8,0},{16,8},{24,16},{9,1},{17,9},{25,17},{10,2},{18,10},{26,18},{... | collective-permute-start | bytes 196616 | tf_op jit(solution)/shard_map/ppermute | solution.py:378
  41.3 4.3 %border.1 = (f32[16,2,32,256]{3,2,1,0:T(8,128)S(1)}, f32[16,32,256]{2,1,0:T(8,128)S(1)}, f32[16,32,256]{2,1,0:T(8,128)S(1)}, f32[96,96]{1,0:T(8,128)S(1)}) custom-call(f32[16,8,32,256]{3,2,1,0:T(8,128)S(1)} %get-tuple-element.31.u_ref, f32[16,6,32,256]{3,2,1,0:T(8,128)S(1)} %get-tuple-element.34.v_ref, f32[16,32,256]{2,1,0:T(8,128)S(1)} %get-tuple-element.46.vlow_ref, ...), custom_call_target="tpu_custom_call" | custom-call | tf_op jit(solution)/shard_map/border/pallas_call | solution.py:20
  45.7 0.0 collective-permute-done.6.lo_ref
  45.7 10.8 %collective-permute-done.7.hi_ref = f32[2,32,256]{2,1,0:T(8,128)S(1)} collective-permute-done((f32[2,32,256]{2,1,0:T(8,128)S(1)}, f32[2,32,256]{2,1,0:T(8,128)S(1)}, u32[]{:S(2)}, u32[]{:S(2)}) %collective-permute-start.7) | collective-permute-done | bytes 65568 | tf_op jit(solution)/shard_map/ppermute | solution.py:378
  56.5 0.8 %collective-permute-done.2.below_ref = f32[16,32,256]{2,1,0:T(8,128)S(1)} collective-permute-done((f32[16,32,256]{2,1,0:T(8,128)S(1)}, f32[16,32,256]{2,1,0:T(8,128)S(1)}, u32[]{:S(2)}, u32[]{:S(2)}) %collective-permute-start.2) | collective-permute-done | bytes 524320 | tf_op jit(solution)/shard_map/ppermute | solution.py:369
  57.3 0.0 collective-permute-done.3.above_ref
  57.3 0.9 %last.1 = (f32[16,32,256]{2,1,0:T(8,128)S(1)}, f32[16,32,256]{2,1,0:T(8,128)S(1)}, f32[32,8,128]{2,1,0:T(8,128)S(1)}) custom-call(f32[7,16,8,256]{3,2,1,0:T(8,128)S(1)} %get-tuple-element.30.c_ref, f32[16,32,256]{2,1,0:T(8,128)S(1)} %collective-permute-done.2.below_ref, f32[16,32,256]{2,1,0:T(8,128)S(1)} %collective-permute-done.3.above_ref, ...), custom_call_target="tpu_custom_call" | custom-call | tf_op jit(solution)/shard_map/last/pallas_call | solution.py:20
  58.2 16.2 %all_to_all.5.g_ref = f32[32,8,128]{2,1,0:T(8,128)S(1)} all-to-all(f32[32,8,128]{2,1,0:T(8,128)S(1)} %get-tuple-element.51), channel_id=1, replica_groups=mesh['gx'=4,'gy'=8] {'gx','gy'}, dimensions={0} | all-to-all | bytes 262144 | tf_op jit(solution)/shard_map/all_to_all | solution.py:391
  74.4 4.1 %basis.1 = (f32[32,16,16,128]{3,2,1,0:T(8,128)}, f32[32,32]{1,0:T(8,128)}) custom-call(f32[32,8,128]{2,1,0:T(8,128)S(1)} %all_to_all.5.g_ref, f32[16,4,32,256]{3,2,1,0:T(8,128)S(1)} %get-tuple-element.52.w_ref, f32[16,2,32,256]{3,2,1,0:T(8,128)S(1)} %get-tuple-element.53.wside_ref, f32[16,32,256]{2,1,0:T(8,128)S(1)} %get-tuple-element.54.wlow_ref, ...), custom_call_target="tpu_custom_call" | custom-call | tf_op jit(solution)/shard_map/basis/pallas_call | solution.py:20
Async XLA Ops:
  0.6 12.6 %copy-start.2 = (f32[16,8,256]{2,1,0:T(8,128)S(1)}, f32[16,8,256]{2,1,0:T(8,128)}, u32[]{:S(2)}) copy-start(f32[16,8,256]{2,1,0:T(8,128)} %d_ref.1) | copy-start | bytes 393220
  0.6 12.6 %copy-start.1 = (f32[3,16,8,256]{3,2,1,0:T(8,128)S(1)}, f32[3,16,8,256]{3,2,1,0:T(8,128)}, u32[]{:S(2)}) copy-start(f32[3,16,8,256]{3,2,1,0:T(8,128)} %v_ref.1) | copy-start | bytes 1179652
  3.9 14.0 %collective-permute-start = (f32[1088,128]{1,0:T(8,128)}, f32[1088,128]{1,0:T(8,128)S(1)}, u32[]{:S(2)}, u32[]{:S(2)}) collective-permute-start(f32[1088,128]{1,0:T(8,128)} %get-tuple-element.32), channel_id=1, source_target_pairs={{0,8},{8,16},{16,24},{1,9},{9,17},{17,25},{2,10},{10,18},{18,26},{... | collective-permute-start | bytes 1671176 | tf_op jit(solution)/shard_map/ppermute | solution.py:348
  6.3 11.6 %collective-permute-start.1 = (f32[1088,128]{1,0:T(8,128)}, f32[1088,128]{1,0:T(8,128)S(1)}, u32[]{:S(2)}, u32[]{:S(2)}) collective-permute-start(f32[1088,128]{1,0:T(8,128)} %get-tuple-element.33), channel_id=1, source_target_pairs={{8,0},{16,8},{24,16},{9,1},{17,9},{25,17},{10,2},{18,10},{26,18},{... | collective-permute-start | bytes 1671176 | tf_op jit(solution)/shard_map/ppermute | solution.py:349
  7.6 27.4 %collective-permute-start.4 = (f32[528,256]{1,0:T(8,128)}, f32[528,256]{1,0:T(8,128)S(1)}, u32[]{:S(2)}, u32[]{:S(2)}) collective-permute-start(f32[528,256]{1,0:T(8,128)} %get-tuple-element.41), channel_id=1, source_target_pairs={{0,1},{1,2},{2,3},{3,4},{4,5},{5,6},{6,7},{8,9},{9,10},{10,11},{11... | collective-permute-start | bytes 1622024 | tf_op jit(solution)/shard_map/ppermute | solution.py:346
  11.9 23.1 %collective-permute-start.5 = (f32[528,256]{1,0:T(8,128)}, f32[528,256]{1,0:T(8,128)S(1)}, u32[]{:S(2)}, u32[]{:S(2)}) collective-permute-start(f32[528,256]{1,0:T(8,128)} %get-tuple-element.42), channel_id=1, source_target_pairs={{1,0},{2,1},{3,2},{4,3},{5,4},{6,5},{7,6},{9,8},{10,9},{11,10},{12... | collective-permute-start | bytes 1622024 | tf_op jit(solution)/shard_map/ppermute | solution.py:347
  13.2 2.2 %copy-start = (f32[32,16,8,256]{3,2,1,0:T(8,128)S(1)}, f32[32,16,8,256]{3,2,1,0:T(8,128)}, u32[]{:S(2)}) copy-start(f32[32,16,8,256]{3,2,1,0:T(8,128)} %param.3) | copy-start | bytes 12582916
  27.2 30.1 %collective-permute-start.2 = (f32[16,32,256]{2,1,0:T(8,128)S(1)}, f32[16,32,256]{2,1,0:T(8,128)S(1)}, u32[]{:S(2)}, u32[]{:S(2)}) collective-permute-start(f32[16,32,256]{2,1,0:T(8,128)S(1)} %get-tuple-element.39.up_ref), channel_id=1, source_target_pairs={{0,1},{1,2},{2,3},{3,4},{4,5},{5,6},{6,7},{8,9},{9,10},{10,11},{11... | collective-permute-start | bytes 1572872 | tf_op jit(solution)/shard_map/ppermute | solution.py:369
  31.8 25.5 %collective-permute-start.3 = (f32[16,32,256]{2,1,0:T(8,128)S(1)}, f32[16,32,256]{2,1,0:T(8,128)S(1)}, u32[]{:S(2)}, u32[]{:S(2)}) collective-permute-start(f32[16,32,256]{2,1,0:T(8,128)S(1)} %get-tuple-element.40.dn_ref), channel_id=1, source_target_pairs={{1,0},{2,1},{3,2},{4,3},{5,4},{6,5},{7,6},{9,8},{10,9},{11,10},{12... | collective-permute-start | bytes 1572872 | tf_op jit(solution)/shard_map/ppermute | solution.py:370
  35.1 10.6 %collective-permute-start.6 = (f32[2,32,256]{2,1,0:T(8,128)S(1)}, f32[2,32,256]{2,1,0:T(8,128)S(1)}, u32[]{:S(2)}, u32[]{:S(2)}) collective-permute-start(f32[2,32,256]{2,1,0:T(8,128)S(1)} %get-tuple-element.43), channel_id=1, source_target_pairs={{0,8},{8,16},{16,24},{1,9},{9,17},{17,25},{2,10},{10,18},{18,26},{... | collective-permute-start | bytes 196616 | tf_op jit(solution)/shard_map/ppermute | solution.py:377
  40.0 16.5 %collective-permute-start.7 = (f32[2,32,256]{2,1,0:T(8,128)S(1)}, f32[2,32,256]{2,1,0:T(8,128)S(1)}, u32[]{:S(2)}, u32[]{:S(2)}) collective-permute-start(f32[2,32,256]{2,1,0:T(8,128)S(1)} %get-tuple-element.44), channel_id=1, source_target_pairs={{8,0},{16,8},{24,16},{9,1},{17,9},{25,17},{10,2},{18,10},{26,18},{... | collective-permute-start | bytes 196616 | tf_op jit(solution)/shard_map/ppermute | solution.py:378

commit v3 on v2

--- a/solution.py
+++ b/solution.py
@@ -16,19 +16,28 @@
 W0, XP, XM, YP, YM, ZP, ZM = range(7)
 
 
-def call(body, outs, ins, scratch=(), in_specs=None, out_specs=None, name=None, vmem=24):
+def call(body, outs, ins, scratch=(), in_specs=None, out_specs=None, name=None, vmem=24, aliases=None):
     return pl.pallas_call(
         body,
         out_shape=[jax.ShapeDtypeStruct(s, F32) for s in outs],
         in_specs=in_specs or [VMEM] * len(ins),
         out_specs=out_specs or [VMEM] * len(outs),
         scratch_shapes=list(scratch),
+        input_output_aliases=aliases or {},
         compiler_params=pltpu.CompilerParams(vmem_limit_bytes=vmem << 20),
         name=name,
     )(*ins)
 
 
-def edge_kernel(nx, ny, np_, parts, p_ref, d_ref, v_ref, up_ref, dn_ref, xlo_ref, xhi_ref, terms, sem):
+def move(pairs, sem):
+    copies = [pltpu.make_async_copy(src, dst, sem) for src, dst in pairs]
+    for copy in copies:
+        copy.start()
+    for copy in copies:
+        copy.wait()
+
+
+def edge_kernel(nx, ny, np_, parts, p_ref, d_ref, v_ref, up_ref, dn_ref, terms, sem):
     last = ny - 1
     half = nx * np_
     copies = []
@@ -42,20 +51,20 @@
         for i, y in enumerate((0, last)):
             copies.append((d_ref.at[:, h, y, :], terms.at[i, :, pl.ds(h * LANES, LANES)]))
             copies.append((v_ref.at[1, :, h, y, :], terms.at[2 + i, :, pl.ds(h * LANES, LANES)]))
+    move(copies, sem)
+    dn_ref[half : half + nx, :] = terms[0] + 0.5 * terms[2]
+    up_ref[half : half + nx, :] = terms[1] - 0.5 * terms[3]
+
+
+def side_kernel(nx, ny, np_, parts, p_ref, d_ref, v_ref, lo_ref, hi_ref, sem):
     layers = np_ * 2 * parts * ny
     some = parts * ny
-    for ref, first, outer in ((xlo_ref, 0, 0), (xhi_ref, nx - 2, nx - 1)):
-        face = ref.at[pl.ds(0, layers)].reshape(np_, 2, parts, ny, LANES)
-        copies.append((p_ref.at[:, pl.ds(first, 2)], face))
+    copies = []
+    for ref, first, outer in ((lo_ref, 0, 0), (hi_ref, nx - 2, nx - 1)):
+        copies.append((p_ref.at[:, pl.ds(first, 2)], ref.at[pl.ds(0, layers)].reshape(np_, 2, parts, ny, LANES)))
         copies.append((d_ref.at[outer], ref.at[pl.ds(layers, some)].reshape(parts, ny, LANES)))
         copies.append((v_ref.at[:, outer], ref.at[pl.ds(layers + some, 3 * some)].reshape(3, parts, ny, LANES)))
-    copies = [pltpu.make_async_copy(src, dst, sem) for src, dst in copies]
-    for copy in copies:
-        copy.start()
-    for copy in copies:
-        copy.wait()
-    dn_ref[half : half + nx, :] = terms[0] + 0.5 * terms[2]
-    up_ref[half : half + nx, :] = terms[1] - 0.5 * terms[3]
+    move(copies, sem)
 
 
 def coefficients(d, vx, vy, vz):
@@ -71,13 +80,15 @@
     )
 
 
-def spread_kernel(nx, ny, np_, nz, p_ref, d_ref, v_ref, u_ref, c_ref):
-    parts = nz // LANES
+def spread(nx, ny, np_, parts, p_ref, u_ref):
     for x in range(nx):
         for y in range(ny):
             for h in range(parts):
                 block = p_ref[pl.ds((x * parts + h) * ny + y, np_, stride=nx * parts * ny), :]
                 u_ref[x, y, :, h * LANES : (h + 1) * LANES] = block
+
+
+def coefficient_kernel(d_ref, v_ref, c_ref):
     for i, c in enumerate(coefficients(d_ref[...], v_ref[0], v_ref[1], v_ref[2])):
         c_ref[i] = c
 
@@ -101,19 +112,19 @@
         emit(y, total)
 
 
-def sweep(nx, ny, nz, ys, get, c_ref, lo, hi, ring, emit):
+def sweep(nx, ny, nz, ys, get, c_ref, lo, hi, ring, emit, loop=None, ends=None):
     def at(x, before, after):
         outside = None if ring is None else lambda y: ring(x, y)
         coef = lambda i, y: c_ref[i, x, pl.ds(y, 1), :]
         column(ny, nz, ys, lambda y: get(x, y), before, after, coef, outside, lambda y, total: emit(x, y, total))
 
-    at(0, lo, lambda y: get(1, y))
-
-    @pl.loop(1, nx - 1)
-    def _(x):
-        at(x, lambda y: get(x - 1, y), lambda y: get(x + 1, y))
-
-    at(nx - 1, lambda y: get(nx - 2, y), hi)
+    for x in ends:
+        at(x, lo if x == 0 else lambda y: get(x - 1, y), hi if x == nx - 1 else lambda y: get(x + 1, y))
+    if loop is not None:
+
+        @pl.loop(*loop)
+        def _(x):
+            at(x, lambda y: get(x - 1, y), lambda y: get(x + 1, y))
 
 
 def split(ny, low, inner, high):
@@ -131,17 +142,41 @@
     return get, put
 
 
-def first_kernel(nx, ny, np_, nz, u_ref, c_ref, lo_ref, hi_ref, v_ref, dn_ref, up_ref, vlo_ref, vhi_ref, k_ref):
+def face(ref):
+    return lambda y: ref[y]
+
+
+def layer(ref, i, parts, ny, np_):
+    def get(y):
+        each = [ref[pl.ds((i * parts + h) * ny + y, np_, stride=2 * parts * ny), :] for h in range(parts)]
+        return jnp.concatenate(each, axis=1)
+
+    return get
+
+
+def face(ref):
+    return lambda y: ref[y]
+
+
+def first_kernel(nx, ny, np_, nz, p_ref, d_ref, v_ref, u_ref, c_ref, out_ref, dn_ref, up_ref, w_ref, g_ref):
+    spread(nx, ny, np_, nz // LANES, p_ref, u_ref)
+    coefficient_kernel(d_ref, v_ref, c_ref)
+    get, put = split(ny, dn_ref, out_ref, up_ref)
+    sweep(nx, ny, nz, range(ny), lambda x, y: u_ref[x, y], c_ref, None, None, None, put, (1, nx - 1), ())
+    g_ref[...] = jnp.zeros_like(g_ref)
+
+    def emit(x, y, total):
+        w_ref[x - 2, y - 2] = total
+        g_ref[...] += square(total)
+
+    sweep(nx, ny, nz, range(2, ny - 2), get, c_ref, None, None, None, emit, (2, nx - 2), ())
+
+
+def outer_kernel(
+    nx, ny, np_, nz, u_ref, c_ref, lo_ref, hi_ref, v_in, dn_in, up_in, v_ref, dn_ref, up_ref, vlo_ref, vhi_ref, k_ref
+):
     parts = nz // LANES
     layers = np_ * 2 * parts * ny
-
-    def layer(ref, i):
-        def get(y):
-            each = [ref[pl.ds((i * parts + h) * ny + y, np_, stride=2 * parts * ny), :] for h in range(parts)]
-            return jnp.concatenate(each, axis=1)
-
-        return get
-
     for side, ref in enumerate((lo_ref, hi_ref)):
         tile = lambda i: jnp.concatenate(
             [ref[layers + (i * parts + h) * ny : layers + (i * parts + h + 1) * ny, :] for h in range(parts)], axis=1
@@ -149,17 +184,21 @@
         for i, c in enumerate(coefficients(tile(0), tile(1), tile(2), tile(3))):
             k_ref[side, i] = c
 
-    def outer(side, row, before, after, out_ref):
+    get = lambda x, y: u_ref[x, y]
+    (far_lo, near_lo), (near_hi, far_hi) = [[layer(ref, i, parts, ny, np_) for i in (0, 1)] for ref in (lo_ref, hi_ref)]
+    for old, new in ((v_in, v_ref), (dn_in, dn_ref), (up_in, up_ref)):
+        new[1 : nx - 1] = old[1 : nx - 1]
+    _, put = split(ny, dn_ref, v_ref, up_ref)
+    sweep(nx, ny, nz, range(ny), get, c_ref, near_lo, near_hi, None, put, None, (0, nx - 1))
+
+    def beyond(side, row, before, after, out_ref):
         def emit(y, total):
             out_ref[y] = total
 
         column(ny, nz, range(ny), row, before, after, lambda i, y: k_ref[side, i, pl.ds(y, 1), :], None, emit)
 
-    get = lambda x, y: u_ref[x, y]
-    outer(0, layer(lo_ref, 1), layer(lo_ref, 0), lambda y: get(0, y), vlo_ref)
-    outer(1, layer(hi_ref, 0), lambda y: get(nx - 1, y), layer(hi_ref, 1), vhi_ref)
-    _, put = split(ny, dn_ref, v_ref, up_ref)
-    sweep(nx, ny, nz, range(ny), get, c_ref, layer(lo_ref, 1), layer(hi_ref, 0), None, put)
+    beyond(0, near_lo, far_lo, lambda y: get(0, y), vlo_ref)
+    beyond(1, near_hi, lambda y: get(nx - 1, y), far_hi, vhi_ref)
 
 
 def close_kernel(nx, ny, np_, c_ref, below_ref, above_ref, dn_ref, up_ref, low_ref, high_ref, xlo_ref, xhi_ref):
@@ -193,32 +232,16 @@
     return block(0, 0) + ((block(0, 1) + block(1, 0)) + (block(1, 1) + (block(0, 2) + block(2, 0))))
 
 
-def face(ref):
-    return lambda y: ref[y]
-
-
-def middle_kernel(nx, ny, nz, v_ref, c_ref, lo_ref, hi_ref, dn_ref, up_ref, w_ref, g_ref, dn_out, up_out):
-    g_ref[...] = jnp.zeros_like(g_ref)
-
-    def emit(x, y, total):
-        w_ref[x, y - 2] = total
-        g_ref[...] += square(total)
-
-    sweep(nx, ny, nz, range(2, ny - 2), lambda x, y: v_ref[x, y - 1], c_ref, face(lo_ref), face(hi_ref), None, emit)
-    dn_out[...] = dn_ref[...]
-    up_out[...] = up_ref[...]
-
-
 def border_kernel(
-    nx, ny, np_, nz, u_ref, v_ref, vlow_ref, vhigh_ref, c_ref, below_ref, above_ref, lo_ref, hi_ref,
-    w_ref, wlow_ref, whigh_ref, g_ref,
+    nx, ny, np_, nz, up_ref, dn_ref, v_ref, vlow_ref, vhigh_ref, c_ref, below_ref, above_ref, lo_ref, hi_ref,
+    w_ref, wends_ref, wlow_ref, whigh_ref, g_ref,
 ):
     half = nx * np_
     get, _ = split(ny, vlow_ref, v_ref, vhigh_ref)
 
     def ring(x, y):
-        side = below_ref if y == 0 else above_ref
-        return side[pl.ds(half + x, 1), :] * u_ref[x, y]
+        side, own = (below_ref, dn_ref) if y == 0 else (above_ref, up_ref)
+        return side[pl.ds(half + x, 1), :] * own[pl.ds(x * np_, np_), :]
 
     g_ref[...] = jnp.zeros_like(g_ref)
 
@@ -231,7 +254,15 @@
             w_ref[x, 0 if y == 1 else 1] = total
             g_ref[...] += square(total)
 
-    sweep(nx, ny, nz, (0, 1, ny - 2, ny - 1), get, c_ref, face(lo_ref), face(hi_ref), ring, emit)
+    ends = (0, 1, nx - 2, nx - 1)
+
+    def emit_ends(x, y, total):
+        wends_ref[ends.index(x), y - 2] = total
+        g_ref[...] += square(total)
+
+    lo, hi = face(lo_ref), face(hi_ref)
+    sweep(nx, ny, nz, (0, 1, ny - 2, ny - 1), get, c_ref, lo, hi, ring, emit, (1, nx - 1), (0, nx - 1))
+    sweep(nx, ny, nz, range(2, ny - 2), get, c_ref, lo, hi, None, emit_ends, None, ends)
 
 
 def last_kernel(
@@ -280,14 +311,15 @@
 
 
 def basis_kernel(
-    nx, ny, np_, scale, g_ref, w_ref, wside_ref, wlow_ref, whigh_ref, out_ref, factor_ref, inv_ref, stage, sems
+    nx, ny, np_, scale, g_ref, w_ref, wside_ref, wends_ref, wlow_ref, whigh_ref, out_ref, factor_ref, inv_ref, stage, sems
 ):
     def get(x, y):
         if y in (0, ny - 1):
             return wlow_ref[x] if y == 0 else whigh_ref[x]
         if y in (1, ny - 2):
             return wside_ref[x, 0 if y == 1 else 1]
-        return w_ref[x, y - 2]
+        ends = (0, 1, nx - 2, nx - 1)
+        return wends_ref[ends.index(x), y - 2] if x in ends else w_ref[x - 2, y - 2]
 
     n = np_
     total = jnp.sum(g_ref[...], axis=0) * scale
@@ -334,40 +366,56 @@
     tiled = lambda a: jnp.swapaxes(a.reshape(a.shape[:-1] + (parts, LANES)), -2, -3)
     tiles = tiled(probes)
     wide = ((2 * np_ + 4) * parts * ny, LANES)
-    up, dn, xlo, xhi = call(
+    hbm = pl.BlockSpec(memory_space=pltpu.HBM)
+    operands = [tiles, tiled(diffusion), tiled(velocity)]
+    up, dn = call(
         functools.partial(edge_kernel, nx, ny, np_, parts),
-        [tall, tall, wide, wide],
-        [tiles, tiled(diffusion), tiled(velocity)],
+        [tall, tall],
+        operands,
         scratch=[pltpu.VMEM((4, nx, nz), F32), pltpu.SemaphoreType.DMA],
-        in_specs=[pl.BlockSpec(memory_space=pltpu.HBM)] * 3,
+        in_specs=[hbm] * 3,
         name="edge",
         vmem=61,
     )
     below = lax.ppermute(up, "gy", up_y)
     above = lax.ppermute(dn, "gy", dn_y)
-    before = lax.ppermute(xhi, "gx", up_x)
-    after = lax.ppermute(xlo, "gx", dn_x)
-    u, coef = call(
-        functools.partial(spread_kernel, nx, ny, np_, nz),
-        [grid, (7, nx, ny, nz)],
-        [tiles.reshape(-1, LANES), diffusion, velocity],
-        name="spread",
-    )
-    v, dn2, up2, vlo, vhi = call(
-        functools.partial(first_kernel, nx, ny, np_, nz),
-        [(nx, ny - 2, np_, nz), plane, plane, face_shape, face_shape],
-        [u, coef, before, after],
-        scratch=[pltpu.VMEM((2, 7, ny, nz), F32)],
-        name="first",
-    )
-    w, gram, dn2, up2 = call(
-        functools.partial(middle_kernel, nx, ny, nz),
-        [(nx, ny - 4, np_, nz), square_sum, plane, plane],
-        [v, coef, vlo, vhi, dn2, up2],
-        name="middle",
-    )
+    some = (nx, ny - 2, np_, nz)
+    shapes = [some, plane, plane, face_shape, face_shape, (nx - 4, ny - 4, np_, nz), square_sum]
+
+    def inside(tiles, diffusion, velocity):
+        xlo, xhi = call(
+            functools.partial(side_kernel, nx, ny, np_, parts),
+            [wide, wide],
+            [tiles, tiled(diffusion), tiled(velocity)],
+            scratch=[pltpu.SemaphoreType.DMA],
+            in_specs=[hbm] * 3,
+            name="side",
+        )
+        before = lax.ppermute(xhi, "gx", up_x)
+        after = lax.ppermute(xlo, "gx", dn_x)
+        u, coef, v, dn2, up2, w, gram = call(
+            functools.partial(first_kernel, nx, ny, np_, nz),
+            [grid, (7, nx, ny, nz), some, plane, plane, *shapes[5:]],
+            [tiles.reshape(-1, LANES), diffusion, velocity],
+            name="first",
+        )
+        made = call(
+            functools.partial(outer_kernel, nx, ny, np_, nz),
+            shapes[:5],
+            [u, coef, before, after, v, dn2, up2],
+            scratch=[pltpu.VMEM((2, 7, ny, nz), F32)],
+            name="outer",
+        )
+        return (*made, w, gram)
+
+    def outside(*_):
+        return tuple(jnp.zeros(shape, F32) for shape in shapes)
+
+    always = lax.axis_index("gx") >= 0
+    v, dn2, up2, vlo, vhi, w, gram = lax.cond(always, inside, outside, tiles, diffusion, velocity)
     below2 = lax.ppermute(up2, "gy", up_y)
     above2 = lax.ppermute(dn2, "gy", dn_y)
+    (coef,) = call(coefficient_kernel, [(7, nx, ny, nz)], [diffusion, velocity], name="coef")
     vlow, vhigh, xlo3, xhi3 = call(
         functools.partial(close_kernel, nx, ny, np_),
         [plane, plane, corner, corner],
@@ -376,10 +424,10 @@
     )
     before3 = lax.ppermute(xhi3, "gx", up_x)
     after3 = lax.ppermute(xlo3, "gx", dn_x)
-    wside, wlow, whigh, gram2 = call(
+    wside, wends, wlow, whigh, gram2 = call(
         functools.partial(border_kernel, nx, ny, np_, nz),
-        [(nx, 2, np_, nz), plane, plane, square_sum],
-        [u, v, vlow, vhigh, coef, below, above, vlo, vhi],
+        [(nx, 2, np_, nz), (4, ny - 4, np_, nz), plane, plane, square_sum],
+        [up, dn, v, vlow, vhigh, coef, below, above, vlo, vhi],
         name="border",
     )
     wlow, whigh, grams = call(
@@ -392,7 +440,7 @@
     basis, factor = call(
         functools.partial(basis_kernel, nx, ny, np_, 1.0 / cells),
         [(np_, nx, parts * ny, LANES), (np_, np_)],
-        [grams, w, wside, wlow, whigh],
+        [grams, w, wside, wends, wlow, whigh],
         scratch=[
             pltpu.VMEM((np_, np_), F32),
             pltpu.VMEM((nx, np_ * parts * ny, LANES), F32),

time: 78.9 us -> 73.8 us (0.935)
  local copies, waits for them, and re-layouts: 2.19 us -> 0.03 us
  starting transfers between devices: 21.4 us -> 19.8 us
    ppermute x1, waiting for transfers between devices: 0.81 us -> 11.9 us  [on_device(): below2 = lax.ppermute(up2, 'gy', up_y)]
    ppermute x1, waiting for transfers between devices: 10.8 us -> 0.01 us  [on_device(): after3 = lax.ppermute(xlo3, 'gx', dn_x)]
    unnamed x6 -> x8, local copies, waits for them, and re-layouts: 2.19 us -> 0.02 us
    ppermute x1, starting transfers between devices: 4.94 us -> 3.54 us  [on_device(): before3 = lax.ppermute(xhi3, 'gx', up_x)]
    ppermute x1, waiting for transfers between devices: 1.87 us -> 0.93 us  [on_device(): below = lax.ppermute(up, 'gy', up_y)]
    pallas_call x8 -> x9, Pallas kernels: 24.4 us -> 24.5 us  [call(): pl.pallas_call(body, out_shape=[jax.ShapeDtypeStruct(s, F32) for s in out...]
  transfers between devices with their start and end apart: 8 -> 8, of which waited for: 3 -> 2; matrix products, arithmetic and copies ran while one was open for 0% -> 0% of each run, Pallas kernels for 21% -> 23%
where the time goes in v3:
time: 73.8 us; the launch traced here: 73.5 us
  Pallas kernels  24.5 us (33%)
  starting transfers between devices  19.8 us (27%)
  blocking collectives  15.5 us (21%)
  waiting for transfers between devices  12.8 us (17%)
  between operations  0.79 us (1%)
    pallas_call x9, Pallas kernels, call(): pl.pallas_call(body, out_shape=[jax.ShapeDtypeStruct(s, F32) for s in out...  24.5 us
    all_to_all x1, blocking collectives, on_device(): grams = lax.all_to_all(grams, ('gx', 'gy'), 0, 0, tiled=True)  15.5 us
    ppermute x1, waiting for transfers between devices, on_device(): below2 = lax.ppermute(up2, 'gy', up_y)  11.9 us
    ppermute x1, starting transfers between devices, on_device(): below = lax.ppermute(up, 'gy', up_y)  4.9 us
    ppermute x1, starting transfers between devices, on_device(): below2 = lax.ppermute(up2, 'gy', up_y)  4.54 us
    ppermute x1, starting transfers between devices, on_device(): before3 = lax.ppermute(xhi3, 'gx', up_x)  3.54 us
    ppermute x1, starting transfers between devices, inside(): before = lax.ppermute(xhi, 'gx', up_x)  1.63 us
  transfers between devices with their start and end apart: 8, of which 2 were waited for; matrix products, arithmetic and copies ran while one was open for 0% of the time, Pallas kernels for 23%

profile of v3, /device:TPU:0, one launch (start us, length us, event | category | flops | bytes accessed | tf_op | source)
XLA Modules:
  0.0 73.5 jit_solution(2931398693938375150)
XLA Ops:
  0.6 0.0 copy-start.4
  0.6 0.0 copy-start.3
  0.6 2.4 %edge.1 = (f32[528,256]{1,0:T(8,128)}, f32[528,256]{1,0:T(8,128)}) custom-call(f32[32,16,2,8,128]{4,3,2,1,0:T(8,128)} %bitcast.21, f32[16,2,8,128]{3,2,1,0:T(8,128)} %bitcast.26, f32[3,16,2,8,128]{4,3,2,1,0:T(8,128)} %bitcast.24), custom_call_target="tpu_custom_call" | custom-call | tf_op jit(solution)/shard_map/edge/pallas_call | solution.py:20
  3.0 4.9 %collective-permute-start.4 = (f32[528,256]{1,0:T(8,128)}, f32[528,256]{1,0:T(8,128)S(1)}, u32[]{:S(2)}, u32[]{:S(2)}) collective-permute-start(f32[528,256]{1,0:T(8,128)} %get-tuple-element.50.up_ref), channel_id=1, source_target_pairs={{0,1},{1,2},{2,3},{3,4},{4,5},{5,6},{6,7},{8,9},{9,10},{10,11},{11... | collective-permute-start | bytes 1622024 | tf_op jit(solution)/shard_map/ppermute | solution.py:380
  7.9 1.3 %collective-permute-start.5 = (f32[528,256]{1,0:T(8,128)}, f32[528,256]{1,0:T(8,128)S(1)}, u32[]{:S(2)}, u32[]{:S(2)}) collective-permute-start(f32[528,256]{1,0:T(8,128)} %get-tuple-element.51.dn_ref), channel_id=1, source_target_pairs={{1,0},{2,1},{3,2},{4,3},{5,4},{6,5},{7,6},{9,8},{10,9},{11,10},{12... | collective-permute-start | bytes 1622024 | tf_op jit(solution)/shard_map/ppermute | solution.py:381
  9.2 0.0 copy-done.4
  9.3 0.0 copy-done.3
  9.3 15.2 %conditional.1 = (f32[16,6,32,256]{3,2,1,0:T(8,128)S(1)}, f32[16,32,256]{2,1,0:T(8,128)S(1)}, f32[16,32,256]{2,1,0:T(8,128)S(1)}, f32[8,32,256]{2,1,0:T(8,128)S(...) conditional(s32[]{:T(128)} %convert_element_type.3, () %tuple.16, ...), branch_computations={%region_0.0_spmd, %region_1.0_spmd} | conditional | bytes 21233828 | solution.py:415
  9.3 0.0 copy-start.2
  9.3 1.4 %side.1 = (f32[1088,128]{1,0:T(8,128)S(1)}, f32[1088,128]{1,0:T(8,128)S(1)}) custom-call(f32[32,16,2,8,128]{4,3,2,1,0:T(8,128)} %get-tuple-element.6.p_ref, f32[16,2,8,128]{3,2,1,0:T(8,128)S(1)} %bitcast.27, f32[3,16,2,8,128]{4,3,2,1,0:T(8,128)S(1)} %bitcast.25), custom_call_target="tpu_custom_call" | custom-call | tf_op jit(solution)/shard_map/cond/branch_1_fun/side/pallas_call | solution.py:20
  10.7 1.6 %collective-permute-start = (f32[1088,128]{1,0:T(8,128)S(1)}, f32[1088,128]{1,0:T(8,128)S(1)}, u32[]{:S(2)}, u32[]{:S(2)}) collective-permute-start(f32[1088,128]{1,0:T(8,128)S(1)} %get-tuple-element.11), channel_id=1, source_target_pairs={{0,8},{8,16},{16,24},{1,9},{9,17},{17,25},{2,10},{10,18},{18,26},{... | collective-permute-start | bytes 1671176 | tf_op jit(solution)/shard_map/cond/branch_1_fun/ppermute | solution.py:394
  12.3 1.3 %collective-permute-start.1 = (f32[1088,128]{1,0:T(8,128)S(1)}, f32[1088,128]{1,0:T(8,128)S(1)}, u32[]{:S(2)}, u32[]{:S(2)}) collective-permute-start(f32[1088,128]{1,0:T(8,128)S(1)} %get-tuple-element.12), channel_id=1, source_target_pairs={{8,0},{16,8},{24,16},{9,1},{17,9},{25,17},{10,2},{18,10},{26,18},{... | collective-permute-start | bytes 1671176 | tf_op jit(solution)/shard_map/cond/branch_1_fun/ppermute | solution.py:395
  13.6 0.0 copy-done.2
  13.6 9.3 %first.1 = (f32[16,8,32,256]{3,2,1,0:T(8,128)S(1)}, f32[7,16,8,256]{3,2,1,0:T(8,128)S(1)}, f32[16,6,32,256]{3,2,1,0:T(8,128)S(1)}, f32[16,32,256]{2,1,0:T(8,128)...) custom-call(f32[8192,128]{1,0:T(8,128)S(1)} %bitcast.23, ...), custom_call_target="tpu_custom_call" | custom-call | tf_op jit(solution)/shard_map/cond/branch_1_fun/first/pallas_call | solution.py:20
  22.9 0.0 collective-permute-done.lo_ref
  22.9 0.0 collective-permute-done.1.hi_ref
  22.9 1.5 %outer.1 = (f32[16,6,32,256]{3,2,1,0:T(8,128)S(1)}, f32[16,32,256]{2,1,0:T(8,128)S(1)}, f32[16,32,256]{2,1,0:T(8,128)S(1)}, f32[8,32,256]{2,1,0:T(8,128)S(1)}, f32[8,32,256]{2,1,0:T(8,128)S(1)}) custom-call(f32[16,8,32,256]{3,2,1,0:T(8,128)S(1)} %get-tuple-element.9.u_ref, f32[7,16,8,256]{3,2,1,0:T(8,128)S(1)} %get-tuple-element.10.c_ref, ...), custom_call_target="tpu_custom_call" | custom-call | tf_op jit(solution)/shard_map/cond/branch_1_fun/outer/pallas_call | solution.py:20
  24.4 0.0 copy-start
  24.4 0.0 copy-start.1
  24.5 4.5 %collective-permute-start.2 = (f32[16,32,256]{2,1,0:T(8,128)S(1)}, f32[16,32,256]{2,1,0:T(8,128)S(1)}, u32[]{:S(2)}, u32[]{:S(2)}) collective-permute-start(f32[16,32,256]{2,1,0:T(8,128)S(1)} %get-tuple-element.48.up_ref), channel_id=1, source_target_pairs={{0,1},{1,2},{2,3},{3,4},{4,5},{5,6},{6,7},{8,9},{9,10},{10,11},{11... | collective-permute-start | bytes 1572872 | tf_op jit(solution)/shard_map/ppermute | solution.py:416
  29.0 1.3 %collective-permute-start.3 = (f32[16,32,256]{2,1,0:T(8,128)S(1)}, f32[16,32,256]{2,1,0:T(8,128)S(1)}, u32[]{:S(2)}, u32[]{:S(2)}) collective-permute-start(f32[16,32,256]{2,1,0:T(8,128)S(1)} %get-tuple-element.49.dn_ref), channel_id=1, source_target_pairs={{1,0},{2,1},{3,2},{4,3},{5,4},{6,5},{7,6},{9,8},{10,9},{11,10},{12... | collective-permute-start | bytes 1572872 | tf_op jit(solution)/shard_map/ppermute | solution.py:417
  30.3 0.1 coef.1.c_ref
  30.4 0.9 %collective-permute-done.4.below_ref = f32[528,256]{1,0:T(8,128)S(1)} collective-permute-done((f32[528,256]{1,0:T(8,128)}, f32[528,256]{1,0:T(8,128)S(1)}, u32[]{:S(2)}, u32[]{:S(2)}) %collective-permute-start.4) | collective-permute-done | bytes 540704 | tf_op jit(solution)/shard_map/ppermute | solution.py:380
  31.3 0.0 collective-permute-done.5.above_ref
  31.3 0.1 close.1
  31.5 3.5 %collective-permute-start.6 = (f32[2,32,256]{2,1,0:T(8,128)S(1)}, f32[2,32,256]{2,1,0:T(8,128)S(1)}, u32[]{:S(2)}, u32[]{:S(2)}) collective-permute-start(f32[2,32,256]{2,1,0:T(8,128)S(1)} %get-tuple-element.52), channel_id=1, source_target_pairs={{0,8},{8,16},{16,24},{1,9},{9,17},{17,25},{2,10},{10,18},{18,26},{... | collective-permute-start | bytes 196616 | tf_op jit(solution)/shard_map/ppermute | solution.py:425
  35.0 1.3 %collective-permute-start.7 = (f32[2,32,256]{2,1,0:T(8,128)S(1)}, f32[2,32,256]{2,1,0:T(8,128)S(1)}, u32[]{:S(2)}, u32[]{:S(2)}) collective-permute-start(f32[2,32,256]{2,1,0:T(8,128)S(1)} %get-tuple-element.53), channel_id=1, source_target_pairs={{8,0},{16,8},{24,16},{9,1},{17,9},{25,17},{10,2},{18,10},{26,18},{... | collective-permute-start | bytes 196616 | tf_op jit(solution)/shard_map/ppermute | solution.py:426
  36.3 0.0 copy-done
  36.3 0.0 copy-done.1
  36.3 4.8 %border.1 = (f32[16,2,32,256]{3,2,1,0:T(8,128)S(1)}, f32[4,4,32,256]{3,2,1,0:T(8,128)S(1)}, f32[16,32,256]{2,1,0:T(8,128)S(1)}, f32[16,32,256]{2,1,0:T(8,128)S(1)}, f32[96,96]{1,0:T(8,128)S(1)}) custom-call(f32[528,256]{1,0:T(8,128)S(1)} %copy-done, f32[528,256]{1,0:T(8,128)S(1)} %copy-done.1, f32[16,6,32,256]{3,2,1,0:T(8,128)S(1)} %get-tuple-element.55.v_ref, ...), custom_call_target="tpu_custom_call" | custom-call | tf_op jit(solution)/shard_map/border/pallas_call | solution.py:20
  41.1 11.9 %collective-permute-done.2.below_ref = f32[16,32,256]{2,1,0:T(8,128)S(1)} collective-permute-done((f32[16,32,256]{2,1,0:T(8,128)S(1)}, f32[16,32,256]{2,1,0:T(8,128)S(1)}, u32[]{:S(2)}, u32[]{:S(2)}) %collective-permute-start.2) | collective-permute-done | bytes 524320 | tf_op jit(solution)/shard_map/ppermute | solution.py:416
  53.0 0.0 collective-permute-done.3.above_ref
  53.0 0.0 collective-permute-done.6.lo_ref
  53.0 0.0 collective-permute-done.7.hi_ref
  53.0 0.9 %last.1 = (f32[16,32,256]{2,1,0:T(8,128)S(1)}, f32[16,32,256]{2,1,0:T(8,128)S(1)}, f32[32,8,128]{2,1,0:T(8,128)S(1)}) custom-call(f32[7,16,8,256]{3,2,1,0:T(8,128)S(1)} %coef.1.c_ref, f32[16,32,256]{2,1,0:T(8,128)S(1)} %collective-permute-done.2.below_ref, f32[16,32,256]{2,1,0:T(8,128)S(1)} %collective-permute-done.3.above_ref, ...), custom_call_target="tpu_custom_call" | custom-call | tf_op jit(solution)/shard_map/last/pallas_call | solution.py:20
  53.8 15.5 %all_to_all.5.g_ref = f32[32,8,128]{2,1,0:T(8,128)S(1)} all-to-all(f32[32,8,128]{2,1,0:T(8,128)S(1)} %get-tuple-element.63), channel_id=1, replica_groups=mesh['gx'=4,'gy'=8] {'gx','gy'}, dimensions={0} | all-to-all | bytes 262144 | tf_op jit(solution)/shard_map/all_to_all | solution.py:439
  69.3 4.1 %basis.1 = (f32[32,16,16,128]{3,2,1,0:T(8,128)}, f32[32,32]{1,0:T(8,128)}) custom-call(f32[32,8,128]{2,1,0:T(8,128)S(1)} %all_to_all.5.g_ref, f32[12,4,32,256]{3,2,1,0:T(8,128)S(1)} %get-tuple-element.64.w_ref, f32[16,2,32,256]{3,2,1,0:T(8,128)S(1)} %get-tuple-element.65.wside_ref, f32[4,4,32,256]{3,2,1,0:T(8,128)S(1)} %get-tuple-element.66.wends_ref, ...), custom_call_target="tpu_custom_call" | custom-call | tf_op jit(solution)/shard_map/basis/pallas_call | solution.py:20
Async XLA Ops:
  0.6 8.6 %copy-start.4 = (f32[16,8,256]{2,1,0:T(8,128)S(1)}, f32[16,8,256]{2,1,0:T(8,128)}, u32[]{:S(2)}) copy-start(f32[16,8,256]{2,1,0:T(8,128)} %d_ref.1) | copy-start | bytes 393220
  0.6 8.6 %copy-start.3 = (f32[3,16,8,256]{3,2,1,0:T(8,128)S(1)}, f32[3,16,8,256]{3,2,1,0:T(8,128)}, u32[]{:S(2)}) copy-start(f32[3,16,8,256]{3,2,1,0:T(8,128)} %v_ref.1) | copy-start | bytes 1179652
  3.0 28.3 %collective-permute-start.4 = (f32[528,256]{1,0:T(8,128)}, f32[528,256]{1,0:T(8,128)S(1)}, u32[]{:S(2)}, u32[]{:S(2)}) collective-permute-start(f32[528,256]{1,0:T(8,128)} %get-tuple-element.50.up_ref), channel_id=1, source_target_pairs={{0,1},{1,2},{2,3},{3,4},{4,5},{5,6},{6,7},{8,9},{9,10},{10,11},{11... | collective-permute-start | bytes 1622024 | tf_op jit(solution)/shard_map/ppermute | solution.py:380
  7.9 23.4 %collective-permute-start.5 = (f32[528,256]{1,0:T(8,128)}, f32[528,256]{1,0:T(8,128)S(1)}, u32[]{:S(2)}, u32[]{:S(2)}) collective-permute-start(f32[528,256]{1,0:T(8,128)} %get-tuple-element.51.dn_ref), channel_id=1, source_target_pairs={{1,0},{2,1},{3,2},{4,3},{5,4},{6,5},{7,6},{9,8},{10,9},{11,10},{12... | collective-permute-start | bytes 1622024 | tf_op jit(solution)/shard_map/ppermute | solution.py:381
  9.3 4.3 %copy-start.2 = (f32[32,16,2,8,128]{4,3,2,1,0:T(8,128)S(1)}, f32[32,16,2,8,128]{4,3,2,1,0:T(8,128)}, u32[]{:S(2)}) copy-start(f32[32,16,2,8,128]{4,3,2,1,0:T(8,128)} %get-tuple-element.6.p_ref) | copy-start | bytes 12582916 | tf_op jit(solution)/shard_map/cond
  10.7 12.3 %collective-permute-start = (f32[1088,128]{1,0:T(8,128)S(1)}, f32[1088,128]{1,0:T(8,128)S(1)}, u32[]{:S(2)}, u32[]{:S(2)}) collective-permute-start(f32[1088,128]{1,0:T(8,128)S(1)} %get-tuple-element.11), channel_id=1, source_target_pairs={{0,8},{8,16},{16,24},{1,9},{9,17},{17,25},{2,10},{10,18},{18,26},{... | collective-permute-start | bytes 1671176 | tf_op jit(solution)/shard_map/cond/branch_1_fun/ppermute | solution.py:394
  12.3 10.6 %collective-permute-start.1 = (f32[1088,128]{1,0:T(8,128)S(1)}, f32[1088,128]{1,0:T(8,128)S(1)}, u32[]{:S(2)}, u32[]{:S(2)}) collective-permute-start(f32[1088,128]{1,0:T(8,128)S(1)} %get-tuple-element.12), channel_id=1, source_target_pairs={{8,0},{16,8},{24,16},{9,1},{17,9},{25,17},{10,2},{18,10},{26,18},{... | collective-permute-start | bytes 1671176 | tf_op jit(solution)/shard_map/cond/branch_1_fun/ppermute | solution.py:395
  24.4 11.9 %copy-start = (f32[528,256]{1,0:T(8,128)S(1)}, f32[528,256]{1,0:T(8,128)}, u32[]{:S(2)}) copy-start(f32[528,256]{1,0:T(8,128)} %get-tuple-element.50.up_ref) | copy-start | bytes 1622020
  24.4 11.9 %copy-start.1 = (f32[528,256]{1,0:T(8,128)S(1)}, f32[528,256]{1,0:T(8,128)}, u32[]{:S(2)}) copy-start(f32[528,256]{1,0:T(8,128)} %get-tuple-element.51.dn_ref) | copy-start | bytes 1622020
  24.5 28.5 %collective-permute-start.2 = (f32[16,32,256]{2,1,0:T(8,128)S(1)}, f32[16,32,256]{2,1,0:T(8,128)S(1)}, u32[]{:S(2)}, u32[]{:S(2)}) collective-permute-start(f32[16,32,256]{2,1,0:T(8,128)S(1)} %get-tuple-element.48.up_ref), channel_id=1, source_target_pairs={{0,1},{1,2},{2,3},{3,4},{4,5},{5,6},{6,7},{8,9},{9,10},{10,11},{11... | collective-permute-start | bytes 1572872 | tf_op jit(solution)/shard_map/ppermute | solution.py:416
  29.0 24.0 %collective-permute-start.3 = (f32[16,32,256]{2,1,0:T(8,128)S(1)}, f32[16,32,256]{2,1,0:T(8,128)S(1)}, u32[]{:S(2)}, u32[]{:S(2)}) collective-permute-start(f32[16,32,256]{2,1,0:T(8,128)S(1)} %get-tuple-element.49.dn_ref), channel_id=1, source_target_pairs={{1,0},{2,1},{3,2},{4,3},{5,4},{6,5},{7,6},{9,8},{10,9},{11,10},{12... | collective-permute-start | bytes 1572872 | tf_op jit(solution)/shard_map/ppermute | solution.py:417
  31.5 21.5 %collective-permute-start.6 = (f32[2,32,256]{2,1,0:T(8,128)S(1)}, f32[2,32,256]{2,1,0:T(8,128)S(1)}, u32[]{:S(2)}, u32[]{:S(2)}) collective-permute-start(f32[2,32,256]{2,1,0:T(8,128)S(1)} %get-tuple-element.52), channel_id=1, source_target_pairs={{0,8},{8,16},{16,24},{1,9},{9,17},{17,25},{2,10},{10,18},{18,26},{... | collective-permute-start | bytes 196616 | tf_op jit(solution)/shard_map/ppermute | solution.py:425
  35.0 18.0 %collective-permute-start.7 = (f32[2,32,256]{2,1,0:T(8,128)S(1)}, f32[2,32,256]{2,1,0:T(8,128)S(1)}, u32[]{:S(2)}, u32[]{:S(2)}) collective-permute-start(f32[2,32,256]{2,1,0:T(8,128)S(1)} %get-tuple-element.53), channel_id=1, source_target_pairs={{8,0},{16,8},{24,16},{9,1},{17,9},{25,17},{10,2},{18,10},{26,18},{... | collective-permute-start | bytes 196616 | tf_op jit(solution)/shard_map/ppermute | solution.py:426

commit v4 on v3

--- a/solution.py
+++ b/solution.py
@@ -12,7 +12,7 @@
 VMEM = pl.BlockSpec(memory_space=pltpu.VMEM)
 ANY = pl.BlockSpec(memory_space=pl.ANY)
 LANES = 128
-BLOCK = 8
+BLOCK = 16
 W0, XP, XM, YP, YM, ZP, ZM = range(7)
 
 
@@ -29,6 +29,26 @@
     )(*ins)
 
 
+def even(axis):
+    return lax.rem(lax.axis_index(axis), 2) == 0
+
+
+def swaps(count):
+    pairs = [[(i, i + 1) for i in range(first, count - 1, 2)] for first in (0, 1)]
+    return [[(i, j) for pair in each for i, j in (pair, pair[::-1])] for each in pairs]
+
+
+def exchange(one, two, axis):
+    first, second = swaps(lax.axis_size(axis))
+    return lax.ppermute(one, axis, first), lax.ppermute(two, axis, second)
+
+
+def sides(is_even, one, two):
+    low = lambda *at: jnp.where(is_even, two[at], one[at])
+    high = lambda *at: jnp.where(is_even, one[at], two[at])
+    return low, high
+
+
 def move(pairs, sem):
     copies = [pltpu.make_async_copy(src, dst, sem) for src, dst in pairs]
     for copy in copies:
@@ -37,34 +57,58 @@
         copy.wait()
 
 
-def edge_kernel(nx, ny, np_, parts, p_ref, d_ref, v_ref, up_ref, dn_ref, terms, sem):
+def edge_kernel(nx, ny, np_, parts, p_ref, d_ref, v_ref, one_ref, two_ref, terms, sem):
     last = ny - 1
     half = nx * np_
-    copies = []
-    for x in range(nx):
-        rows = pl.ds(x * np_, np_)
+
+    def fill(up_ref, dn_ref):
+        copies = []
+        for x in range(nx):
+            rows = pl.ds(x * np_, np_)
+            for h in range(parts):
+                lanes = pl.ds(h * LANES, LANES)
+                copies.append((p_ref.at[:, x, h, last, :], up_ref.at[rows, lanes]))
+                copies.append((p_ref.at[:, x, h, 0, :], dn_ref.at[rows, lanes]))
         for h in range(parts):
-            lanes = pl.ds(h * LANES, LANES)
-            copies.append((p_ref.at[:, x, h, last, :], up_ref.at[rows, lanes]))
-            copies.append((p_ref.at[:, x, h, 0, :], dn_ref.at[rows, lanes]))
-    for h in range(parts):
-        for i, y in enumerate((0, last)):
-            copies.append((d_ref.at[:, h, y, :], terms.at[i, :, pl.ds(h * LANES, LANES)]))
-            copies.append((v_ref.at[1, :, h, y, :], terms.at[2 + i, :, pl.ds(h * LANES, LANES)]))
-    move(copies, sem)
-    dn_ref[half : half + nx, :] = terms[0] + 0.5 * terms[2]
-    up_ref[half : half + nx, :] = terms[1] - 0.5 * terms[3]
-
-
-def side_kernel(nx, ny, np_, parts, p_ref, d_ref, v_ref, lo_ref, hi_ref, sem):
+            for i, y in enumerate((0, last)):
+                copies.append((d_ref.at[:, h, y, :], terms.at[i, :, pl.ds(h * LANES, LANES)]))
+                copies.append((v_ref.at[1, :, h, y, :], terms.at[2 + i, :, pl.ds(h * LANES, LANES)]))
+        move(copies, sem)
+        dn_ref[half : half + nx, :] = terms[0] + 0.5 * terms[2]
+        up_ref[half : half + nx, :] = terms[1] - 0.5 * terms[3]
+
+    is_even = even("gy")
+
+    @pl.when(is_even)
+    def _():
+        fill(one_ref, two_ref)
+
+    @pl.when(jnp.logical_not(is_even))
+    def _():
+        fill(two_ref, one_ref)
+
+
+def side_kernel(nx, ny, np_, parts, p_ref, d_ref, v_ref, one_ref, two_ref, sem):
     layers = np_ * 2 * parts * ny
     some = parts * ny
-    copies = []
-    for ref, first, outer in ((lo_ref, 0, 0), (hi_ref, nx - 2, nx - 1)):
-        copies.append((p_ref.at[:, pl.ds(first, 2)], ref.at[pl.ds(0, layers)].reshape(np_, 2, parts, ny, LANES)))
-        copies.append((d_ref.at[outer], ref.at[pl.ds(layers, some)].reshape(parts, ny, LANES)))
-        copies.append((v_ref.at[:, outer], ref.at[pl.ds(layers + some, 3 * some)].reshape(3, parts, ny, LANES)))
-    move(copies, sem)
+
+    def fill(hi_ref, lo_ref):
+        copies = []
+        for ref, first, outer in ((lo_ref, 0, 0), (hi_ref, nx - 2, nx - 1)):
+            copies.append((p_ref.at[:, pl.ds(first, 2)], ref.at[pl.ds(0, layers)].reshape(np_, 2, parts, ny, LANES)))
+            copies.append((d_ref.at[outer], ref.at[pl.ds(layers, some)].reshape(parts, ny, LANES)))
+            copies.append((v_ref.at[:, outer], ref.at[pl.ds(layers + some, 3 * some)].reshape(3, parts, ny, LANES)))
+        move(copies, sem)
+
+    is_even = even("gx")
+
+    @pl.when(is_even)
+    def _():
+        fill(one_ref, two_ref)
+
+    @pl.when(jnp.logical_not(is_even))
+    def _():
+        fill(two_ref, one_ref)
 
 
 def coefficients(d, vx, vy, vz):
@@ -142,13 +186,9 @@
     return get, put
 
 
-def face(ref):
-    return lambda y: ref[y]
-
-
-def layer(ref, i, parts, ny, np_):
+def layer(rows, i, parts, ny, np_):
     def get(y):
-        each = [ref[pl.ds((i * parts + h) * ny + y, np_, stride=2 * parts * ny), :] for h in range(parts)]
+        each = [rows(pl.ds((i * parts + h) * ny + y, np_, stride=2 * parts * ny), slice(None)) for h in range(parts)]
         return jnp.concatenate(each, axis=1)
 
     return get
@@ -173,23 +213,38 @@
 
 
 def outer_kernel(
-    nx, ny, np_, nz, u_ref, c_ref, lo_ref, hi_ref, v_in, dn_in, up_in, v_ref, dn_ref, up_ref, vlo_ref, vhi_ref, k_ref
+    nx, ny, np_, nz, u_ref, c_ref, xone_ref, xtwo_ref, v_in, dn_in, up_in,
+    v_ref, one_ref, two_ref, vlo_ref, vhi_ref, k_ref, dn_ends, up_ends,
 ):
     parts = nz // LANES
     layers = np_ * 2 * parts * ny
-    for side, ref in enumerate((lo_ref, hi_ref)):
+    messages = sides(even("gx"), xone_ref, xtwo_ref)
+    for side, rows in enumerate(messages):
         tile = lambda i: jnp.concatenate(
-            [ref[layers + (i * parts + h) * ny : layers + (i * parts + h + 1) * ny, :] for h in range(parts)], axis=1
+            [rows(pl.ds(layers + (i * parts + h) * ny, ny), slice(None)) for h in range(parts)], axis=1
         )
         for i, c in enumerate(coefficients(tile(0), tile(1), tile(2), tile(3))):
             k_ref[side, i] = c
 
     get = lambda x, y: u_ref[x, y]
-    (far_lo, near_lo), (near_hi, far_hi) = [[layer(ref, i, parts, ny, np_) for i in (0, 1)] for ref in (lo_ref, hi_ref)]
-    for old, new in ((v_in, v_ref), (dn_in, dn_ref), (up_in, up_ref)):
-        new[1 : nx - 1] = old[1 : nx - 1]
-    _, put = split(ny, dn_ref, v_ref, up_ref)
+    (far_lo, near_lo), (near_hi, far_hi) = [[layer(rows, i, parts, ny, np_) for i in (0, 1)] for rows in messages]
+    v_ref[1 : nx - 1] = v_in[1 : nx - 1]
+    ends = {0: 0, nx - 1: 1}
+
+    def put(x, y, total):
+        if y == 0:
+            dn_ends[ends[x]] = total
+        elif y == ny - 1:
+            up_ends[ends[x]] = total
+        else:
+            v_ref[x, y - 1] = total
+
     sweep(nx, ny, nz, range(ny), get, c_ref, near_lo, near_hi, None, put, None, (0, nx - 1))
+    is_even = even("gy")
+    for x in range(nx):
+        dn, up = (dn_ends[ends[x]], up_ends[ends[x]]) if x in ends else (dn_in[x], up_in[x])
+        one_ref[x] = jnp.where(is_even, up, dn)
+        two_ref[x] = jnp.where(is_even, dn, up)
 
     def beyond(side, row, before, after, out_ref):
         def emit(y, total):
@@ -201,18 +256,25 @@
     beyond(1, near_hi, lambda y: get(nx - 1, y), far_hi, vhi_ref)
 
 
-def close_kernel(nx, ny, np_, c_ref, below_ref, above_ref, dn_ref, up_ref, low_ref, high_ref, xlo_ref, xhi_ref):
+def close_kernel(
+    nx, ny, np_, c_ref, rone_ref, rtwo_ref, one_ref, two_ref, low_ref, high_ref, xone_ref, xtwo_ref
+):
     last = ny - 1
+    below, above = sides(even("gy"), rone_ref, rtwo_ref)
+    dn, up = sides(even("gy"), one_ref, two_ref)
+    ends = {}
     for x in range(nx):
         rows = slice(x * np_, (x + 1) * np_)
-        low = c_ref[YM, x, 0:1, :] * below_ref[rows, :]
-        high = c_ref[YP, x, last : last + 1, :] * above_ref[rows, :]
-        low_ref[x] = dn_ref[x] + low
-        high_ref[x] = up_ref[x] + high
-        if x == 0:
-            xlo_ref[0], xlo_ref[1] = low, high
-        if x == nx - 1:
-            xhi_ref[0], xhi_ref[1] = low, high
+        low = c_ref[YM, x, 0:1, :] * below(rows, slice(None))
+        high = c_ref[YP, x, last : last + 1, :] * above(rows, slice(None))
+        low_ref[x] = dn(x) + low
+        high_ref[x] = up(x) + high
+        ends[x] = low, high
+    is_even = even("gx")
+    for i in range(2):
+        lo, hi = ends[0][i], ends[nx - 1][i]
+        xone_ref[i] = jnp.where(is_even, hi, lo)
+        xtwo_ref[i] = jnp.where(is_even, lo, hi)
 
 
 def pieces(a):
@@ -233,15 +295,18 @@
 
 
 def border_kernel(
-    nx, ny, np_, nz, up_ref, dn_ref, v_ref, vlow_ref, vhigh_ref, c_ref, below_ref, above_ref, lo_ref, hi_ref,
+    nx, ny, np_, nz, one_ref, two_ref, v_ref, vlow_ref, vhigh_ref, c_ref, rone_ref, rtwo_ref, lo_ref, hi_ref,
     w_ref, wends_ref, wlow_ref, whigh_ref, g_ref,
 ):
     half = nx * np_
     get, _ = split(ny, vlow_ref, v_ref, vhigh_ref)
 
+    received = sides(even("gy"), rone_ref, rtwo_ref)
+    sent = sides(even("gy"), one_ref, two_ref)
+
     def ring(x, y):
-        side, own = (below_ref, dn_ref) if y == 0 else (above_ref, up_ref)
-        return side[pl.ds(half + x, 1), :] * own[pl.ds(x * np_, np_), :]
+        side, all_z = 0 if y == 0 else 1, slice(None)
+        return received[side](pl.ds(half + x, 1), all_z) * sent[side](pl.ds(x * np_, np_), all_z)
 
     g_ref[...] = jnp.zeros_like(g_ref)
 
@@ -266,20 +331,22 @@
 
 
 def last_kernel(
-    nx, ny, np_, copies, c_ref, below_ref, above_ref, lo_ref, hi_ref, ga_ref, gb_ref, wlow_in, whigh_in,
+    nx, ny, np_, copies, c_ref, rone_ref, rtwo_ref, xone_ref, xtwo_ref, ga_ref, gb_ref, wlow_in, whigh_in,
     wlow_ref, whigh_ref, g_ref,
 ):
     last = ny - 1
     gram = ga_ref[...] + gb_ref[...]
+    below, above = sides(even("gy"), rone_ref, rtwo_ref)
+    before, after = sides(even("gx"), xone_ref, xtwo_ref)
     for x in range(nx):
-        low = wlow_in[x] + c_ref[YM, x, 0:1, :] * below_ref[x]
-        high = whigh_in[x] + c_ref[YP, x, last : last + 1, :] * above_ref[x]
+        low = wlow_in[x] + c_ref[YM, x, 0:1, :] * below(x)
+        high = whigh_in[x] + c_ref[YP, x, last : last + 1, :] * above(x)
         if x == 0:
-            low = low + c_ref[XM, x, 0:1, :] * lo_ref[0]
-            high = high + c_ref[XM, x, last : last + 1, :] * lo_ref[1]
+            low = low + c_ref[XM, x, 0:1, :] * before(0)
+            high = high + c_ref[XM, x, last : last + 1, :] * before(1)
         if x == nx - 1:
-            low = low + c_ref[XP, x, 0:1, :] * hi_ref[0]
-            high = high + c_ref[XP, x, last : last + 1, :] * hi_ref[1]
+            low = low + c_ref[XP, x, 0:1, :] * after(0)
+            high = high + c_ref[XP, x, last : last + 1, :] * after(1)
         wlow_ref[x] = low
         whigh_ref[x] = high
         gram = gram + (square(low) + square(high))
@@ -357,18 +424,13 @@
     plane = (nx, np_, nz)
     face_shape = (ny, np_, nz)
     tall = (nx * np_ + nx, nz)
-    up_x = [(i, i + 1) for i in range(mx - 1)]
-    dn_x = [(i + 1, i) for i in range(mx - 1)]
-    up_y = [(i, i + 1) for i in range(my - 1)]
-    dn_y = [(i + 1, i) for i in range(my - 1)]
-
     parts = nz // LANES
     tiled = lambda a: jnp.swapaxes(a.reshape(a.shape[:-1] + (parts, LANES)), -2, -3)
     tiles = tiled(probes)
     wide = ((2 * np_ + 4) * parts * ny, LANES)
     hbm = pl.BlockSpec(memory_space=pltpu.HBM)
     operands = [tiles, tiled(diffusion), tiled(velocity)]
-    up, dn = call(
+    one, two = call(
         functools.partial(edge_kernel, nx, ny, np_, parts),
         [tall, tall],
         operands,
@@ -377,13 +439,12 @@
         name="edge",
         vmem=61,
     )
-    below = lax.ppermute(up, "gy", up_y)
-    above = lax.ppermute(dn, "gy", dn_y)
+    rone, rtwo = exchange(one, two, "gy")
     some = (nx, ny - 2, np_, nz)
     shapes = [some, plane, plane, face_shape, face_shape, (nx - 4, ny - 4, np_, nz), square_sum]
 
     def inside(tiles, diffusion, velocity):
-        xlo, xhi = call(
+        xone, xtwo = call(
             functools.partial(side_kernel, nx, ny, np_, parts),
             [wide, wide],
             [tiles, tiled(diffusion), tiled(velocity)],
@@ -391,8 +452,7 @@
             in_specs=[hbm] * 3,
             name="side",
         )
-        before = lax.ppermute(xhi, "gx", up_x)
-        after = lax.ppermute(xlo, "gx", dn_x)
+        xone, xtwo = exchange(xone, xtwo, "gx")
         u, coef, v, dn2, up2, w, gram = call(
             functools.partial(first_kernel, nx, ny, np_, nz),
             [grid, (7, nx, ny, nz), some, plane, plane, *shapes[5:]],
@@ -402,8 +462,8 @@
         made = call(
             functools.partial(outer_kernel, nx, ny, np_, nz),
             shapes[:5],
-            [u, coef, before, after, v, dn2, up2],
-            scratch=[pltpu.VMEM((2, 7, ny, nz), F32)],
+            [u, coef, xone, xtwo, v, dn2, up2],
+            scratch=[pltpu.VMEM((2, 7, ny, nz), F32), pltpu.VMEM((2, np_, nz), F32), pltpu.VMEM((2, np_, nz), F32)],
             name="outer",
         )
         return (*made, w, gram)
@@ -412,28 +472,26 @@
         return tuple(jnp.zeros(shape, F32) for shape in shapes)
 
     always = lax.axis_index("gx") >= 0
-    v, dn2, up2, vlo, vhi, w, gram = lax.cond(always, inside, outside, tiles, diffusion, velocity)
-    below2 = lax.ppermute(up2, "gy", up_y)
-    above2 = lax.ppermute(dn2, "gy", dn_y)
+    v, one2, two2, vlo, vhi, w, gram = lax.cond(always, inside, outside, tiles, diffusion, velocity)
+    rone2, rtwo2 = exchange(one2, two2, "gy")
     (coef,) = call(coefficient_kernel, [(7, nx, ny, nz)], [diffusion, velocity], name="coef")
-    vlow, vhigh, xlo3, xhi3 = call(
+    vlow, vhigh, xone3, xtwo3 = call(
         functools.partial(close_kernel, nx, ny, np_),
         [plane, plane, corner, corner],
-        [coef, below, above, dn2, up2],
+        [coef, rone, rtwo, one2, two2],
         name="close",
     )
-    before3 = lax.ppermute(xhi3, "gx", up_x)
-    after3 = lax.ppermute(xlo3, "gx", dn_x)
+    xone3, xtwo3 = exchange(xone3, xtwo3, "gx")
     wside, wends, wlow, whigh, gram2 = call(
         functools.partial(border_kernel, nx, ny, np_, nz),
         [(nx, 2, np_, nz), (4, ny - 4, np_, nz), plane, plane, square_sum],
-        [up, dn, v, vlow, vhigh, coef, below, above, vlo, vhi],
+        [one, two, v, vlow, vhigh, coef, rone, rtwo, vlo, vhi],
         name="border",
     )
     wlow, whigh, grams = call(
         functools.partial(last_kernel, nx, ny, np_, mx * my),
         [plane, plane, (mx * my, 8, np_ * np_ // 8)],
-        [coef, below2, above2, before3, after3, gram, gram2, wlow, whigh],
+        [coef, rone2, rtwo2, xone3, xtwo3, gram, gram2, wlow, whigh],
         name="last",
     )
     grams = lax.all_to_all(grams, ("gx", "gy"), 0, 0, tiled=True)

time: 73.8 us -> 70.4 us (0.954)
  starting transfers between devices: 19.8 us -> 10.3 us
  waiting for transfers between devices: 12.8 us -> 19.9 us
  blocking collectives: 15.5 us -> 13.4 us
  Pallas kernels: 24.5 us -> 25.5 us
    ppermute x8, starting transfers between devices: 19.8 us -> 10.3 us  [exchange(): return (lax.ppermute(one, axis, first), lax.ppermute(two, axis, second))]
    ppermute x8, waiting for transfers between devices: 12.8 us -> 19.9 us  [exchange(): return (lax.ppermute(one, axis, first), lax.ppermute(two, axis, second))]
    all_to_all x1, blocking collectives: 15.5 us -> 13.4 us  [on_device(): grams = lax.all_to_all(grams, ('gx', 'gy'), 0, 0, tiled=True)]
    pallas_call x9, Pallas kernels: 24.5 us -> 25.5 us  [call(): pl.pallas_call(body, out_shape=[jax.ShapeDtypeStruct(s, F32) for s in out...]
  transfers between devices with their start and end apart: 8 -> 8, of which waited for: 2 -> 2; matrix products, arithmetic and copies ran while one was open for 0% -> 0% of each run, Pallas kernels for 23% -> 26%
where the time goes in v4:
time: 70.4 us; the launch traced here: 70.2 us
  Pallas kernels  25.5 us (36%)
  waiting for transfers between devices  19.9 us (28%)
  blocking collectives  13.4 us (19%)
  starting transfers between devices  10.3 us (15%)
  between operations  0.78 us (1%)
    pallas_call x9, Pallas kernels, call(): pl.pallas_call(body, out_shape=[jax.ShapeDtypeStruct(s, F32) for s in out...  25.5 us
    ppermute x8, waiting for transfers between devices, exchange(): return (lax.ppermute(one, axis, first), lax.ppermute(two, axis, second))  19.9 us
    all_to_all x1, blocking collectives, on_device(): grams = lax.all_to_all(grams, ('gx', 'gy'), 0, 0, tiled=True)  13.4 us
    ppermute x8, starting transfers between devices, exchange(): return (lax.ppermute(one, axis, first), lax.ppermute(two, axis, second))  10.3 us
  transfers between devices with their start and end apart: 8, of which 2 were waited for; matrix products, arithmetic and copies ran while one was open for 0% of the time, Pallas kernels for 26%

profile of v4, /device:TPU:0, one launch (start us, length us, event | category | flops | bytes accessed | tf_op | source)
XLA Modules:
  0.0 70.2 jit_solution(16241869033205851864)
XLA Ops:
  0.6 0.0 copy-start.4
  0.6 0.0 copy-start.3
  0.6 2.4 %edge.1 = (f32[528,256]{1,0:T(8,128)}, f32[528,256]{1,0:T(8,128)}) custom-call(f32[32,16,2,8,128]{4,3,2,1,0:T(8,128)} %bitcast.21, f32[16,2,8,128]{3,2,1,0:T(8,128)} %bitcast.26, f32[3,16,2,8,128]{4,3,2,1,0:T(8,128)} %bitcast.24), custom_call_target="tpu_custom_call" | custom-call | tf_op jit(solution)/shard_map/edge/pallas_call | solution.py:20
  3.0 3.0 %collective-permute-start.4 = (f32[528,256]{1,0:T(8,128)}, f32[528,256]{1,0:T(8,128)S(1)}, u32[]{:S(2)}, u32[]{:S(2)}) collective-permute-start(f32[528,256]{1,0:T(8,128)} %get-tuple-element.50.one_ref), channel_id=1, source_target_pairs={{0,1},{1,0},{2,3},{3,2},{4,5},{5,4},{6,7},{7,6},{8,9},{9,8},{10,11... | collective-permute-start | bytes 1622024 | tf_op jit(solution)/shard_map/ppermute | solution.py:43
  6.1 0.7 collective-permute-start.5
  6.8 0.0 copy-done.4
  6.8 0.0 copy-done.3
  6.8 14.4 %conditional.1 = (f32[16,6,32,256]{3,2,1,0:T(8,128)S(1)}, f32[16,32,256]{2,1,0:T(8,128)S(1)}, f32[16,32,256]{2,1,0:T(8,128)S(1)}, f32[8,32,256]{2,1,0:T(8,128)S(...) conditional(s32[]{:T(128)} %convert_element_type.3, () %tuple.16, ...), branch_computations={%region_0.0_spmd, %region_1.0_spmd} | conditional | bytes 21233828 | solution.py:475
  6.8 0.0 copy-start.2
  6.8 1.4 %side.1 = (f32[1088,128]{1,0:T(8,128)S(1)}, f32[1088,128]{1,0:T(8,128)S(1)}) custom-call(f32[32,16,2,8,128]{4,3,2,1,0:T(8,128)} %get-tuple-element.6.p_ref, f32[16,2,8,128]{3,2,1,0:T(8,128)S(1)} %bitcast.27, f32[3,16,2,8,128]{4,3,2,1,0:T(8,128)S(1)} %bitcast.25), custom_call_target="tpu_custom_call" | custom-call | tf_op jit(solution)/shard_map/cond/branch_1_fun/side/pallas_call | solution.py:20
  8.2 0.1 collective-permute-start
  8.3 0.8 %collective-permute-start.1 = (f32[1088,128]{1,0:T(8,128)S(1)}, f32[1088,128]{1,0:T(8,128)S(1)}, u32[]{:S(2)}, u32[]{:S(2)}) collective-permute-start(f32[1088,128]{1,0:T(8,128)S(1)} %get-tuple-element.12), channel_id=1, source_target_pairs={{8,16},{16,8},{9,17},{17,9},{10,18},{18,10},{11,19},{19,11},{12,20... | collective-permute-start | bytes 1671176 | tf_op jit(solution)/shard_map/cond/branch_1_fun/ppermute | solution.py:43
  9.1 0.2 copy-done.2
  9.3 9.3 %first.1 = (f32[16,8,32,256]{3,2,1,0:T(8,128)S(1)}, f32[7,16,8,256]{3,2,1,0:T(8,128)S(1)}, f32[16,6,32,256]{3,2,1,0:T(8,128)S(1)}, f32[16,32,256]{2,1,0:T(8,128)...) custom-call(f32[8192,128]{1,0:T(8,128)S(1)} %bitcast.23, ...), custom_call_target="tpu_custom_call" | custom-call | tf_op jit(solution)/shard_map/cond/branch_1_fun/first/pallas_call | solution.py:20
  18.6 0.0 collective-permute-done.xone_ref
  18.6 0.0 collective-permute-done.1.xtwo_ref
  18.6 2.5 %outer.1 = (f32[16,6,32,256]{3,2,1,0:T(8,128)S(1)}, f32[16,32,256]{2,1,0:T(8,128)S(1)}, f32[16,32,256]{2,1,0:T(8,128)S(1)}, f32[8,32,256]{2,1,0:T(8,128)S(1)}, f32[8,32,256]{2,1,0:T(8,128)S(1)}) custom-call(f32[16,8,32,256]{3,2,1,0:T(8,128)S(1)} %get-tuple-element.9.u_ref, f32[7,16,8,256]{3,2,1,0:T(8,128)S(1)} %get-tuple-element.10.c_ref, ...), custom_call_target="tpu_custom_call" | custom-call | tf_op jit(solution)/shard_map/cond/branch_1_fun/outer/pallas_call | solution.py:20
  21.2 0.0 copy-start
  21.2 0.0 copy-start.1
  21.2 4.3 %collective-permute-start.2 = (f32[16,32,256]{2,1,0:T(8,128)S(1)}, f32[16,32,256]{2,1,0:T(8,128)S(1)}, u32[]{:S(2)}, u32[]{:S(2)}) collective-permute-start(f32[16,32,256]{2,1,0:T(8,128)S(1)} %get-tuple-element.48.one_ref), channel_id=1, source_target_pairs={{0,1},{1,0},{2,3},{3,2},{4,5},{5,4},{6,7},{7,6},{8,9},{9,8},{10,11... | collective-permute-start | bytes 1572872 | tf_op jit(solution)/shard_map/ppermute | solution.py:43
  25.5 0.7 collective-permute-start.3
  26.2 0.1 coef.1.c_ref
  26.3 15.6 %collective-permute-done.4.rone_ref = f32[528,256]{1,0:T(8,128)S(1)} collective-permute-done((f32[528,256]{1,0:T(8,128)}, f32[528,256]{1,0:T(8,128)S(1)}, u32[]{:S(2)}, u32[]{:S(2)}) %collective-permute-start.4) | collective-permute-done | bytes 540704 | tf_op jit(solution)/shard_map/ppermute | solution.py:43
  41.9 0.0 collective-permute-done.5.rtwo_ref
  41.9 0.2 close.1
  42.1 0.1 collective-permute-start.6
  42.1 0.7 collective-permute-start.7
  42.8 0.0 copy-done
  42.8 0.0 copy-done.1
  42.8 4.7 %border.1 = (f32[16,2,32,256]{3,2,1,0:T(8,128)S(1)}, f32[4,4,32,256]{3,2,1,0:T(8,128)S(1)}, f32[16,32,256]{2,1,0:T(8,128)S(1)}, f32[16,32,256]{2,1,0:T(8,128)S(1)}, f32[96,96]{1,0:T(8,128)S(1)}) custom-call(f32[528,256]{1,0:T(8,128)S(1)} %copy-done, f32[528,256]{1,0:T(8,128)S(1)} %copy-done.1, f32[16,6,32,256]{3,2,1,0:T(8,128)S(1)} %get-tuple-element.55.v_ref, ...), custom_call_target="tpu_custom_call" | custom-call | tf_op jit(solution)/shard_map/border/pallas_call | solution.py:20
  47.6 4.3 %collective-permute-done.2.rone_ref = f32[16,32,256]{2,1,0:T(8,128)S(1)} collective-permute-done((f32[16,32,256]{2,1,0:T(8,128)S(1)}, f32[16,32,256]{2,1,0:T(8,128)S(1)}, u32[]{:S(2)}, u32[]{:S(2)}) %collective-permute-start.2) | collective-permute-done | bytes 524320 | tf_op jit(solution)/shard_map/ppermute | solution.py:43
  51.9 0.0 collective-permute-done.3.rtwo_ref
  51.9 0.0 collective-permute-done.6.xone_ref
  51.9 0.0 collective-permute-done.7.xtwo_ref
  51.9 0.9 %last.1 = (f32[16,32,256]{2,1,0:T(8,128)S(1)}, f32[16,32,256]{2,1,0:T(8,128)S(1)}, f32[32,8,128]{2,1,0:T(8,128)S(1)}) custom-call(f32[7,16,8,256]{3,2,1,0:T(8,128)S(1)} %coef.1.c_ref, f32[16,32,256]{2,1,0:T(8,128)S(1)} %collective-permute-done.2.rone_ref, f32[16,32,256]{2,1,0:T(8,128)S(1)} %collective-permute-done.3.rtwo_ref, ...), custom_call_target="tpu_custom_call" | custom-call | tf_op jit(solution)/shard_map/last/pallas_call | solution.py:20
  52.8 13.4 %all_to_all.5.g_ref = f32[32,8,128]{2,1,0:T(8,128)S(1)} all-to-all(f32[32,8,128]{2,1,0:T(8,128)S(1)} %get-tuple-element.63), channel_id=1, replica_groups=mesh['gx'=4,'gy'=8] {'gx','gy'}, dimensions={0} | all-to-all | bytes 262144 | tf_op jit(solution)/shard_map/all_to_all | solution.py:497
  66.2 4.0 %basis.1 = (f32[32,16,16,128]{3,2,1,0:T(8,128)}, f32[32,32]{1,0:T(8,128)}) custom-call(f32[32,8,128]{2,1,0:T(8,128)S(1)} %all_to_all.5.g_ref, f32[12,4,32,256]{3,2,1,0:T(8,128)S(1)} %get-tuple-element.64.w_ref, f32[16,2,32,256]{3,2,1,0:T(8,128)S(1)} %get-tuple-element.65.wside_ref, f32[4,4,32,256]{3,2,1,0:T(8,128)S(1)} %get-tuple-element.66.wends_ref, ...), custom_call_target="tpu_custom_call" | custom-call | tf_op jit(solution)/shard_map/basis/pallas_call | solution.py:20
Async XLA Ops:
  0.6 6.1 %copy-start.4 = (f32[16,8,256]{2,1,0:T(8,128)S(1)}, f32[16,8,256]{2,1,0:T(8,128)}, u32[]{:S(2)}) copy-start(f32[16,8,256]{2,1,0:T(8,128)} %d_ref.1) | copy-start | bytes 393220
  0.6 6.1 %copy-start.3 = (f32[3,16,8,256]{3,2,1,0:T(8,128)S(1)}, f32[3,16,8,256]{3,2,1,0:T(8,128)}, u32[]{:S(2)}) copy-start(f32[3,16,8,256]{3,2,1,0:T(8,128)} %v_ref.1) | copy-start | bytes 1179652
  3.0 38.9 %collective-permute-start.4 = (f32[528,256]{1,0:T(8,128)}, f32[528,256]{1,0:T(8,128)S(1)}, u32[]{:S(2)}, u32[]{:S(2)}) collective-permute-start(f32[528,256]{1,0:T(8,128)} %get-tuple-element.50.one_ref), channel_id=1, source_target_pairs={{0,1},{1,0},{2,3},{3,2},{4,5},{5,4},{6,7},{7,6},{8,9},{9,8},{10,11... | collective-permute-start | bytes 1622024 | tf_op jit(solution)/shard_map/ppermute | solution.py:43
  6.1 35.8 %collective-permute-start.5 = (f32[528,256]{1,0:T(8,128)}, f32[528,256]{1,0:T(8,128)S(1)}, u32[]{:S(2)}, u32[]{:S(2)}) collective-permute-start(f32[528,256]{1,0:T(8,128)} %get-tuple-element.51.two_ref), channel_id=1, source_target_pairs={{1,2},{2,1},{3,4},{4,3},{5,6},{6,5},{9,10},{10,9},{11,12},{12,11},... | collective-permute-start | bytes 1622024 | tf_op jit(solution)/shard_map/ppermute | solution.py:43
  6.8 2.5 %copy-start.2 = (f32[32,16,2,8,128]{4,3,2,1,0:T(8,128)S(1)}, f32[32,16,2,8,128]{4,3,2,1,0:T(8,128)}, u32[]{:S(2)}) copy-start(f32[32,16,2,8,128]{4,3,2,1,0:T(8,128)} %get-tuple-element.6.p_ref) | copy-start | bytes 12582916 | tf_op jit(solution)/shard_map/cond
  8.2 10.4 %collective-permute-start = (f32[1088,128]{1,0:T(8,128)S(1)}, f32[1088,128]{1,0:T(8,128)S(1)}, u32[]{:S(2)}, u32[]{:S(2)}) collective-permute-start(f32[1088,128]{1,0:T(8,128)S(1)} %get-tuple-element.11), channel_id=1, source_target_pairs={{0,8},{8,0},{16,24},{24,16},{1,9},{9,1},{17,25},{25,17},{2,10},{10... | collective-permute-start | bytes 1671176 | tf_op jit(solution)/shard_map/cond/branch_1_fun/ppermute | solution.py:43
  8.3 10.4 %collective-permute-start.1 = (f32[1088,128]{1,0:T(8,128)S(1)}, f32[1088,128]{1,0:T(8,128)S(1)}, u32[]{:S(2)}, u32[]{:S(2)}) collective-permute-start(f32[1088,128]{1,0:T(8,128)S(1)} %get-tuple-element.12), channel_id=1, source_target_pairs={{8,16},{16,8},{9,17},{17,9},{10,18},{18,10},{11,19},{19,11},{12,20... | collective-permute-start | bytes 1671176 | tf_op jit(solution)/shard_map/cond/branch_1_fun/ppermute | solution.py:43
  21.2 21.7 %copy-start = (f32[528,256]{1,0:T(8,128)S(1)}, f32[528,256]{1,0:T(8,128)}, u32[]{:S(2)}) copy-start(f32[528,256]{1,0:T(8,128)} %get-tuple-element.50.one_ref) | copy-start | bytes 1622020
  21.2 21.7 %copy-start.1 = (f32[528,256]{1,0:T(8,128)S(1)}, f32[528,256]{1,0:T(8,128)}, u32[]{:S(2)}) copy-start(f32[528,256]{1,0:T(8,128)} %get-tuple-element.51.two_ref) | copy-start | bytes 1622020
  21.2 30.7 %collective-permute-start.2 = (f32[16,32,256]{2,1,0:T(8,128)S(1)}, f32[16,32,256]{2,1,0:T(8,128)S(1)}, u32[]{:S(2)}, u32[]{:S(2)}) collective-permute-start(f32[16,32,256]{2,1,0:T(8,128)S(1)} %get-tuple-element.48.one_ref), channel_id=1, source_target_pairs={{0,1},{1,0},{2,3},{3,2},{4,5},{5,4},{6,7},{7,6},{8,9},{9,8},{10,11... | collective-permute-start | bytes 1572872 | tf_op jit(solution)/shard_map/ppermute | solution.py:43
  25.5 26.4 %collective-permute-start.3 = (f32[16,32,256]{2,1,0:T(8,128)S(1)}, f32[16,32,256]{2,1,0:T(8,128)S(1)}, u32[]{:S(2)}, u32[]{:S(2)}) collective-permute-start(f32[16,32,256]{2,1,0:T(8,128)S(1)} %get-tuple-element.49.two_ref), channel_id=1, source_target_pairs={{1,2},{2,1},{3,4},{4,3},{5,6},{6,5},{9,10},{10,9},{11,12},{12,11},... | collective-permute-start | bytes 1572872 | tf_op jit(solution)/shard_map/ppermute | solution.py:43
  42.1 9.8 %collective-permute-start.6 = (f32[2,32,256]{2,1,0:T(8,128)S(1)}, f32[2,32,256]{2,1,0:T(8,128)S(1)}, u32[]{:S(2)}, u32[]{:S(2)}) collective-permute-start(f32[2,32,256]{2,1,0:T(8,128)S(1)} %get-tuple-element.52), channel_id=1, source_target_pairs={{0,8},{8,0},{16,24},{24,16},{1,9},{9,1},{17,25},{25,17},{2,10},{10... | collective-permute-start | bytes 196616 | tf_op jit(solution)/shard_map/ppermute | solution.py:43
  42.1 9.7 %collective-permute-start.7 = (f32[2,32,256]{2,1,0:T(8,128)S(1)}, f32[2,32,256]{2,1,0:T(8,128)S(1)}, u32[]{:S(2)}, u32[]{:S(2)}) collective-permute-start(f32[2,32,256]{2,1,0:T(8,128)S(1)} %get-tuple-element.53), channel_id=1, source_target_pairs={{8,16},{16,8},{9,17},{17,9},{10,18},{18,10},{11,19},{19,11},{12,20... | collective-permute-start | bytes 196616 | tf_op jit(solution)/shard_map/ppermute | solution.py:43

commit v5 on v4

--- a/solution.py
+++ b/solution.py
@@ -437,7 +437,7 @@
         scratch=[pltpu.VMEM((4, nx, nz), F32), pltpu.SemaphoreType.DMA],
         in_specs=[hbm] * 3,
         name="edge",
-        vmem=61,
+        vmem=24,
     )
     rone, rtwo = exchange(one, two, "gy")
     some = (nx, ny - 2, np_, nz)

time: 70.4 us -> 69.2 us (0.983)
  Pallas kernels: 25.5 us -> 24.5 us
    pallas_call x9, Pallas kernels: 25.5 us -> 24.5 us  [call(): pl.pallas_call(body, out_shape=[jax.ShapeDtypeStruct(s, F32) for s in out...]
where the time goes in v5:
time: 69.2 us; the launch traced here: 69 us
  Pallas kernels  24.5 us (35%)
  waiting for transfers between devices  19.8 us (29%)
  blocking collectives  13.4 us (19%)
  starting transfers between devices  10.4 us (15%)
  between operations  0.74 us (1%)
    pallas_call x9, Pallas kernels, call(): pl.pallas_call(body, out_shape=[jax.ShapeDtypeStruct(s, F32) for s in out...  24.5 us
    ppermute x8, waiting for transfers between devices, exchange(): return (lax.ppermute(one, axis, first), lax.ppermute(two, axis, second))  19.8 us
    all_to_all x1, blocking collectives, on_device(): grams = lax.all_to_all(grams, ('gx', 'gy'), 0, 0, tiled=True)  13.4 us
    ppermute x8, starting transfers between devices, exchange(): return (lax.ppermute(one, axis, first), lax.ppermute(two, axis, second))  10.4 us
  transfers between devices with their start and end apart: 8, of which 2 were waited for; matrix products, arithmetic and copies ran while one was open for 0% of the time, Pallas kernels for 26%

profile of v5, /device:TPU:0, one launch (start us, length us, event | category | flops | bytes accessed | tf_op | source)
XLA Modules:
  0.0 69.0 jit_solution(6449217237665181957)
XLA Ops:
  0.6 0.0 copy-start.2
  0.6 0.0 copy-start.1
  0.6 1.4 %edge.1 = (f32[528,256]{1,0:T(8,128)S(1)}, f32[528,256]{1,0:T(8,128)S(1)}) custom-call(f32[32,16,2,8,128]{4,3,2,1,0:T(8,128)} %bitcast.21, f32[16,2,8,128]{3,2,1,0:T(8,128)} %bitcast.26, f32[3,16,2,8,128]{4,3,2,1,0:T(8,128)} %bitcast.24), custom_call_target="tpu_custom_call" | custom-call | tf_op jit(solution)/shard_map/edge/pallas_call | solution.py:20
  2.1 3.0 %collective-permute-start.4 = (f32[528,256]{1,0:T(8,128)S(1)}, f32[528,256]{1,0:T(8,128)S(1)}, u32[]{:S(2)}, u32[]{:S(2)}) collective-permute-start(f32[528,256]{1,0:T(8,128)S(1)} %get-tuple-element.50.one_ref), channel_id=1, source_target_pairs={{0,1},{1,0},{2,3},{3,2},{4,5},{5,4},{6,7},{7,6},{8,9},{9,8},{10,11... | collective-permute-start | bytes 1622024 | tf_op jit(solution)/shard_map/ppermute | solution.py:43
  5.1 0.7 collective-permute-start.5
  5.8 0.0 copy-done.2
  5.8 0.0 copy-done.1
  5.8 14.4 %conditional.1 = (f32[16,6,32,256]{3,2,1,0:T(8,128)S(1)}, f32[16,32,256]{2,1,0:T(8,128)S(1)}, f32[16,32,256]{2,1,0:T(8,128)S(1)}, f32[8,32,256]{2,1,0:T(8,128)S(...) conditional(s32[]{:T(128)} %convert_element_type.3, () %tuple.16, ...), branch_computations={%region_0.0_spmd, %region_1.0_spmd} | conditional | bytes 21233828 | solution.py:475
  5.8 0.0 copy-start
  5.8 1.4 %side.1 = (f32[1088,128]{1,0:T(8,128)S(1)}, f32[1088,128]{1,0:T(8,128)S(1)}) custom-call(f32[32,16,2,8,128]{4,3,2,1,0:T(8,128)} %get-tuple-element.6.p_ref, f32[16,2,8,128]{3,2,1,0:T(8,128)S(1)} %bitcast.27, f32[3,16,2,8,128]{4,3,2,1,0:T(8,128)S(1)} %bitcast.25), custom_call_target="tpu_custom_call" | custom-call | tf_op jit(solution)/shard_map/cond/branch_1_fun/side/pallas_call | solution.py:20
  7.2 0.1 collective-permute-start
  7.3 0.8 %collective-permute-start.1 = (f32[1088,128]{1,0:T(8,128)S(1)}, f32[1088,128]{1,0:T(8,128)S(1)}, u32[]{:S(2)}, u32[]{:S(2)}) collective-permute-start(f32[1088,128]{1,0:T(8,128)S(1)} %get-tuple-element.12), channel_id=1, source_target_pairs={{8,16},{16,8},{9,17},{17,9},{10,18},{18,10},{11,19},{19,11},{12,20... | collective-permute-start | bytes 1671176 | tf_op jit(solution)/shard_map/cond/branch_1_fun/ppermute | solution.py:43
  8.1 0.2 copy-done
  8.3 9.3 %first.1 = (f32[16,8,32,256]{3,2,1,0:T(8,128)S(1)}, f32[7,16,8,256]{3,2,1,0:T(8,128)S(1)}, f32[16,6,32,256]{3,2,1,0:T(8,128)S(1)}, f32[16,32,256]{2,1,0:T(8,128)...) custom-call(f32[8192,128]{1,0:T(8,128)S(1)} %bitcast.23, ...), custom_call_target="tpu_custom_call" | custom-call | tf_op jit(solution)/shard_map/cond/branch_1_fun/first/pallas_call | solution.py:20
  17.6 0.0 collective-permute-done.xone_ref
  17.6 0.0 collective-permute-done.1.xtwo_ref
  17.7 2.5 %outer.1 = (f32[16,6,32,256]{3,2,1,0:T(8,128)S(1)}, f32[16,32,256]{2,1,0:T(8,128)S(1)}, f32[16,32,256]{2,1,0:T(8,128)S(1)}, f32[8,32,256]{2,1,0:T(8,128)S(1)}, f32[8,32,256]{2,1,0:T(8,128)S(1)}) custom-call(f32[16,8,32,256]{3,2,1,0:T(8,128)S(1)} %get-tuple-element.9.u_ref, f32[7,16,8,256]{3,2,1,0:T(8,128)S(1)} %get-tuple-element.10.c_ref, ...), custom_call_target="tpu_custom_call" | custom-call | tf_op jit(solution)/shard_map/cond/branch_1_fun/outer/pallas_call | solution.py:20
  20.2 4.3 %collective-permute-start.2 = (f32[16,32,256]{2,1,0:T(8,128)S(1)}, f32[16,32,256]{2,1,0:T(8,128)S(1)}, u32[]{:S(2)}, u32[]{:S(2)}) collective-permute-start(f32[16,32,256]{2,1,0:T(8,128)S(1)} %get-tuple-element.48.one_ref), channel_id=1, source_target_pairs={{0,1},{1,0},{2,3},{3,2},{4,5},{5,4},{6,7},{7,6},{8,9},{9,8},{10,11... | collective-permute-start | bytes 1572872 | tf_op jit(solution)/shard_map/ppermute | solution.py:43
  24.5 0.7 collective-permute-start.3
  25.2 0.1 coef.1.c_ref
  25.3 15.0 %collective-permute-done.4.rone_ref = f32[528,256]{1,0:T(8,128)S(1)} collective-permute-done((f32[528,256]{1,0:T(8,128)S(1)}, f32[528,256]{1,0:T(8,128)S(1)}, u32[]{:S(2)}, u32[]{:S(2)}) %collective-permute-start.4) | collective-permute-done | bytes 540704 | tf_op jit(solution)/shard_map/ppermute | solution.py:43
  40.2 0.0 collective-permute-done.5.rtwo_ref
  40.2 0.2 close.1
  40.4 0.1 collective-permute-start.6
  40.5 0.7 collective-permute-start.7
  41.1 4.7 %border.1 = (f32[16,2,32,256]{3,2,1,0:T(8,128)S(1)}, f32[4,4,32,256]{3,2,1,0:T(8,128)S(1)}, f32[16,32,256]{2,1,0:T(8,128)S(1)}, f32[16,32,256]{2,1,0:T(8,128)S(1)}, f32[96,96]{1,0:T(8,128)S(1)}) custom-call(f32[528,256]{1,0:T(8,128)S(1)} %get-tuple-element.50.one_ref, f32[528,256]{1,0:T(8,128)S(1)} %get-tuple-element.51.two_ref, ...), custom_call_target="tpu_custom_call" | custom-call | tf_op jit(solution)/shard_map/border/pallas_call | solution.py:20
  45.9 4.8 %collective-permute-done.2.rone_ref = f32[16,32,256]{2,1,0:T(8,128)S(1)} collective-permute-done((f32[16,32,256]{2,1,0:T(8,128)S(1)}, f32[16,32,256]{2,1,0:T(8,128)S(1)}, u32[]{:S(2)}, u32[]{:S(2)}) %collective-permute-start.2) | collective-permute-done | bytes 524320 | tf_op jit(solution)/shard_map/ppermute | solution.py:43
  50.7 0.0 collective-permute-done.3.rtwo_ref
  50.7 0.0 collective-permute-done.6.xone_ref
  50.7 0.0 collective-permute-done.7.xtwo_ref
  50.7 0.9 %last.1 = (f32[16,32,256]{2,1,0:T(8,128)S(1)}, f32[16,32,256]{2,1,0:T(8,128)S(1)}, f32[32,8,128]{2,1,0:T(8,128)S(1)}) custom-call(f32[7,16,8,256]{3,2,1,0:T(8,128)S(1)} %coef.1.c_ref, f32[16,32,256]{2,1,0:T(8,128)S(1)} %collective-permute-done.2.rone_ref, f32[16,32,256]{2,1,0:T(8,128)S(1)} %collective-permute-done.3.rtwo_ref, ...), custom_call_target="tpu_custom_call" | custom-call | tf_op jit(solution)/shard_map/last/pallas_call | solution.py:20
  51.6 13.4 %all_to_all.5.g_ref = f32[32,8,128]{2,1,0:T(8,128)S(1)} all-to-all(f32[32,8,128]{2,1,0:T(8,128)S(1)} %get-tuple-element.63), channel_id=1, replica_groups=mesh['gx'=4,'gy'=8] {'gx','gy'}, dimensions={0} | all-to-all | bytes 262144 | tf_op jit(solution)/shard_map/all_to_all | solution.py:497
  65.0 4.0 %basis.1 = (f32[32,16,16,128]{3,2,1,0:T(8,128)}, f32[32,32]{1,0:T(8,128)}) custom-call(f32[32,8,128]{2,1,0:T(8,128)S(1)} %all_to_all.5.g_ref, f32[12,4,32,256]{3,2,1,0:T(8,128)S(1)} %get-tuple-element.64.w_ref, f32[16,2,32,256]{3,2,1,0:T(8,128)S(1)} %get-tuple-element.65.wside_ref, f32[4,4,32,256]{3,2,1,0:T(8,128)S(1)} %get-tuple-element.66.wends_ref, ...), custom_call_target="tpu_custom_call" | custom-call | tf_op jit(solution)/shard_map/basis/pallas_call | solution.py:20
Async XLA Ops:
  0.6 5.2 %copy-start.2 = (f32[16,8,256]{2,1,0:T(8,128)S(1)}, f32[16,8,256]{2,1,0:T(8,128)}, u32[]{:S(2)}) copy-start(f32[16,8,256]{2,1,0:T(8,128)} %d_ref.1) | copy-start | bytes 393220
  0.6 5.2 %copy-start.1 = (f32[3,16,8,256]{3,2,1,0:T(8,128)S(1)}, f32[3,16,8,256]{3,2,1,0:T(8,128)}, u32[]{:S(2)}) copy-start(f32[3,16,8,256]{3,2,1,0:T(8,128)} %v_ref.1) | copy-start | bytes 1179652
  2.1 38.2 %collective-permute-start.4 = (f32[528,256]{1,0:T(8,128)S(1)}, f32[528,256]{1,0:T(8,128)S(1)}, u32[]{:S(2)}, u32[]{:S(2)}) collective-permute-start(f32[528,256]{1,0:T(8,128)S(1)} %get-tuple-element.50.one_ref), channel_id=1, source_target_pairs={{0,1},{1,0},{2,3},{3,2},{4,5},{5,4},{6,7},{7,6},{8,9},{9,8},{10,11... | collective-permute-start | bytes 1622024 | tf_op jit(solution)/shard_map/ppermute | solution.py:43
  5.1 35.1 %collective-permute-start.5 = (f32[528,256]{1,0:T(8,128)S(1)}, f32[528,256]{1,0:T(8,128)S(1)}, u32[]{:S(2)}, u32[]{:S(2)}) collective-permute-start(f32[528,256]{1,0:T(8,128)S(1)} %get-tuple-element.51.two_ref), channel_id=1, source_target_pairs={{1,2},{2,1},{3,4},{4,3},{5,6},{6,5},{9,10},{10,9},{11,12},{12,11},... | collective-permute-start | bytes 1622024 | tf_op jit(solution)/shard_map/ppermute | solution.py:43
  5.8 2.5 %copy-start = (f32[32,16,2,8,128]{4,3,2,1,0:T(8,128)S(1)}, f32[32,16,2,8,128]{4,3,2,1,0:T(8,128)}, u32[]{:S(2)}) copy-start(f32[32,16,2,8,128]{4,3,2,1,0:T(8,128)} %get-tuple-element.6.p_ref) | copy-start | bytes 12582916 | tf_op jit(solution)/shard_map/cond
  7.2 10.4 %collective-permute-start = (f32[1088,128]{1,0:T(8,128)S(1)}, f32[1088,128]{1,0:T(8,128)S(1)}, u32[]{:S(2)}, u32[]{:S(2)}) collective-permute-start(f32[1088,128]{1,0:T(8,128)S(1)} %get-tuple-element.11), channel_id=1, source_target_pairs={{0,8},{8,0},{16,24},{24,16},{1,9},{9,1},{17,25},{25,17},{2,10},{10... | collective-permute-start | bytes 1671176 | tf_op jit(solution)/shard_map/cond/branch_1_fun/ppermute | solution.py:43
  7.3 10.4 %collective-permute-start.1 = (f32[1088,128]{1,0:T(8,128)S(1)}, f32[1088,128]{1,0:T(8,128)S(1)}, u32[]{:S(2)}, u32[]{:S(2)}) collective-permute-start(f32[1088,128]{1,0:T(8,128)S(1)} %get-tuple-element.12), channel_id=1, source_target_pairs={{8,16},{16,8},{9,17},{17,9},{10,18},{18,10},{11,19},{19,11},{12,20... | collective-permute-start | bytes 1671176 | tf_op jit(solution)/shard_map/cond/branch_1_fun/ppermute | solution.py:43
  20.2 30.5 %collective-permute-start.2 = (f32[16,32,256]{2,1,0:T(8,128)S(1)}, f32[16,32,256]{2,1,0:T(8,128)S(1)}, u32[]{:S(2)}, u32[]{:S(2)}) collective-permute-start(f32[16,32,256]{2,1,0:T(8,128)S(1)} %get-tuple-element.48.one_ref), channel_id=1, source_target_pairs={{0,1},{1,0},{2,3},{3,2},{4,5},{5,4},{6,7},{7,6},{8,9},{9,8},{10,11... | collective-permute-start | bytes 1572872 | tf_op jit(solution)/shard_map/ppermute | solution.py:43
  24.5 26.2 %collective-permute-start.3 = (f32[16,32,256]{2,1,0:T(8,128)S(1)}, f32[16,32,256]{2,1,0:T(8,128)S(1)}, u32[]{:S(2)}, u32[]{:S(2)}) collective-permute-start(f32[16,32,256]{2,1,0:T(8,128)S(1)} %get-tuple-element.49.two_ref), channel_id=1, source_target_pairs={{1,2},{2,1},{3,4},{4,3},{5,6},{6,5},{9,10},{10,9},{11,12},{12,11},... | collective-permute-start | bytes 1572872 | tf_op jit(solution)/shard_map/ppermute | solution.py:43
  40.4 10.3 %collective-permute-start.6 = (f32[2,32,256]{2,1,0:T(8,128)S(1)}, f32[2,32,256]{2,1,0:T(8,128)S(1)}, u32[]{:S(2)}, u32[]{:S(2)}) collective-permute-start(f32[2,32,256]{2,1,0:T(8,128)S(1)} %get-tuple-element.52), channel_id=1, source_target_pairs={{0,8},{8,0},{16,24},{24,16},{1,9},{9,1},{17,25},{25,17},{2,10},{10... | collective-permute-start | bytes 196616 | tf_op jit(solution)/shard_map/ppermute | solution.py:43
  40.5 10.2 %collective-permute-start.7 = (f32[2,32,256]{2,1,0:T(8,128)S(1)}, f32[2,32,256]{2,1,0:T(8,128)S(1)}, u32[]{:S(2)}, u32[]{:S(2)}) collective-permute-start(f32[2,32,256]{2,1,0:T(8,128)S(1)} %get-tuple-element.53), channel_id=1, source_target_pairs={{8,16},{16,8},{9,17},{17,9},{10,18},{18,10},{11,19},{19,11},{12,20... | collective-permute-start | bytes 196616 | tf_op jit(solution)/shard_map/ppermute | solution.py:43

commit v6 on v5

--- a/solution.py
+++ b/solution.py
@@ -57,35 +57,29 @@
         copy.wait()
 
 
-def edge_kernel(nx, ny, np_, parts, p_ref, d_ref, v_ref, one_ref, two_ref, terms, sem):
-    last = ny - 1
+def edge_kernel(nx, ny, np_, parts, upward, p_ref, d_ref, v_ref, out_ref, terms, sem):
     half = nx * np_
 
-    def fill(up_ref, dn_ref):
+    def fill(y, sign):
         copies = []
-        for x in range(nx):
-            rows = pl.ds(x * np_, np_)
-            for h in range(parts):
-                lanes = pl.ds(h * LANES, LANES)
-                copies.append((p_ref.at[:, x, h, last, :], up_ref.at[rows, lanes]))
-                copies.append((p_ref.at[:, x, h, 0, :], dn_ref.at[rows, lanes]))
         for h in range(parts):
-            for i, y in enumerate((0, last)):
-                copies.append((d_ref.at[:, h, y, :], terms.at[i, :, pl.ds(h * LANES, LANES)]))
-                copies.append((v_ref.at[1, :, h, y, :], terms.at[2 + i, :, pl.ds(h * LANES, LANES)]))
+            lanes = pl.ds(h * LANES, LANES)
+            for x in range(nx):
+                copies.append((p_ref.at[:, x, h, y, :], out_ref.at[pl.ds(x * np_, np_), lanes]))
+            copies.append((d_ref.at[:, h, y, :], terms.at[0, :, lanes]))
+            copies.append((v_ref.at[1, :, h, y, :], terms.at[1, :, lanes]))
         move(copies, sem)
-        dn_ref[half : half + nx, :] = terms[0] + 0.5 * terms[2]
-        up_ref[half : half + nx, :] = terms[1] - 0.5 * terms[3]
-
-    is_even = even("gy")
-
-    @pl.when(is_even)
+        out_ref[half : half + nx, :] = terms[0] + sign * 0.5 * terms[1]
+
+    is_up = even("gy") == upward
+
+    @pl.when(is_up)
     def _():
-        fill(one_ref, two_ref)
-
-    @pl.when(jnp.logical_not(is_even))
+        fill(ny - 1, -1.0)
+
+    @pl.when(jnp.logical_not(is_up))
     def _():
-        fill(two_ref, one_ref)
+        fill(0, 1.0)
 
 
 def side_kernel(nx, ny, np_, parts, p_ref, d_ref, v_ref, one_ref, two_ref, sem):
@@ -430,15 +424,17 @@
     wide = ((2 * np_ + 4) * parts * ny, LANES)
     hbm = pl.BlockSpec(memory_space=pltpu.HBM)
     operands = [tiles, tiled(diffusion), tiled(velocity)]
-    one, two = call(
-        functools.partial(edge_kernel, nx, ny, np_, parts),
-        [tall, tall],
-        operands,
-        scratch=[pltpu.VMEM((4, nx, nz), F32), pltpu.SemaphoreType.DMA],
-        in_specs=[hbm] * 3,
-        name="edge",
-        vmem=24,
-    )
+    (one,), (two,) = [
+        call(
+            functools.partial(edge_kernel, nx, ny, np_, parts, upward),
+            [tall],
+            operands,
+            scratch=[pltpu.VMEM((2, nx, nz), F32), pltpu.SemaphoreType.DMA],
+            in_specs=[hbm] * 3,
+            name=name,
+        )
+        for upward, name in ((True, "edge_one"), (False, "edge_two"))
+    ]
     rone, rtwo = exchange(one, two, "gy")
     some = (nx, ny - 2, np_, nz)
     shapes = [some, plane, plane, face_shape, face_shape, (nx - 4, ny - 4, np_, nz), square_sum]

time: 69.2 us -> 69 us (level)
    pallas_call x9 -> x10, Pallas kernels: 24.5 us -> 24.9 us  [call(): pl.pallas_call(body, out_shape=[jax.ShapeDtypeStruct(s, F32) for s in out...]
  transfers between devices with their start and end apart: 8 -> 8, of which waited for: 2 -> 2; matrix products, arithmetic and copies ran while one was open for 0% -> 0% of each run, Pallas kernels for 26% -> 27%
where the time goes in v6:
time: 69 us; the launch traced here: 68.8 us
  Pallas kernels  24.9 us (36%)
  waiting for transfers between devices  19.2 us (28%)
  blocking collectives  13.4 us (19%)
  starting transfers between devices  10.4 us (15%)
  between operations  0.75 us (1%)
    pallas_call x10, Pallas kernels, call(): pl.pallas_call(body, out_shape=[jax.ShapeDtypeStruct(s, F32) for s in out...  24.9 us
    ppermute x8, waiting for transfers between devices, exchange(): return (lax.ppermute(one, axis, first), lax.ppermute(two, axis, second))  19.2 us
    all_to_all x1, blocking collectives, on_device(): grams = lax.all_to_all(grams, ('gx', 'gy'), 0, 0, tiled=True)  13.4 us
    ppermute x8, starting transfers between devices, exchange(): return (lax.ppermute(one, axis, first), lax.ppermute(two, axis, second))  10.4 us
  transfers between devices with their start and end apart: 8, of which 2 were waited for; matrix products, arithmetic and copies ran while one was open for 0% of the time, Pallas kernels for 27%

profile of v6, /device:TPU:0, one launch (start us, length us, event | category | flops | bytes accessed | tf_op | source)
XLA Modules:
  0.0 68.8 jit_solution(14614681374507703783)
XLA Ops:
  0.6 0.0 copy-start
  0.6 0.0 copy-start.3
  0.7 0.0 copy-start.2
  0.7 1.2 %edge_one.1.one_ref = f32[528,256]{1,0:T(8,128)S(1)} custom-call(f32[32,16,2,8,128]{4,3,2,1,0:T(8,128)} %bitcast.21, f32[16,2,8,128]{3,2,1,0:T(8,128)} %bitcast.28, f32[3,16,2,8,128]{4,3,2,1,0:T(8,128)} %bitcast.25), custom_call_target="tpu_custom_call" | custom-call | tf_op jit(solution)/shard_map/edge_one/pallas_call | solution.py:20
  1.9 3.0 %collective-permute-start.4 = (f32[528,256]{1,0:T(8,128)S(1)}, f32[528,256]{1,0:T(8,128)S(1)}, u32[]{:S(2)}, u32[]{:S(2)}) collective-permute-start(f32[528,256]{1,0:T(8,128)S(1)} %edge_one.1.one_ref), channel_id=1, source_target_pairs={{0,1},{1,0},{2,3},{3,2},{4,5},{5,4},{6,7},{7,6},{8,9},{9,8},{10,11... | collective-permute-start | bytes 1622024 | tf_op jit(solution)/shard_map/ppermute | solution.py:43
  4.9 0.0 copy-done
  4.9 0.0 copy-done.3
  4.9 0.0 copy-done.2
  4.9 0.6 edge_two.1.two_ref
  5.5 0.7 %collective-permute-start.5 = (f32[528,256]{1,0:T(8,128)S(1)}, f32[528,256]{1,0:T(8,128)S(1)}, u32[]{:S(2)}, u32[]{:S(2)}) collective-permute-start(f32[528,256]{1,0:T(8,128)S(1)} %edge_two.1.two_ref), channel_id=1, source_target_pairs={{1,2},{2,1},{3,4},{4,3},{5,6},{6,5},{9,10},{10,9},{11,12},{12,11},... | collective-permute-start | bytes 1622024 | tf_op jit(solution)/shard_map/ppermute | solution.py:43
  6.2 14.4 %conditional.1 = (f32[16,6,32,256]{3,2,1,0:T(8,128)S(1)}, f32[16,32,256]{2,1,0:T(8,128)S(1)}, f32[16,32,256]{2,1,0:T(8,128)S(1)}, f32[8,32,256]{2,1,0:T(8,128)S(...) conditional(s32[]{:T(128)} %convert_element_type.3, () %tuple.16, ...), branch_computations={%region_0.0_spmd, %region_1.0_spmd} | conditional | bytes 21233828 | solution.py:471
  6.2 0.0 copy-start.1
  6.3 1.4 %side.1 = (f32[1088,128]{1,0:T(8,128)S(1)}, f32[1088,128]{1,0:T(8,128)S(1)}) custom-call(f32[32,16,2,8,128]{4,3,2,1,0:T(8,128)} %get-tuple-element.6.p_ref, f32[16,2,8,128]{3,2,1,0:T(8,128)S(1)} %bitcast.30, f32[3,16,2,8,128]{4,3,2,1,0:T(8,128)S(1)} %bitcast.27), custom_call_target="tpu_custom_call" | custom-call | tf_op jit(solution)/shard_map/cond/branch_1_fun/side/pallas_call | solution.py:20
  7.6 0.1 collective-permute-start
  7.7 0.8 %collective-permute-start.1 = (f32[1088,128]{1,0:T(8,128)S(1)}, f32[1088,128]{1,0:T(8,128)S(1)}, u32[]{:S(2)}, u32[]{:S(2)}) collective-permute-start(f32[1088,128]{1,0:T(8,128)S(1)} %get-tuple-element.12), channel_id=1, source_target_pairs={{8,16},{16,8},{9,17},{17,9},{10,18},{18,10},{11,19},{19,11},{12,20... | collective-permute-start | bytes 1671176 | tf_op jit(solution)/shard_map/cond/branch_1_fun/ppermute | solution.py:43
  8.6 0.2 copy-done.1
  8.8 9.3 %first.1 = (f32[16,8,32,256]{3,2,1,0:T(8,128)S(1)}, f32[7,16,8,256]{3,2,1,0:T(8,128)S(1)}, f32[16,6,32,256]{3,2,1,0:T(8,128)S(1)}, f32[16,32,256]{2,1,0:T(8,128)...) custom-call(f32[8192,128]{1,0:T(8,128)S(1)} %bitcast.24, ...), custom_call_target="tpu_custom_call" | custom-call | tf_op jit(solution)/shard_map/cond/branch_1_fun/first/pallas_call | solution.py:20
  18.1 0.0 collective-permute-done.xone_ref
  18.1 0.0 collective-permute-done.1.xtwo_ref
  18.1 2.5 %outer.1 = (f32[16,6,32,256]{3,2,1,0:T(8,128)S(1)}, f32[16,32,256]{2,1,0:T(8,128)S(1)}, f32[16,32,256]{2,1,0:T(8,128)S(1)}, f32[8,32,256]{2,1,0:T(8,128)S(1)}, f32[8,32,256]{2,1,0:T(8,128)S(1)}) custom-call(f32[16,8,32,256]{3,2,1,0:T(8,128)S(1)} %get-tuple-element.9.u_ref, f32[7,16,8,256]{3,2,1,0:T(8,128)S(1)} %get-tuple-element.10.c_ref, ...), custom_call_target="tpu_custom_call" | custom-call | tf_op jit(solution)/shard_map/cond/branch_1_fun/outer/pallas_call | solution.py:20
  20.6 4.3 %collective-permute-start.2 = (f32[16,32,256]{2,1,0:T(8,128)S(1)}, f32[16,32,256]{2,1,0:T(8,128)S(1)}, u32[]{:S(2)}, u32[]{:S(2)}) collective-permute-start(f32[16,32,256]{2,1,0:T(8,128)S(1)} %get-tuple-element.46.one_ref), channel_id=1, source_target_pairs={{0,1},{1,0},{2,3},{3,2},{4,5},{5,4},{6,7},{7,6},{8,9},{9,8},{10,11... | collective-permute-start | bytes 1572872 | tf_op jit(solution)/shard_map/ppermute | solution.py:43
  24.9 0.7 collective-permute-start.3
  25.6 0.1 coef.1.c_ref
  25.7 2.6 %collective-permute-done.4.rone_ref = f32[528,256]{1,0:T(8,128)S(1)} collective-permute-done((f32[528,256]{1,0:T(8,128)S(1)}, f32[528,256]{1,0:T(8,128)S(1)}, u32[]{:S(2)}, u32[]{:S(2)}) %collective-permute-start.4) | collective-permute-done | bytes 540704 | tf_op jit(solution)/shard_map/ppermute | solution.py:43
  28.3 0.0 collective-permute-done.5.rtwo_ref
  28.3 0.2 close.1
  28.5 0.1 collective-permute-start.6
  28.6 0.7 collective-permute-start.7
  29.2 4.7 %border.1 = (f32[16,2,32,256]{3,2,1,0:T(8,128)S(1)}, f32[4,4,32,256]{3,2,1,0:T(8,128)S(1)}, f32[16,32,256]{2,1,0:T(8,128)S(1)}, f32[16,32,256]{2,1,0:T(8,128)S(1)}, f32[96,96]{1,0:T(8,128)S(1)}) custom-call(f32[528,256]{1,0:T(8,128)S(1)} %edge_one.1.one_ref, f32[528,256]{1,0:T(8,128)S(1)} %edge_two.1.two_ref, ...), custom_call_target="tpu_custom_call" | custom-call | tf_op jit(solution)/shard_map/border/pallas_call | solution.py:20
  34.0 16.5 %collective-permute-done.2.rone_ref = f32[16,32,256]{2,1,0:T(8,128)S(1)} collective-permute-done((f32[16,32,256]{2,1,0:T(8,128)S(1)}, f32[16,32,256]{2,1,0:T(8,128)S(1)}, u32[]{:S(2)}, u32[]{:S(2)}) %collective-permute-start.2) | collective-permute-done | bytes 524320 | tf_op jit(solution)/shard_map/ppermute | solution.py:43
  50.5 0.0 collective-permute-done.3.rtwo_ref
  50.5 0.0 collective-permute-done.6.xone_ref
  50.5 0.0 collective-permute-done.7.xtwo_ref
  50.5 0.9 %last.1 = (f32[16,32,256]{2,1,0:T(8,128)S(1)}, f32[16,32,256]{2,1,0:T(8,128)S(1)}, f32[32,8,128]{2,1,0:T(8,128)S(1)}) custom-call(f32[7,16,8,256]{3,2,1,0:T(8,128)S(1)} %coef.1.c_ref, f32[16,32,256]{2,1,0:T(8,128)S(1)} %collective-permute-done.2.rone_ref, f32[16,32,256]{2,1,0:T(8,128)S(1)} %collective-permute-done.3.rtwo_ref, ...), custom_call_target="tpu_custom_call" | custom-call | tf_op jit(solution)/shard_map/last/pallas_call | solution.py:20
  51.4 13.4 %all_to_all.5.g_ref = f32[32,8,128]{2,1,0:T(8,128)S(1)} all-to-all(f32[32,8,128]{2,1,0:T(8,128)S(1)} %get-tuple-element.59), channel_id=1, replica_groups=mesh['gx'=4,'gy'=8] {'gx','gy'}, dimensions={0} | all-to-all | bytes 262144 | tf_op jit(solution)/shard_map/all_to_all | solution.py:493
  64.8 4.0 %basis.1 = (f32[32,16,16,128]{3,2,1,0:T(8,128)}, f32[32,32]{1,0:T(8,128)}) custom-call(f32[32,8,128]{2,1,0:T(8,128)S(1)} %all_to_all.5.g_ref, f32[12,4,32,256]{3,2,1,0:T(8,128)S(1)} %get-tuple-element.60.w_ref, f32[16,2,32,256]{3,2,1,0:T(8,128)S(1)} %get-tuple-element.61.wside_ref, f32[4,4,32,256]{3,2,1,0:T(8,128)S(1)} %get-tuple-element.62.wends_ref, ...), custom_call_target="tpu_custom_call" | custom-call | tf_op jit(solution)/shard_map/basis/pallas_call | solution.py:20
Async XLA Ops:
  0.6 4.3 %copy-start = (f32[32,16,8,256]{3,2,1,0:T(8,128)S(1)}, f32[32,16,8,256]{3,2,1,0:T(8,128)}, u32[]{:S(2)}) copy-start(f32[32,16,8,256]{3,2,1,0:T(8,128)} %param.5) | copy-start | bytes 12582916
  0.6 4.3 %copy-start.3 = (f32[16,8,256]{2,1,0:T(8,128)S(1)}, f32[16,8,256]{2,1,0:T(8,128)}, u32[]{:S(2)}) copy-start(f32[16,8,256]{2,1,0:T(8,128)} %d_ref.1) | copy-start | bytes 393220
  0.7 4.3 %copy-start.2 = (f32[3,16,8,256]{3,2,1,0:T(8,128)S(1)}, f32[3,16,8,256]{3,2,1,0:T(8,128)}, u32[]{:S(2)}) copy-start(f32[3,16,8,256]{3,2,1,0:T(8,128)} %v_ref.1) | copy-start | bytes 1179652
  1.9 26.5 %collective-permute-start.4 = (f32[528,256]{1,0:T(8,128)S(1)}, f32[528,256]{1,0:T(8,128)S(1)}, u32[]{:S(2)}, u32[]{:S(2)}) collective-permute-start(f32[528,256]{1,0:T(8,128)S(1)} %edge_one.1.one_ref), channel_id=1, source_target_pairs={{0,1},{1,0},{2,3},{3,2},{4,5},{5,4},{6,7},{7,6},{8,9},{9,8},{10,11... | collective-permute-start | bytes 1622024 | tf_op jit(solution)/shard_map/ppermute | solution.py:43
  5.5 22.8 %collective-permute-start.5 = (f32[528,256]{1,0:T(8,128)S(1)}, f32[528,256]{1,0:T(8,128)S(1)}, u32[]{:S(2)}, u32[]{:S(2)}) collective-permute-start(f32[528,256]{1,0:T(8,128)S(1)} %edge_two.1.two_ref), channel_id=1, source_target_pairs={{1,2},{2,1},{3,4},{4,3},{5,6},{6,5},{9,10},{10,9},{11,12},{12,11},... | collective-permute-start | bytes 1622024 | tf_op jit(solution)/shard_map/ppermute | solution.py:43
  6.2 2.5 %copy-start.1 = (f32[32,16,2,8,128]{4,3,2,1,0:T(8,128)S(1)}, f32[32,16,2,8,128]{4,3,2,1,0:T(8,128)}, u32[]{:S(2)}) copy-start(f32[32,16,2,8,128]{4,3,2,1,0:T(8,128)} %get-tuple-element.6.p_ref) | copy-start | bytes 12582916 | tf_op jit(solution)/shard_map/cond
  7.6 10.4 %collective-permute-start = (f32[1088,128]{1,0:T(8,128)S(1)}, f32[1088,128]{1,0:T(8,128)S(1)}, u32[]{:S(2)}, u32[]{:S(2)}) collective-permute-start(f32[1088,128]{1,0:T(8,128)S(1)} %get-tuple-element.11), channel_id=1, source_target_pairs={{0,8},{8,0},{16,24},{24,16},{1,9},{9,1},{17,25},{25,17},{2,10},{10... | collective-permute-start | bytes 1671176 | tf_op jit(solution)/shard_map/cond/branch_1_fun/ppermute | solution.py:43
  7.7 10.4 %collective-permute-start.1 = (f32[1088,128]{1,0:T(8,128)S(1)}, f32[1088,128]{1,0:T(8,128)S(1)}, u32[]{:S(2)}, u32[]{:S(2)}) collective-permute-start(f32[1088,128]{1,0:T(8,128)S(1)} %get-tuple-element.12), channel_id=1, source_target_pairs={{8,16},{16,8},{9,17},{17,9},{10,18},{18,10},{11,19},{19,11},{12,20... | collective-permute-start | bytes 1671176 | tf_op jit(solution)/shard_map/cond/branch_1_fun/ppermute | solution.py:43
  20.6 29.9 %collective-permute-start.2 = (f32[16,32,256]{2,1,0:T(8,128)S(1)}, f32[16,32,256]{2,1,0:T(8,128)S(1)}, u32[]{:S(2)}, u32[]{:S(2)}) collective-permute-start(f32[16,32,256]{2,1,0:T(8,128)S(1)} %get-tuple-element.46.one_ref), channel_id=1, source_target_pairs={{0,1},{1,0},{2,3},{3,2},{4,5},{5,4},{6,7},{7,6},{8,9},{9,8},{10,11... | collective-permute-start | bytes 1572872 | tf_op jit(solution)/shard_map/ppermute | solution.py:43
  24.9 25.6 %collective-permute-start.3 = (f32[16,32,256]{2,1,0:T(8,128)S(1)}, f32[16,32,256]{2,1,0:T(8,128)S(1)}, u32[]{:S(2)}, u32[]{:S(2)}) collective-permute-start(f32[16,32,256]{2,1,0:T(8,128)S(1)} %get-tuple-element.47.two_ref), channel_id=1, source_target_pairs={{1,2},{2,1},{3,4},{4,3},{5,6},{6,5},{9,10},{10,9},{11,12},{12,11},... | collective-permute-start | bytes 1572872 | tf_op jit(solution)/shard_map/ppermute | solution.py:43
  28.5 22.0 %collective-permute-start.6 = (f32[2,32,256]{2,1,0:T(8,128)S(1)}, f32[2,32,256]{2,1,0:T(8,128)S(1)}, u32[]{:S(2)}, u32[]{:S(2)}) collective-permute-start(f32[2,32,256]{2,1,0:T(8,128)S(1)} %get-tuple-element.48), channel_id=1, source_target_pairs={{0,8},{8,0},{16,24},{24,16},{1,9},{9,1},{17,25},{25,17},{2,10},{10... | collective-permute-start | bytes 196616 | tf_op jit(solution)/shard_map/ppermute | solution.py:43
  28.6 21.9 %collective-permute-start.7 = (f32[2,32,256]{2,1,0:T(8,128)S(1)}, f32[2,32,256]{2,1,0:T(8,128)S(1)}, u32[]{:S(2)}, u32[]{:S(2)}) collective-permute-start(f32[2,32,256]{2,1,0:T(8,128)S(1)} %get-tuple-element.49), channel_id=1, source_target_pairs={{8,16},{16,8},{9,17},{17,9},{10,18},{18,10},{11,19},{19,11},{12,20... | collective-permute-start | bytes 196616 | tf_op jit(solution)/shard_map/ppermute | solution.py:43

commit v7 on v6

--- a/solution.py
+++ b/solution.py
@@ -12,7 +12,7 @@
 VMEM = pl.BlockSpec(memory_space=pltpu.VMEM)
 ANY = pl.BlockSpec(memory_space=pl.ANY)
 LANES = 128
-BLOCK = 16
+BLOCK = 32
 W0, XP, XM, YP, YM, ZP, ZM = range(7)
 
 

time: 69 us -> 69.4 us (level)
  no operation moved by 1% of the time
where the time goes in v7:
time: 69.4 us; the launch traced here: 69.2 us
  Pallas kernels  25.1 us (36%)
  waiting for transfers between devices  19.2 us (28%)
  blocking collectives  13.4 us (19%)
  starting transfers between devices  10.4 us (15%)
  between operations  0.91 us (1%)
    pallas_call x10, Pallas kernels, call(): pl.pallas_call(body, out_shape=[jax.ShapeDtypeStruct(s, F32) for s in out...  25.1 us
    ppermute x8, waiting for transfers between devices, exchange(): return (lax.ppermute(one, axis, first), lax.ppermute(two, axis, second))  19.2 us
    all_to_all x1, blocking collectives, on_device(): grams = lax.all_to_all(grams, ('gx', 'gy'), 0, 0, tiled=True)  13.4 us
    ppermute x8, starting transfers between devices, exchange(): return (lax.ppermute(one, axis, first), lax.ppermute(two, axis, second))  10.4 us
  transfers between devices with their start and end apart: 8, of which 2 were waited for; matrix products, arithmetic and copies ran while one was open for 0% of the time, Pallas kernels for 27%

profile of v7, /device:TPU:0, one launch (start us, length us, event | category | flops | bytes accessed | tf_op | source)
XLA Modules:
  0.0 69.2 jit_solution(1583765399466402091)
XLA Ops:
  0.6 0.0 copy-start
  0.6 0.0 copy-start.3
  0.7 0.0 copy-start.2
  0.7 1.2 %edge_one.1.one_ref = f32[528,256]{1,0:T(8,128)S(1)} custom-call(f32[32,16,2,8,128]{4,3,2,1,0:T(8,128)} %bitcast.21, f32[16,2,8,128]{3,2,1,0:T(8,128)} %bitcast.28, f32[3,16,2,8,128]{4,3,2,1,0:T(8,128)} %bitcast.25), custom_call_target="tpu_custom_call" | custom-call | tf_op jit(solution)/shard_map/edge_one/pallas_call | solution.py:20
  1.9 3.0 %collective-permute-start.4 = (f32[528,256]{1,0:T(8,128)S(1)}, f32[528,256]{1,0:T(8,128)S(1)}, u32[]{:S(2)}, u32[]{:S(2)}) collective-permute-start(f32[528,256]{1,0:T(8,128)S(1)} %edge_one.1.one_ref), channel_id=1, source_target_pairs={{0,1},{1,0},{2,3},{3,2},{4,5},{5,4},{6,7},{7,6},{8,9},{9,8},{10,11... | collective-permute-start | bytes 1622024 | tf_op jit(solution)/shard_map/ppermute | solution.py:43
  4.9 0.0 copy-done
  4.9 0.0 copy-done.3
  4.9 0.0 copy-done.2
  4.9 0.6 edge_two.1.two_ref
  5.5 0.7 %collective-permute-start.5 = (f32[528,256]{1,0:T(8,128)S(1)}, f32[528,256]{1,0:T(8,128)S(1)}, u32[]{:S(2)}, u32[]{:S(2)}) collective-permute-start(f32[528,256]{1,0:T(8,128)S(1)} %edge_two.1.two_ref), channel_id=1, source_target_pairs={{1,2},{2,1},{3,4},{4,3},{5,6},{6,5},{9,10},{10,9},{11,12},{12,11},... | collective-permute-start | bytes 1622024 | tf_op jit(solution)/shard_map/ppermute | solution.py:43
  6.2 14.4 %conditional.1 = (f32[16,6,32,256]{3,2,1,0:T(8,128)S(1)}, f32[16,32,256]{2,1,0:T(8,128)S(1)}, f32[16,32,256]{2,1,0:T(8,128)S(1)}, f32[8,32,256]{2,1,0:T(8,128)S(...) conditional(s32[]{:T(128)} %convert_element_type.3, () %tuple.16, ...), branch_computations={%region_0.0_spmd, %region_1.0_spmd} | conditional | bytes 21233828 | solution.py:471
  6.2 0.0 copy-start.1
  6.3 1.4 %side.1 = (f32[1088,128]{1,0:T(8,128)S(1)}, f32[1088,128]{1,0:T(8,128)S(1)}) custom-call(f32[32,16,2,8,128]{4,3,2,1,0:T(8,128)} %get-tuple-element.6.p_ref, f32[16,2,8,128]{3,2,1,0:T(8,128)S(1)} %bitcast.30, f32[3,16,2,8,128]{4,3,2,1,0:T(8,128)S(1)} %bitcast.27), custom_call_target="tpu_custom_call" | custom-call | tf_op jit(solution)/shard_map/cond/branch_1_fun/side/pallas_call | solution.py:20
  7.6 0.1 collective-permute-start
  7.7 0.8 %collective-permute-start.1 = (f32[1088,128]{1,0:T(8,128)S(1)}, f32[1088,128]{1,0:T(8,128)S(1)}, u32[]{:S(2)}, u32[]{:S(2)}) collective-permute-start(f32[1088,128]{1,0:T(8,128)S(1)} %get-tuple-element.12), channel_id=1, source_target_pairs={{8,16},{16,8},{9,17},{17,9},{10,18},{18,10},{11,19},{19,11},{12,20... | collective-permute-start | bytes 1671176 | tf_op jit(solution)/shard_map/cond/branch_1_fun/ppermute | solution.py:43
  8.6 0.2 copy-done.1
  8.8 9.3 %first.1 = (f32[16,8,32,256]{3,2,1,0:T(8,128)S(1)}, f32[7,16,8,256]{3,2,1,0:T(8,128)S(1)}, f32[16,6,32,256]{3,2,1,0:T(8,128)S(1)}, f32[16,32,256]{2,1,0:T(8,128)...) custom-call(f32[8192,128]{1,0:T(8,128)S(1)} %bitcast.24, ...), custom_call_target="tpu_custom_call" | custom-call | tf_op jit(solution)/shard_map/cond/branch_1_fun/first/pallas_call | solution.py:20
  18.1 0.0 collective-permute-done.xone_ref
  18.1 0.0 collective-permute-done.1.xtwo_ref
  18.1 2.5 %outer.1 = (f32[16,6,32,256]{3,2,1,0:T(8,128)S(1)}, f32[16,32,256]{2,1,0:T(8,128)S(1)}, f32[16,32,256]{2,1,0:T(8,128)S(1)}, f32[8,32,256]{2,1,0:T(8,128)S(1)}, f32[8,32,256]{2,1,0:T(8,128)S(1)}) custom-call(f32[16,8,32,256]{3,2,1,0:T(8,128)S(1)} %get-tuple-element.9.u_ref, f32[7,16,8,256]{3,2,1,0:T(8,128)S(1)} %get-tuple-element.10.c_ref, ...), custom_call_target="tpu_custom_call" | custom-call | tf_op jit(solution)/shard_map/cond/branch_1_fun/outer/pallas_call | solution.py:20
  20.6 4.3 %collective-permute-start.2 = (f32[16,32,256]{2,1,0:T(8,128)S(1)}, f32[16,32,256]{2,1,0:T(8,128)S(1)}, u32[]{:S(2)}, u32[]{:S(2)}) collective-permute-start(f32[16,32,256]{2,1,0:T(8,128)S(1)} %get-tuple-element.46.one_ref), channel_id=1, source_target_pairs={{0,1},{1,0},{2,3},{3,2},{4,5},{5,4},{6,7},{7,6},{8,9},{9,8},{10,11... | collective-permute-start | bytes 1572872 | tf_op jit(solution)/shard_map/ppermute | solution.py:43
  24.9 0.7 collective-permute-start.3
  25.6 0.1 coef.1.c_ref
  25.7 2.6 %collective-permute-done.4.rone_ref = f32[528,256]{1,0:T(8,128)S(1)} collective-permute-done((f32[528,256]{1,0:T(8,128)S(1)}, f32[528,256]{1,0:T(8,128)S(1)}, u32[]{:S(2)}, u32[]{:S(2)}) %collective-permute-start.4) | collective-permute-done | bytes 540704 | tf_op jit(solution)/shard_map/ppermute | solution.py:43
  28.3 0.0 collective-permute-done.5.rtwo_ref
  28.3 0.2 close.1
  28.5 0.1 collective-permute-start.6
  28.6 0.7 collective-permute-start.7
  29.2 4.7 %border.1 = (f32[16,2,32,256]{3,2,1,0:T(8,128)S(1)}, f32[4,4,32,256]{3,2,1,0:T(8,128)S(1)}, f32[16,32,256]{2,1,0:T(8,128)S(1)}, f32[16,32,256]{2,1,0:T(8,128)S(1)}, f32[96,96]{1,0:T(8,128)S(1)}) custom-call(f32[528,256]{1,0:T(8,128)S(1)} %edge_one.1.one_ref, f32[528,256]{1,0:T(8,128)S(1)} %edge_two.1.two_ref, ...), custom_call_target="tpu_custom_call" | custom-call | tf_op jit(solution)/shard_map/border/pallas_call | solution.py:20
  34.0 16.5 %collective-permute-done.2.rone_ref = f32[16,32,256]{2,1,0:T(8,128)S(1)} collective-permute-done((f32[16,32,256]{2,1,0:T(8,128)S(1)}, f32[16,32,256]{2,1,0:T(8,128)S(1)}, u32[]{:S(2)}, u32[]{:S(2)}) %collective-permute-start.2) | collective-permute-done | bytes 524320 | tf_op jit(solution)/shard_map/ppermute | solution.py:43
  50.5 0.0 collective-permute-done.3.rtwo_ref
  50.5 0.0 collective-permute-done.6.xone_ref
  50.5 0.0 collective-permute-done.7.xtwo_ref
  50.5 0.9 %last.1 = (f32[16,32,256]{2,1,0:T(8,128)S(1)}, f32[16,32,256]{2,1,0:T(8,128)S(1)}, f32[32,8,128]{2,1,0:T(8,128)S(1)}) custom-call(f32[7,16,8,256]{3,2,1,0:T(8,128)S(1)} %coef.1.c_ref, f32[16,32,256]{2,1,0:T(8,128)S(1)} %collective-permute-done.2.rone_ref, f32[16,32,256]{2,1,0:T(8,128)S(1)} %collective-permute-done.3.rtwo_ref, ...), custom_call_target="tpu_custom_call" | custom-call | tf_op jit(solution)/shard_map/last/pallas_call | solution.py:20
  51.4 13.4 %all_to_all.5.g_ref = f32[32,8,128]{2,1,0:T(8,128)S(1)} all-to-all(f32[32,8,128]{2,1,0:T(8,128)S(1)} %get-tuple-element.59), channel_id=1, replica_groups=mesh['gx'=4,'gy'=8] {'gx','gy'}, dimensions={0} | all-to-all | bytes 262144 | tf_op jit(solution)/shard_map/all_to_all | solution.py:493
  64.8 4.2 %basis.1 = (f32[32,16,16,128]{3,2,1,0:T(8,128)}, f32[32,32]{1,0:T(8,128)}) custom-call(f32[32,8,128]{2,1,0:T(8,128)S(1)} %all_to_all.5.g_ref, f32[12,4,32,256]{3,2,1,0:T(8,128)S(1)} %get-tuple-element.60.w_ref, f32[16,2,32,256]{3,2,1,0:T(8,128)S(1)} %get-tuple-element.61.wside_ref, f32[4,4,32,256]{3,2,1,0:T(8,128)S(1)} %get-tuple-element.62.wends_ref, ...), custom_call_target="tpu_custom_call" | custom-call | tf_op jit(solution)/shard_map/basis/pallas_call | solution.py:20
Async XLA Ops:
  0.6 4.3 %copy-start = (f32[32,16,8,256]{3,2,1,0:T(8,128)S(1)}, f32[32,16,8,256]{3,2,1,0:T(8,128)}, u32[]{:S(2)}) copy-start(f32[32,16,8,256]{3,2,1,0:T(8,128)} %param.5) | copy-start | bytes 12582916
  0.6 4.3 %copy-start.3 = (f32[16,8,256]{2,1,0:T(8,128)S(1)}, f32[16,8,256]{2,1,0:T(8,128)}, u32[]{:S(2)}) copy-start(f32[16,8,256]{2,1,0:T(8,128)} %d_ref.1) | copy-start | bytes 393220
  0.7 4.3 %copy-start.2 = (f32[3,16,8,256]{3,2,1,0:T(8,128)S(1)}, f32[3,16,8,256]{3,2,1,0:T(8,128)}, u32[]{:S(2)}) copy-start(f32[3,16,8,256]{3,2,1,0:T(8,128)} %v_ref.1) | copy-start | bytes 1179652
  1.9 26.5 %collective-permute-start.4 = (f32[528,256]{1,0:T(8,128)S(1)}, f32[528,256]{1,0:T(8,128)S(1)}, u32[]{:S(2)}, u32[]{:S(2)}) collective-permute-start(f32[528,256]{1,0:T(8,128)S(1)} %edge_one.1.one_ref), channel_id=1, source_target_pairs={{0,1},{1,0},{2,3},{3,2},{4,5},{5,4},{6,7},{7,6},{8,9},{9,8},{10,11... | collective-permute-start | bytes 1622024 | tf_op jit(solution)/shard_map/ppermute | solution.py:43
  5.5 22.8 %collective-permute-start.5 = (f32[528,256]{1,0:T(8,128)S(1)}, f32[528,256]{1,0:T(8,128)S(1)}, u32[]{:S(2)}, u32[]{:S(2)}) collective-permute-start(f32[528,256]{1,0:T(8,128)S(1)} %edge_two.1.two_ref), channel_id=1, source_target_pairs={{1,2},{2,1},{3,4},{4,3},{5,6},{6,5},{9,10},{10,9},{11,12},{12,11},... | collective-permute-start | bytes 1622024 | tf_op jit(solution)/shard_map/ppermute | solution.py:43
  6.2 2.5 %copy-start.1 = (f32[32,16,2,8,128]{4,3,2,1,0:T(8,128)S(1)}, f32[32,16,2,8,128]{4,3,2,1,0:T(8,128)}, u32[]{:S(2)}) copy-start(f32[32,16,2,8,128]{4,3,2,1,0:T(8,128)} %get-tuple-element.6.p_ref) | copy-start | bytes 12582916 | tf_op jit(solution)/shard_map/cond
  7.6 10.4 %collective-permute-start = (f32[1088,128]{1,0:T(8,128)S(1)}, f32[1088,128]{1,0:T(8,128)S(1)}, u32[]{:S(2)}, u32[]{:S(2)}) collective-permute-start(f32[1088,128]{1,0:T(8,128)S(1)} %get-tuple-element.11), channel_id=1, source_target_pairs={{0,8},{8,0},{16,24},{24,16},{1,9},{9,1},{17,25},{25,17},{2,10},{10... | collective-permute-start | bytes 1671176 | tf_op jit(solution)/shard_map/cond/branch_1_fun/ppermute | solution.py:43
  7.7 10.4 %collective-permute-start.1 = (f32[1088,128]{1,0:T(8,128)S(1)}, f32[1088,128]{1,0:T(8,128)S(1)}, u32[]{:S(2)}, u32[]{:S(2)}) collective-permute-start(f32[1088,128]{1,0:T(8,128)S(1)} %get-tuple-element.12), channel_id=1, source_target_pairs={{8,16},{16,8},{9,17},{17,9},{10,18},{18,10},{11,19},{19,11},{12,20... | collective-permute-start | bytes 1671176 | tf_op jit(solution)/shard_map/cond/branch_1_fun/ppermute | solution.py:43
  20.6 29.9 %collective-permute-start.2 = (f32[16,32,256]{2,1,0:T(8,128)S(1)}, f32[16,32,256]{2,1,0:T(8,128)S(1)}, u32[]{:S(2)}, u32[]{:S(2)}) collective-permute-start(f32[16,32,256]{2,1,0:T(8,128)S(1)} %get-tuple-element.46.one_ref), channel_id=1, source_target_pairs={{0,1},{1,0},{2,3},{3,2},{4,5},{5,4},{6,7},{7,6},{8,9},{9,8},{10,11... | collective-permute-start | bytes 1572872 | tf_op jit(solution)/shard_map/ppermute | solution.py:43
  24.9 25.6 %collective-permute-start.3 = (f32[16,32,256]{2,1,0:T(8,128)S(1)}, f32[16,32,256]{2,1,0:T(8,128)S(1)}, u32[]{:S(2)}, u32[]{:S(2)}) collective-permute-start(f32[16,32,256]{2,1,0:T(8,128)S(1)} %get-tuple-element.47.two_ref), channel_id=1, source_target_pairs={{1,2},{2,1},{3,4},{4,3},{5,6},{6,5},{9,10},{10,9},{11,12},{12,11},... | collective-permute-start | bytes 1572872 | tf_op jit(solution)/shard_map/ppermute | solution.py:43
  28.5 22.0 %collective-permute-start.6 = (f32[2,32,256]{2,1,0:T(8,128)S(1)}, f32[2,32,256]{2,1,0:T(8,128)S(1)}, u32[]{:S(2)}, u32[]{:S(2)}) collective-permute-start(f32[2,32,256]{2,1,0:T(8,128)S(1)} %get-tuple-element.48), channel_id=1, source_target_pairs={{0,8},{8,0},{16,24},{24,16},{1,9},{9,1},{17,25},{25,17},{2,10},{10... | collective-permute-start | bytes 196616 | tf_op jit(solution)/shard_map/ppermute | solution.py:43
  28.6 21.9 %collective-permute-start.7 = (f32[2,32,256]{2,1,0:T(8,128)S(1)}, f32[2,32,256]{2,1,0:T(8,128)S(1)}, u32[]{:S(2)}, u32[]{:S(2)}) collective-permute-start(f32[2,32,256]{2,1,0:T(8,128)S(1)} %get-tuple-element.49), channel_id=1, source_target_pairs={{8,16},{16,8},{9,17},{17,9},{10,18},{18,10},{11,19},{19,11},{12,20... | collective-permute-start | bytes 196616 | tf_op jit(solution)/shard_map/ppermute | solution.py:43

commit v8 on v6

--- a/solution.py
+++ b/solution.py
@@ -401,9 +401,11 @@
             block = terms[:n] + (terms[n : 2 * n] + terms[2 * n :])
             for h in range(parts):
                 stage.at[x][pl.ds(h * ny + y, n, stride=group), :] = block[:, h * LANES : (h + 1) * LANES]
-        copy = pltpu.make_async_copy(stage.at[x].reshape(n, group, LANES), out_ref.at[:, x], sems.at[x])
-        copy.start()
-        copies.append(copy)
+        slab = stage.at[x].reshape(n, group, LANES)
+        for p in range(0, n, 8):
+            copy = pltpu.make_async_copy(slab.at[pl.ds(p, 8)], out_ref.at[pl.ds(p, 8), x], sems.at[x])
+            copy.start()
+            copies.append(copy)
     for copy in copies:
         copy.wait()
 

time: 69 us -> 69 us (level)
  no operation moved by 1% of the time
where the time goes in v8:
time: 69 us; the launch traced here: 68.8 us
  Pallas kernels  24.9 us (36%)
  waiting for transfers between devices  19.2 us (28%)
  blocking collectives  13.4 us (19%)
  starting transfers between devices  10.4 us (15%)
  between operations  0.75 us (1%)
    pallas_call x10, Pallas kernels, call(): pl.pallas_call(body, out_shape=[jax.ShapeDtypeStruct(s, F32) for s in out...  24.9 us
    ppermute x8, waiting for transfers between devices, exchange(): return (lax.ppermute(one, axis, first), lax.ppermute(two, axis, second))  19.2 us
    all_to_all x1, blocking collectives, on_device(): grams = lax.all_to_all(grams, ('gx', 'gy'), 0, 0, tiled=True)  13.4 us
    ppermute x8, starting transfers between devices, exchange(): return (lax.ppermute(one, axis, first), lax.ppermute(two, axis, second))  10.4 us
  transfers between devices with their start and end apart: 8, of which 2 were waited for; matrix products, arithmetic and copies ran while one was open for 0% of the time, Pallas kernels for 27%

profile of v8, /device:TPU:0, one launch (start us, length us, event | category | flops | bytes accessed | tf_op | source)
XLA Modules:
  0.0 68.8 jit_solution(9325057962372372981)
XLA Ops:
  0.6 0.0 copy-start
  0.6 0.0 copy-start.3
  0.7 0.0 copy-start.2
  0.7 1.2 %edge_one.1.one_ref = f32[528,256]{1,0:T(8,128)S(1)} custom-call(f32[32,16,2,8,128]{4,3,2,1,0:T(8,128)} %bitcast.21, f32[16,2,8,128]{3,2,1,0:T(8,128)} %bitcast.28, f32[3,16,2,8,128]{4,3,2,1,0:T(8,128)} %bitcast.25), custom_call_target="tpu_custom_call" | custom-call | tf_op jit(solution)/shard_map/edge_one/pallas_call | solution.py:20
  1.9 3.0 %collective-permute-start.4 = (f32[528,256]{1,0:T(8,128)S(1)}, f32[528,256]{1,0:T(8,128)S(1)}, u32[]{:S(2)}, u32[]{:S(2)}) collective-permute-start(f32[528,256]{1,0:T(8,128)S(1)} %edge_one.1.one_ref), channel_id=1, source_target_pairs={{0,1},{1,0},{2,3},{3,2},{4,5},{5,4},{6,7},{7,6},{8,9},{9,8},{10,11... | collective-permute-start | bytes 1622024 | tf_op jit(solution)/shard_map/ppermute | solution.py:43
  4.9 0.0 copy-done
  4.9 0.0 copy-done.3
  4.9 0.0 copy-done.2
  4.9 0.6 edge_two.1.two_ref
  5.5 0.7 %collective-permute-start.5 = (f32[528,256]{1,0:T(8,128)S(1)}, f32[528,256]{1,0:T(8,128)S(1)}, u32[]{:S(2)}, u32[]{:S(2)}) collective-permute-start(f32[528,256]{1,0:T(8,128)S(1)} %edge_two.1.two_ref), channel_id=1, source_target_pairs={{1,2},{2,1},{3,4},{4,3},{5,6},{6,5},{9,10},{10,9},{11,12},{12,11},... | collective-permute-start | bytes 1622024 | tf_op jit(solution)/shard_map/ppermute | solution.py:43
  6.2 14.4 %conditional.1 = (f32[16,6,32,256]{3,2,1,0:T(8,128)S(1)}, f32[16,32,256]{2,1,0:T(8,128)S(1)}, f32[16,32,256]{2,1,0:T(8,128)S(1)}, f32[8,32,256]{2,1,0:T(8,128)S(...) conditional(s32[]{:T(128)} %convert_element_type.3, () %tuple.16, ...), branch_computations={%region_0.0_spmd, %region_1.0_spmd} | conditional | bytes 21233828 | solution.py:473
  6.2 0.0 copy-start.1
  6.3 1.4 %side.1 = (f32[1088,128]{1,0:T(8,128)S(1)}, f32[1088,128]{1,0:T(8,128)S(1)}) custom-call(f32[32,16,2,8,128]{4,3,2,1,0:T(8,128)} %get-tuple-element.6.p_ref, f32[16,2,8,128]{3,2,1,0:T(8,128)S(1)} %bitcast.30, f32[3,16,2,8,128]{4,3,2,1,0:T(8,128)S(1)} %bitcast.27), custom_call_target="tpu_custom_call" | custom-call | tf_op jit(solution)/shard_map/cond/branch_1_fun/side/pallas_call | solution.py:20
  7.6 0.1 collective-permute-start
  7.7 0.8 %collective-permute-start.1 = (f32[1088,128]{1,0:T(8,128)S(1)}, f32[1088,128]{1,0:T(8,128)S(1)}, u32[]{:S(2)}, u32[]{:S(2)}) collective-permute-start(f32[1088,128]{1,0:T(8,128)S(1)} %get-tuple-element.12), channel_id=1, source_target_pairs={{8,16},{16,8},{9,17},{17,9},{10,18},{18,10},{11,19},{19,11},{12,20... | collective-permute-start | bytes 1671176 | tf_op jit(solution)/shard_map/cond/branch_1_fun/ppermute | solution.py:43
  8.6 0.2 copy-done.1
  8.8 9.3 %first.1 = (f32[16,8,32,256]{3,2,1,0:T(8,128)S(1)}, f32[7,16,8,256]{3,2,1,0:T(8,128)S(1)}, f32[16,6,32,256]{3,2,1,0:T(8,128)S(1)}, f32[16,32,256]{2,1,0:T(8,128)...) custom-call(f32[8192,128]{1,0:T(8,128)S(1)} %bitcast.24, ...), custom_call_target="tpu_custom_call" | custom-call | tf_op jit(solution)/shard_map/cond/branch_1_fun/first/pallas_call | solution.py:20
  18.1 0.0 collective-permute-done.xone_ref
  18.1 0.0 collective-permute-done.1.xtwo_ref
  18.1 2.5 %outer.1 = (f32[16,6,32,256]{3,2,1,0:T(8,128)S(1)}, f32[16,32,256]{2,1,0:T(8,128)S(1)}, f32[16,32,256]{2,1,0:T(8,128)S(1)}, f32[8,32,256]{2,1,0:T(8,128)S(1)}, f32[8,32,256]{2,1,0:T(8,128)S(1)}) custom-call(f32[16,8,32,256]{3,2,1,0:T(8,128)S(1)} %get-tuple-element.9.u_ref, f32[7,16,8,256]{3,2,1,0:T(8,128)S(1)} %get-tuple-element.10.c_ref, ...), custom_call_target="tpu_custom_call" | custom-call | tf_op jit(solution)/shard_map/cond/branch_1_fun/outer/pallas_call | solution.py:20
  20.6 4.3 %collective-permute-start.2 = (f32[16,32,256]{2,1,0:T(8,128)S(1)}, f32[16,32,256]{2,1,0:T(8,128)S(1)}, u32[]{:S(2)}, u32[]{:S(2)}) collective-permute-start(f32[16,32,256]{2,1,0:T(8,128)S(1)} %get-tuple-element.46.one_ref), channel_id=1, source_target_pairs={{0,1},{1,0},{2,3},{3,2},{4,5},{5,4},{6,7},{7,6},{8,9},{9,8},{10,11... | collective-permute-start | bytes 1572872 | tf_op jit(solution)/shard_map/ppermute | solution.py:43
  24.9 0.7 collective-permute-start.3
  25.6 0.1 coef.1.c_ref
  25.7 2.6 %collective-permute-done.4.rone_ref = f32[528,256]{1,0:T(8,128)S(1)} collective-permute-done((f32[528,256]{1,0:T(8,128)S(1)}, f32[528,256]{1,0:T(8,128)S(1)}, u32[]{:S(2)}, u32[]{:S(2)}) %collective-permute-start.4) | collective-permute-done | bytes 540704 | tf_op jit(solution)/shard_map/ppermute | solution.py:43
  28.3 0.0 collective-permute-done.5.rtwo_ref
  28.3 0.2 close.1
  28.5 0.1 collective-permute-start.6
  28.6 0.7 collective-permute-start.7
  29.2 4.7 %border.1 = (f32[16,2,32,256]{3,2,1,0:T(8,128)S(1)}, f32[4,4,32,256]{3,2,1,0:T(8,128)S(1)}, f32[16,32,256]{2,1,0:T(8,128)S(1)}, f32[16,32,256]{2,1,0:T(8,128)S(1)}, f32[96,96]{1,0:T(8,128)S(1)}) custom-call(f32[528,256]{1,0:T(8,128)S(1)} %edge_one.1.one_ref, f32[528,256]{1,0:T(8,128)S(1)} %edge_two.1.two_ref, ...), custom_call_target="tpu_custom_call" | custom-call | tf_op jit(solution)/shard_map/border/pallas_call | solution.py:20
  34.0 16.5 %collective-permute-done.2.rone_ref = f32[16,32,256]{2,1,0:T(8,128)S(1)} collective-permute-done((f32[16,32,256]{2,1,0:T(8,128)S(1)}, f32[16,32,256]{2,1,0:T(8,128)S(1)}, u32[]{:S(2)}, u32[]{:S(2)}) %collective-permute-start.2) | collective-permute-done | bytes 524320 | tf_op jit(solution)/shard_map/ppermute | solution.py:43
  50.5 0.0 collective-permute-done.3.rtwo_ref
  50.5 0.0 collective-permute-done.6.xone_ref
  50.5 0.0 collective-permute-done.7.xtwo_ref
  50.5 0.9 %last.1 = (f32[16,32,256]{2,1,0:T(8,128)S(1)}, f32[16,32,256]{2,1,0:T(8,128)S(1)}, f32[32,8,128]{2,1,0:T(8,128)S(1)}) custom-call(f32[7,16,8,256]{3,2,1,0:T(8,128)S(1)} %coef.1.c_ref, f32[16,32,256]{2,1,0:T(8,128)S(1)} %collective-permute-done.2.rone_ref, f32[16,32,256]{2,1,0:T(8,128)S(1)} %collective-permute-done.3.rtwo_ref, ...), custom_call_target="tpu_custom_call" | custom-call | tf_op jit(solution)/shard_map/last/pallas_call | solution.py:20
  51.4 13.4 %all_to_all.5.g_ref = f32[32,8,128]{2,1,0:T(8,128)S(1)} all-to-all(f32[32,8,128]{2,1,0:T(8,128)S(1)} %get-tuple-element.59), channel_id=1, replica_groups=mesh['gx'=4,'gy'=8] {'gx','gy'}, dimensions={0} | all-to-all | bytes 262144 | tf_op jit(solution)/shard_map/all_to_all | solution.py:495
  64.8 4.0 %basis.1 = (f32[32,16,16,128]{3,2,1,0:T(8,128)}, f32[32,32]{1,0:T(8,128)}) custom-call(f32[32,8,128]{2,1,0:T(8,128)S(1)} %all_to_all.5.g_ref, f32[12,4,32,256]{3,2,1,0:T(8,128)S(1)} %get-tuple-element.60.w_ref, f32[16,2,32,256]{3,2,1,0:T(8,128)S(1)} %get-tuple-element.61.wside_ref, f32[4,4,32,256]{3,2,1,0:T(8,128)S(1)} %get-tuple-element.62.wends_ref, ...), custom_call_target="tpu_custom_call" | custom-call | tf_op jit(solution)/shard_map/basis/pallas_call | solution.py:20
Async XLA Ops:
  0.6 4.3 %copy-start = (f32[32,16,8,256]{3,2,1,0:T(8,128)S(1)}, f32[32,16,8,256]{3,2,1,0:T(8,128)}, u32[]{:S(2)}) copy-start(f32[32,16,8,256]{3,2,1,0:T(8,128)} %param.5) | copy-start | bytes 12582916
  0.6 4.3 %copy-start.3 = (f32[16,8,256]{2,1,0:T(8,128)S(1)}, f32[16,8,256]{2,1,0:T(8,128)}, u32[]{:S(2)}) copy-start(f32[16,8,256]{2,1,0:T(8,128)} %d_ref.1) | copy-start | bytes 393220
  0.7 4.3 %copy-start.2 = (f32[3,16,8,256]{3,2,1,0:T(8,128)S(1)}, f32[3,16,8,256]{3,2,1,0:T(8,128)}, u32[]{:S(2)}) copy-start(f32[3,16,8,256]{3,2,1,0:T(8,128)} %v_ref.1) | copy-start | bytes 1179652
  1.9 26.5 %collective-permute-start.4 = (f32[528,256]{1,0:T(8,128)S(1)}, f32[528,256]{1,0:T(8,128)S(1)}, u32[]{:S(2)}, u32[]{:S(2)}) collective-permute-start(f32[528,256]{1,0:T(8,128)S(1)} %edge_one.1.one_ref), channel_id=1, source_target_pairs={{0,1},{1,0},{2,3},{3,2},{4,5},{5,4},{6,7},{7,6},{8,9},{9,8},{10,11... | collective-permute-start | bytes 1622024 | tf_op jit(solution)/shard_map/ppermute | solution.py:43
  5.5 22.8 %collective-permute-start.5 = (f32[528,256]{1,0:T(8,128)S(1)}, f32[528,256]{1,0:T(8,128)S(1)}, u32[]{:S(2)}, u32[]{:S(2)}) collective-permute-start(f32[528,256]{1,0:T(8,128)S(1)} %edge_two.1.two_ref), channel_id=1, source_target_pairs={{1,2},{2,1},{3,4},{4,3},{5,6},{6,5},{9,10},{10,9},{11,12},{12,11},... | collective-permute-start | bytes 1622024 | tf_op jit(solution)/shard_map/ppermute | solution.py:43
  6.2 2.5 %copy-start.1 = (f32[32,16,2,8,128]{4,3,2,1,0:T(8,128)S(1)}, f32[32,16,2,8,128]{4,3,2,1,0:T(8,128)}, u32[]{:S(2)}) copy-start(f32[32,16,2,8,128]{4,3,2,1,0:T(8,128)} %get-tuple-element.6.p_ref) | copy-start | bytes 12582916 | tf_op jit(solution)/shard_map/cond
  7.6 10.4 %collective-permute-start = (f32[1088,128]{1,0:T(8,128)S(1)}, f32[1088,128]{1,0:T(8,128)S(1)}, u32[]{:S(2)}, u32[]{:S(2)}) collective-permute-start(f32[1088,128]{1,0:T(8,128)S(1)} %get-tuple-element.11), channel_id=1, source_target_pairs={{0,8},{8,0},{16,24},{24,16},{1,9},{9,1},{17,25},{25,17},{2,10},{10... | collective-permute-start | bytes 1671176 | tf_op jit(solution)/shard_map/cond/branch_1_fun/ppermute | solution.py:43
  7.7 10.4 %collective-permute-start.1 = (f32[1088,128]{1,0:T(8,128)S(1)}, f32[1088,128]{1,0:T(8,128)S(1)}, u32[]{:S(2)}, u32[]{:S(2)}) collective-permute-start(f32[1088,128]{1,0:T(8,128)S(1)} %get-tuple-element.12), channel_id=1, source_target_pairs={{8,16},{16,8},{9,17},{17,9},{10,18},{18,10},{11,19},{19,11},{12,20... | collective-permute-start | bytes 1671176 | tf_op jit(solution)/shard_map/cond/branch_1_fun/ppermute | solution.py:43
  20.6 29.9 %collective-permute-start.2 = (f32[16,32,256]{2,1,0:T(8,128)S(1)}, f32[16,32,256]{2,1,0:T(8,128)S(1)}, u32[]{:S(2)}, u32[]{:S(2)}) collective-permute-start(f32[16,32,256]{2,1,0:T(8,128)S(1)} %get-tuple-element.46.one_ref), channel_id=1, source_target_pairs={{0,1},{1,0},{2,3},{3,2},{4,5},{5,4},{6,7},{7,6},{8,9},{9,8},{10,11... | collective-permute-start | bytes 1572872 | tf_op jit(solution)/shard_map/ppermute | solution.py:43
  24.9 25.6 %collective-permute-start.3 = (f32[16,32,256]{2,1,0:T(8,128)S(1)}, f32[16,32,256]{2,1,0:T(8,128)S(1)}, u32[]{:S(2)}, u32[]{:S(2)}) collective-permute-start(f32[16,32,256]{2,1,0:T(8,128)S(1)} %get-tuple-element.47.two_ref), channel_id=1, source_target_pairs={{1,2},{2,1},{3,4},{4,3},{5,6},{6,5},{9,10},{10,9},{11,12},{12,11},... | collective-permute-start | bytes 1572872 | tf_op jit(solution)/shard_map/ppermute | solution.py:43
  28.5 22.0 %collective-permute-start.6 = (f32[2,32,256]{2,1,0:T(8,128)S(1)}, f32[2,32,256]{2,1,0:T(8,128)S(1)}, u32[]{:S(2)}, u32[]{:S(2)}) collective-permute-start(f32[2,32,256]{2,1,0:T(8,128)S(1)} %get-tuple-element.48), channel_id=1, source_target_pairs={{0,8},{8,0},{16,24},{24,16},{1,9},{9,1},{17,25},{25,17},{2,10},{10... | collective-permute-start | bytes 196616 | tf_op jit(solution)/shard_map/ppermute | solution.py:43
  28.6 21.9 %collective-permute-start.7 = (f32[2,32,256]{2,1,0:T(8,128)S(1)}, f32[2,32,256]{2,1,0:T(8,128)S(1)}, u32[]{:S(2)}, u32[]{:S(2)}) collective-permute-start(f32[2,32,256]{2,1,0:T(8,128)S(1)} %get-tuple-element.49), channel_id=1, source_target_pairs={{8,16},{16,8},{9,17},{17,9},{10,18},{18,10},{11,19},{19,11},{12,20... | collective-permute-start | bytes 196616 | tf_op jit(solution)/shard_map/ppermute | solution.py:43
